TPU v7x, 512 devices: a whole 4x4x16 slice. The times are simulated.
512 devices in a mesh: dp: 8 (over x, core), expert: 64 (over z, y).
Axes of the slice: x: 4, y: 4, z: 16, core: 2. Of those that a mesh axis runs over, the one named last changes fastest.
Arguments:
- cells: bfloat16 [131072, 1024], P(('dp', 'expert')), may hold values from -6 to 6
- cell_bins: int32 [131072], P(('dp', 'expert')), may hold values from 0 to 127
- tile_counts: int32 [512, 8], P(('dp', 'expert')), may hold values from 1 to 96, 256 in all within a row
- bin_base: bfloat16 [65536, 1024], P(('dp', 'expert')), may hold values from -6 to 6
- norm_gain: float32 [1024], replicated, may hold values from 0.1 to 1.9
- expert_ids: int32 [65536, 1], P(('dp', 'expert')), may hold values from 0 to 63; in each aligned block of 128 rows (0 to 127, 128 to 255, ...) at most 3 rows name the same one
- gate_q: bfloat16 [64, 4096, 1024], P('expert', 'dp'), may hold values from -0.1875 to 0.1875
- up_q: bfloat16 [64, 4096, 1024], P('expert', 'dp'), may hold values from -0.1875 to 0.1875
- down_q: bfloat16 [64, 4096, 1024], P('expert', 'dp'), may hold values from -0.09375 to 0.09375
- gate_scales: int32 [64, 32, 8], P('expert', 'dp'), may hold values from -1 to 1
- up_scales: int32 [64, 32, 8], P('expert', 'dp'), may hold values from -1 to 1
- down_scales: int32 [64, 32, 8], P('expert', 'dp'), may hold values from -1 to 1
Outputs:
- encoded: bfloat16 [65536, 1024], P(('dp', 'expert'))
Inputs may be any that keep to these rules, and one draw needn't show every extreme that they name: Each device's cells are stored grouped by tile in order of t; row s of tile_counts gives the lengths of these groups, sums to 256, and its largest entry is 96. `expert_ids`: among the 128 bins of one tile no expert is named more than 3 times, a bound that some block reaches.
All inputs are finite; a program needn't handle non-finite values.
Results may differ from a plain program's by a relative error of at most 0.014.
Values may be sent and summed in bfloat16 or wider, within the bound.
No kernel may reach another device: no remote copies, remote signals or barrier semaphores. Data moves between devices by JAX's collectives and lax.ppermute only.
A program may use at most 64 MiB of HBM per device.

v0:
```python
import jax
import jax.numpy as jnp
from jax import lax
from jax.sharding import PartitionSpec as P

QB = 128


def dequantize(quant, scale):
    factor = jnp.exp2(scale.astype(jnp.float32))
    factor = jnp.repeat(jnp.repeat(factor, QB, axis=0), QB, axis=1).astype(jnp.bfloat16)
    return quant * factor


def on_device(
    cells,
    cell_bins,
    tile_counts,
    bin_base,
    norm_gain,
    expert_ids,
    gate_q,
    up_q,
    down_q,
    gate_scales,
    up_scales,
    down_scales,
):
    dp_size = lax.axis_size("dp")
    expert_count = lax.axis_size("expert") * gate_q.shape[0]
    cell_total = cells.shape[0]
    tile_bins = bin_base.shape[0]
    counts = tile_counts[0]
    run_ends = jnp.cumsum(counts)
    run_starts = run_ends - counts
    bin_iota = jnp.arange(tile_bins, dtype=jnp.int32)
    cell_cap = min(3 * cell_total // dp_size, cell_total - dp_size + 1)
    slot_iota = jnp.arange(cell_cap, dtype=jnp.int32)
    take_rows = jnp.clip(run_starts[:, None] + slot_iota[None, :], 0, cell_total - 1).reshape(-1)
    valid = (slot_iota[None, :] < counts[:, None]).reshape(-1)
    slot_rows = jnp.where(
        valid[:, None], jnp.take(cells, take_rows, axis=0), jnp.zeros((), jnp.bfloat16)
    )
    slot_bins = jnp.where(valid, jnp.take(cell_bins, take_rows), -1)
    got_rows, got_bins = (
        lax.all_to_all(slot_rows, "dp", split_axis=0, concat_axis=0, tiled=True),
        lax.all_to_all(slot_bins, "dp", split_axis=0, concat_axis=0, tiled=True),
    )
    matcher = (bin_iota[:, None] == got_bins[None, :]).astype(jnp.bfloat16)
    splat_sum = jnp.dot(matcher, got_rows, preferred_element_type=jnp.float32)
    residual_in = bin_base.astype(jnp.float32) + splat_sum
    mean_sq = jnp.mean(residual_in * residual_in, axis=1, keepdims=True)
    normed = (residual_in * lax.rsqrt(mean_sq + 1e-06) * norm_gain[None, :]).astype(jnp.bfloat16)
    capacity = max(2, 3 * tile_bins // (2 * expert_count))
    expert_col = expert_ids[:, 0]
    one_hot = (expert_col[:, None] == jnp.arange(expert_count, dtype=jnp.int32)[None, :]).astype(
        jnp.int32
    )
    within = jnp.sum(jnp.cumsum(one_hot, axis=0) * one_hot, axis=1) - 1
    slot_of = expert_col * capacity + within
    placer = (
        jnp.arange(expert_count * capacity, dtype=jnp.int32)[:, None] == slot_of[None, :]
    ).astype(jnp.bfloat16)
    outgoing = jnp.dot(placer, normed, preferred_element_type=jnp.float32).astype(jnp.bfloat16)
    arrived = lax.all_to_all(outgoing, "expert", split_axis=0, concat_axis=0, tiled=True)
    w_gate = dequantize(gate_q[0], gate_scales[0])
    w_up = dequantize(up_q[0], up_scales[0])
    w_down = dequantize(down_q[0], down_scales[0])
    contract = (((1,), (1,)), ((), ()))
    block_rows = lax.all_gather(arrived, "dp", axis=0, tiled=True)
    gate_val = lax.dot_general(block_rows, w_gate, contract, preferred_element_type=jnp.float32)
    up_val = lax.dot_general(block_rows, w_up, contract, preferred_element_type=jnp.float32)
    hidden = (jax.nn.silu(gate_val) * up_val).astype(jnp.bfloat16)
    partial_rows = jnp.dot(hidden, w_down, preferred_element_type=jnp.float32)
    summed = lax.psum_scatter(
        partial_rows.astype(jnp.bfloat16), "dp", scatter_dimension=0, tiled=True
    )
    returned = lax.all_to_all(summed, "expert", split_axis=0, concat_axis=0, tiled=True)
    expert_out = lax.dot_general(
        placer, returned, (((0,), (0,)), ((), ())), preferred_element_type=jnp.float32
    )
    return (residual_in + expert_out).astype(jnp.bfloat16)


def solution(mesh):
    placed = (
        P(("dp", "expert"), None),
        P(("dp", "expert")),
        P(("dp", "expert"), None),
        P(("dp", "expert"), None),
        P(),
        P(("dp", "expert"), None),
        P("expert", "dp", None),
        P("expert", "dp", None),
        P("expert", "dp", None),
        P("expert", "dp", None),
        P("expert", "dp", None),
        P("expert", "dp", None),
    )
    return jax.shard_map(
        on_device, mesh=mesh, in_specs=placed, out_specs=P(("dp", "expert"), None), check_vma=False
    )
```

profile of v0, /device:TPU:6, one launch (start us, length us, event | category | flops | bytes accessed | tf_op | source)
XLA Modules:
  0.0 242.8 jit_solution(11036003348992583538)
XLA Ops:
  6.5 0.0 copy-start
  6.5 0.0 copy-start.7
  6.5 0.9 reduce-window.8
  7.4 0.7 bitcast_subtract_fusion
  8.1 0.1 add_clamp_fusion
  8.2 0.1 min.18
  8.3 4.8 %gather_fusion = s32[768]{0:T(1024)S(1)} fusion(s32[256]{0:T(256)} %param.13, s32[1024]{0:T(1024)S(1)} %pad_clamp_fusion), kind=kCustom, calls=%fused_computation | custom fusion | bytes 9216 | tf_op jit(solution)/shard_map/jit(_take)/gather | solution.py:44
  13.1 0.1 gather.13
  13.2 0.0 copy-done.7
  13.2 0.7 select_select_fusion.1
  13.9 9.1 %all-to-all-start = ((s32[8,96,1]{1,2,0:T(1,128)}), s32[8,96,1]{1,2,0:T(1,128)S(1)}, u32[]{:S(2)}, u32[]{:S(2)}) async-start(s32[8,96,1]{1,2,0:T(1,128)} %bitcast.3), calls=%async_computation | async-start | bytes 8192 | tf_op jit(solution)/shard_map/all_to_all | solution.py:47
  22.9 0.1 iota_compare_fusion.6
  23.0 0.0 copy-done
  23.0 2.8 %gather_fusion.1 = bf16[768,1024]{1,0:T(8,128)(2,1)S(1)} fusion(bf16[256,1024]{1,0:T(8,128)(2,1)S(1)} %copy-done, s32[1024]{0:T(1024)S(1)} %pad_clamp_fusion), kind=kCustom, calls=%fused_computation.1 | custom fusion | bytes 3148800 | tf_op jit(solution)/shard_map/jit(_take)/gather | solution.py:42
  25.8 0.0 copy-start.3
  25.9 0.0 copy-start.1
  25.9 1.5 select_select_fusion
  27.3 0.0 copy-start.2
  27.3 0.0 all-to-all-done
  27.3 4.9 %all-to-all-start.1 = ((bf16[8,96,1024]{2,1,0:T(8,128)(2,1)}), bf16[8,96,1024]{2,1,0:T(8,128)(2,1)S(1)}, u32[]{:S(2)}, u32[]{:S(2)}) async-start(bf16[8,96,1024]{2,1,0:T(8,128)(2,1)} %select_select_fusion), calls=%async_computation.1 | async-start | bytes 3145728 | tf_op jit(solution)/shard_map/all_to_all | solution.py:46
  32.3 0.0 all-gather.2.cloned.1.call-start
  32.3 0.0 copy-done.3
  32.3 0.1 fusion.14
  32.4 0.2 reduce_window_sum.18
  32.5 0.2 select_reduce_fusion
  32.7 0.5 broadcast.229
  33.2 0.7 reduce.5
  33.9 0.1 eq.42
  34.0 17.8 %all-to-all-done.1 = bf16[8,96,1024]{2,1,0:T(8,128)(2,1)S(1)} async-done(((bf16[8,96,1024]{2,1,0:T(8,128)(2,1)}), bf16[8,96,1024]{2,1,0:T(8,128)(2,1)S(1)}, u32[]{:S(2)}, u32[]{:S(2)}) %all-to-all-start.1) | async-done | bytes 1572896 | tf_op jit(solution)/shard_map/all_to_all | solution.py:46
  51.8 0.0 copy-done.1
  51.8 0.0 copy-start.4
  51.8 0.0 copy-start.5
  51.8 0.0 copy-start.6
  51.8 0.5 multiply_reduce_fusion
  52.3 0.0 copy-start.8
  52.3 0.0 copy-done.2
  52.3 0.3 convolution_convert_fusion.1
  52.6 0.2 all_to_all.29
  52.9 46.8 %all_to_all.39 = bf16[64,3,1024]{2,1,0:T(4,128)(2,1)S(1)} all-to-all(bf16[64,3,1024]{2,1,0:T(4,128)(2,1)S(1)} %all_to_all.29), channel_id=1, replica_groups=mesh['dp'=8,'expert'=64] {'expert'}, dimensions={0} | all-to-all | bytes 786432 | tf_op jit(solution)/shard_map/all_to_all | solution.py:65
  99.7 1.1 all_to_all.31
  100.8 0.0 all-gather.2.cloned.1.call-update
  100.8 0.2 reduce-scatter.2.cloned.1.call-start
  101.1 0.0 copy-done.4
  101.1 0.0 copy-done.5
  101.1 0.0 copy-done.6
  101.1 25.4 %all-gather.2.cloned.1.call-done = bf16[1536,1024]{1,0:T(8,128)(2,1)} async-done(((bf16[192,1024]{1,0:T(8,128)(2,1)}), bf16[1536,1024]{1,0:T(8,128)(2,1)}) %all-gather.2.cloned.1.call-update) | async-done | bytes 3145744 | tf_op jit(solution)/shard_map/all_gather | solution.py:70
  126.6 0.6 broadcast_in_dim.67
  127.2 0.0 copy-done.8
  127.2 5.4 %fusion.5 = f32[1536,512]{1,0:T(8,128)} fusion(bf16[1536,1024]{1,0:T(8,128)(2,1)} %all-gather.2.cloned.1.call-done, bf16[64,8,8,128]{3,2,1,0:T(8,128)(2,1)S(1)} %bitcast.57, bf16[1,512,1024]{2,1,0:T(8,128)(2,1)S(1)} %copy-done.8), kind=kOutput, calls=%fused_computation.15 | convolution fusion | flops 1611137024 | bytes 8388608 | tf_op jit(solution)/shard_map/dot_general | solution.py:71
  132.6 0.6 broadcast_in_dim.69
  133.3 0.6 broadcast_in_dim.71
  133.9 8.9 %convolution_convert_fusion = bf16[1536,1024]{1,0:T(8,128)(2,1)} fusion(bf16[1536,1024]{1,0:T(8,128)(2,1)} %all-gather.2.cloned.1.call-done, f32[1536,512]{1,0:T(8,128)} %fusion.5, bf16[64,8,8,128]{3,2,1,0:T(8,128)(2,1)S(1)} %bitcast.56, bf16[64,8,8,128]{3,2,1,0:T(8,128)(2,1)S(1)} %bitcast.55, bf16[1,512,1024]{2,1,0:T(8,128)(2,1)} %param.20, ...), kind=kOutput, calls=%fused_computation.2 | convolution fusion | flops 3228565504 | bytes 13631488 | tf_op jit(solution)/shard_map/dot_general | solution.py:74
  142.8 0.0 reduce-scatter.2.cloned.1.call-update
  142.8 41.4 %reduce-scatter.2.cloned.1.call-done = bf16[192,1024]{1,0:T(8,128)(2,1)} async-done(((bf16[1536,1024]{1,0:T(8,128)(2,1)}), bf16[192,1024]{1,0:T(8,128)(2,1)}) %reduce-scatter.2.cloned.1.call-update) | async-done | bytes 393232 | tf_op jit(solution)/shard_map/reduce_scatter | solution.py:75
  184.2 1.4 all_to_all.32
  185.7 49.0 %all_to_all.40 = bf16[64,3,1024]{2,1,0:T(4,128)(2,1)S(1)} all-to-all(bf16[64,3,1024]{2,1,0:T(4,128)(2,1)S(1)} %all_to_all.32), channel_id=1, replica_groups=mesh['dp'=8,'expert'=64] {'expert'}, dimensions={0} | all-to-all | bytes 786432 | tf_op jit(solution)/shard_map/all_to_all | solution.py:78
  234.6 0.3 all_to_all.34
  234.9 1.0 fusion.1
  (10 shorter events, 0.1 us)
Async XLA Ops:
  6.5 16.5 %copy-start = (bf16[256,1024]{1,0:T(8,128)(2,1)S(1)}, bf16[256,1024]{1,0:T(8,128)(2,1)}, u32[]{:S(2)}) copy-start(bf16[256,1024]{1,0:T(8,128)(2,1)} %param.12) | copy-start | bytes 1572868
  6.5 6.6 %copy-start.7 = (s32[1,8]{1,0:T(1,128)S(1)}, s32[1,8]{1,0:T(1,128)}, u32[]{:S(2)}) copy-start(s32[1,8]{1,0:T(1,128)} %param.14) | copy-start | bytes 100
  13.9 13.5 %all-to-all-start = ((s32[8,96,1]{1,2,0:T(1,128)}), s32[8,96,1]{1,2,0:T(1,128)S(1)}, u32[]{:S(2)}, u32[]{:S(2)}) async-start(s32[8,96,1]{1,2,0:T(1,128)} %bitcast.3), calls=%async_computation | async-start | bytes 8192 | tf_op jit(solution)/shard_map/all_to_all | solution.py:47
  25.8 6.4 %copy-start.3 = (s32[128,1]{0,1:T(1,128)S(1)}, s32[128,1]{0,1:T(1,128)}, u32[]{:S(2)}) copy-start(s32[128,1]{0,1:T(1,128)} %param.17) | copy-start | bytes 1540
  25.9 25.9 %copy-start.1 = (bf16[128,1024]{1,0:T(8,128)(2,1)S(1)}, bf16[128,1024]{1,0:T(8,128)(2,1)}, u32[]{:S(2)}) copy-start(bf16[128,1024]{1,0:T(8,128)(2,1)} %param.15) | copy-start | bytes 786436
  27.3 25.0 %copy-start.2 = (f32[1024]{0:T(1024)S(1)}, f32[1024]{0:T(1024)}, u32[]{:S(2)}) copy-start(f32[1024]{0:T(1024)} %param.16) | copy-start | bytes 12292
  27.3 24.4 %all-to-all-start.1 = ((bf16[8,96,1024]{2,1,0:T(8,128)(2,1)}), bf16[8,96,1024]{2,1,0:T(8,128)(2,1)S(1)}, u32[]{:S(2)}, u32[]{:S(2)}) async-start(bf16[8,96,1024]{2,1,0:T(8,128)(2,1)} %select_select_fusion), calls=%async_computation.1 | async-start | bytes 3145728 | tf_op jit(solution)/shard_map/all_to_all | solution.py:46
  32.3 94.3 %all-gather.2.cloned.1.call-start = ((), (), s32[]{:S(2)}) async-start(), calls=%async_computation.5 | async-start | bytes 3538944 | tf_op jit(solution)/shard_map/all_gather | solution.py:70
  51.8 49.3 %copy-start.4 = (s32[1,4,8]{2,1,0:T(4,128)S(1)}, s32[1,4,8]{2,1,0:T(4,128)}, u32[]{:S(2)}) copy-start(s32[1,4,8]{2,1,0:T(4,128)} %param.21) | copy-start | bytes 388
  51.8 49.3 %copy-start.5 = (s32[1,4,8]{2,1,0:T(4,128)S(1)}, s32[1,4,8]{2,1,0:T(4,128)}, u32[]{:S(2)}) copy-start(s32[1,4,8]{2,1,0:T(4,128)} %param.22) | copy-start | bytes 388
  51.8 49.3 %copy-start.6 = (s32[1,4,8]{2,1,0:T(4,128)S(1)}, s32[1,4,8]{2,1,0:T(4,128)}, u32[]{:S(2)}) copy-start(s32[1,4,8]{2,1,0:T(4,128)} %param.23) | copy-start | bytes 388
  52.3 74.9 %copy-start.8 = (bf16[1,512,1024]{2,1,0:T(8,128)(2,1)S(1)}, bf16[1,512,1024]{2,1,0:T(8,128)(2,1)}, u32[]{:S(2)}) copy-start(bf16[1,512,1024]{2,1,0:T(8,128)(2,1)} %param.18) | copy-start | bytes 3145732
  100.8 83.4 %reduce-scatter.2.cloned.1.call-start = ((), (), s32[]{:S(2)}) async-start(), calls=%async_computation.6 | async-start | bytes 3538944 | tf_op jit(solution)/shard_map/reduce_scatter | solution.py:75
Sparse Core Ops, SparseCore 0:
  101.0 25.5 all-gather.1
  143.0 41.2 reduce-scatter.1
where the time goes:
time: 244 us; the launch traced here: 243 us
  blocking collectives  95.8 us (39%)
  waiting for transfers between devices  84.6 us (35%)
  matrix products  16.1 us (7%)
  starting transfers between devices  14.2 us (6%)
  between operations  13.6 us (6%)
  local copies, waits for them, and re-layouts  13.3 us (5%)
  other arithmetic  4.98 us (2%)
    all_to_all x1, blocking collectives, on_device(): lax.all_to_all(summed, 'expert', split_axis=0, concat_axis=0, tiled=True)  49 us
    all_to_all x1, blocking collectives, on_device(): lax.all_to_all(outgoing, 'expert', split_axis=0, concat_axis=0, tiled=True)  46.8 us
    reduce_scatter x1, waiting for transfers between devices, on_device(): lax.psum_scatter(partial_rows.astype(jnp.bfloat16), 'dp', scatter_dimensi...  41.4 us
    all_gather x1, waiting for transfers between devices, on_device(): block_rows = lax.all_gather(arrived, 'dp', axis=0, tiled=True)  25.4 us
    all_to_all x1, waiting for transfers between devices, on_device(): lax.all_to_all(slot_rows, 'dp', split_axis=0, concat_axis=0, tiled=True)  17.8 us
    all_to_all x1, starting transfers between devices, on_device(): lax.all_to_all(slot_bins, 'dp', split_axis=0, concat_axis=0, tiled=True)  9.1 us
    dot_general x1, matrix products, on_device(): partial_rows = jnp.dot(hidden, w_down, preferred_element_type=jnp.float32)  8.92 us
    dot_general x1, matrix products, on_device(): lax.dot_general(block_rows, w_gate, contract, preferred_element_type=jnp....  5.44 us
  transfers between devices with their start and end apart: 4, of which 3 were waited for; matrix products, arithmetic and copies ran while one was open for 2% of the time, Pallas kernels for 0%

commit v1 on v0

v1 whole, which is shorter than its diff:
```python
import functools

import jax
import jax.numpy as jnp
from jax import lax
from jax.experimental import pallas as pl
from jax.experimental.pallas import tpu as pltpu
from jax.sharding import PartitionSpec as P

QB = 128
CORES = 2


def dequant_kernel(gs, us, ds, gq, uq, dq, gw, uw, dw):
    row = pl.program_id(0)
    for s_ref, q_ref, w_ref in ((gs, gq, gw), (us, uq, uw), (ds, dq, dw)):
        for col in range(q_ref.shape[1] // QB):
            span = slice(col * QB, (col + 1) * QB)
            factor = jnp.exp2(jnp.full((QB, QB), s_ref[row, col], jnp.int32).astype(jnp.float32))
            w_ref[:, span] = q_ref[:, span] * factor.astype(jnp.bfloat16)


def dequantize_all(quants, scales):
    rows, cols = quants[0].shape
    block = pl.BlockSpec((QB, cols), lambda r: (r, 0))
    return pl.pallas_call(
        dequant_kernel,
        grid=(rows // QB,),
        in_specs=[pl.BlockSpec(memory_space=pltpu.SMEM)] * 3 + [block] * 3,
        out_specs=[block] * 3,
        out_shape=[jax.ShapeDtypeStruct((rows, cols), jnp.bfloat16)] * 3,
        name="dequantize",
    )(*scales, *quants)


def ffn_kernel(x_ref, *refs):
    weights, out_ref, total = refs[:6], refs[6], refs[7]
    contract = (((1,), (1,)), ((), ()))
    x = x_ref[...]
    part = jnp.zeros(total.shape, jnp.float32)
    for half in range(2):
        gate_w, up_w, down_w = weights[3 * half : 3 * half + 3]
        gate = lax.dot_general(x, gate_w[...], contract, preferred_element_type=jnp.float32)
        up = lax.dot_general(x, up_w[...], contract, preferred_element_type=jnp.float32)
        hidden = (gate / (1.0 + jnp.exp(-gate)) * up).astype(jnp.bfloat16)
        part = part + jnp.dot(hidden, down_w[...], preferred_element_type=jnp.float32)
    step = pl.program_id(0)

    @pl.when(step == 0)
    def _():
        total[...] = part

    @pl.when(step > 0)
    def _():
        total[...] += part

    @pl.when(step == pl.num_programs(0) - 1)
    def _():
        out_ref[...] = total[...].astype(out_ref.dtype)


def ffn(x, mine, theirs, chunk=256):
    rows, width = x.shape
    hidden = mine[0].shape[0]
    block = pl.BlockSpec((chunk, width), lambda h: (h, 0))
    whole = pl.BlockSpec((rows, width), lambda h: (0, 0))
    return pl.pallas_call(
        ffn_kernel,
        grid=(hidden // chunk,),
        in_specs=[whole] + [block] * 6,
        out_specs=whole,
        out_shape=jax.ShapeDtypeStruct((rows, width), jnp.bfloat16),
        scratch_shapes=[pltpu.VMEM((rows, width), jnp.float32)],
        compiler_params=pltpu.CompilerParams(vmem_limit_bytes=40 << 20),
        name="ffn",
    )(x, *mine, *theirs)


def on_device(
    cells,
    cell_bins,
    tile_counts,
    bin_base,
    norm_gain,
    expert_ids,
    gate_q,
    up_q,
    down_q,
    gate_scales,
    up_scales,
    down_scales,
):
    dp_size = lax.axis_size("dp")
    chips = dp_size // CORES
    expert_count = lax.axis_size("expert") * gate_q.shape[0]
    cell_total, width = cells.shape
    tile_bins = bin_base.shape[0]
    core = lax.axis_index("dp") % CORES
    to_core = [(i, i ^ 1) for i in range(dp_size)]

    def to_chip(k):
        return [(i, (i + CORES * k) % dp_size) for i in range(dp_size)]

    same_core = [[CORES * x + c for x in range(chips)] for c in range(CORES)]

    other_cells = lax.ppermute(cells, "dp", to_core)
    ends = jnp.cumsum(tile_counts[0])
    tile_of = jnp.sum(
        (jnp.arange(cell_total, dtype=jnp.int32)[None, :] >= ends[:, None]).astype(jnp.int32), axis=0
    )
    code = tile_of * tile_bins + cell_bins
    other_code = lax.ppermute(code, "dp", to_core)
    row = jnp.arange(chips * tile_bins, dtype=jnp.int32)
    wanted = (row // tile_bins * CORES + core) * tile_bins + row % tile_bins
    sums = jnp.dot(
        (wanted[:, None] == code[None, :]).astype(jnp.bfloat16), cells, preferred_element_type=jnp.float32
    ) + jnp.dot(
        (wanted[:, None] == other_code[None, :]).astype(jnp.bfloat16),
        other_cells,
        preferred_element_type=jnp.float32,
    )
    sums = sums.astype(jnp.bfloat16).reshape(chips, tile_bins, width)
    weights = dequantize_all(
        (gate_q[0], up_q[0], down_q[0]), (gate_scales[0], up_scales[0], down_scales[0])
    )
    *weights, sums = lax.optimization_barrier((*weights, sums))
    got = lax.all_to_all(
        sums, "dp", split_axis=0, concat_axis=0, tiled=True, axis_index_groups=same_core
    )
    other_weights = [lax.ppermute(w, "dp", to_core) for w in weights]
    residual_in = bin_base.astype(jnp.float32) + jnp.sum(got.astype(jnp.float32), axis=0)
    mean_sq = jnp.mean(residual_in * residual_in, axis=1, keepdims=True)
    normed = (residual_in * lax.rsqrt(mean_sq + 1e-06) * norm_gain[None, :]).astype(jnp.bfloat16)

    capacity = max(2, 3 * tile_bins // (2 * expert_count))
    expert_col = expert_ids[:, 0]
    one_hot = (expert_col[:, None] == jnp.arange(expert_count, dtype=jnp.int32)[None, :]).astype(
        jnp.int32
    )
    within = jnp.sum(jnp.cumsum(one_hot, axis=0) * one_hot, axis=1) - 1
    slot_of = expert_col * capacity + within
    slots = expert_count * capacity
    placer = (jnp.arange(slots, dtype=jnp.int32)[:, None] == slot_of[None, :]).astype(jnp.bfloat16)
    outgoing = jnp.dot(placer, normed, preferred_element_type=jnp.float32).astype(jnp.bfloat16)
    dense = (expert_count, capacity * width // QB, QB)
    arrived = lax.all_to_all(
        outgoing.reshape(dense), "expert", split_axis=0, concat_axis=0, tiled=True
    ).reshape(slots, width)

    others = [lax.ppermute(arrived, "dp", to_chip(k)) for k in range(1, chips)]
    total = ffn(arrived, weights, other_weights).astype(jnp.float32)
    for k, rows in enumerate(others, 1):
        back = lax.ppermute(ffn(rows, weights, other_weights), "dp", to_chip(chips - k))
        total = total + back.astype(jnp.float32)
    returned = lax.all_to_all(
        total.astype(jnp.bfloat16).reshape(dense), "expert", split_axis=0, concat_axis=0, tiled=True
    ).reshape(slots, width)
    expert_out = lax.dot_general(
        placer, returned, (((0,), (0,)), ((), ())), preferred_element_type=jnp.float32
    )
    return (residual_in + expert_out).astype(jnp.bfloat16)


def solution(mesh):
    split = P(("dp", "expert"), None)
    placed = (split, P(("dp", "expert")), split, split, P(), split) + (P("expert", "dp", None),) * 6
    return jax.shard_map(on_device, mesh=mesh, in_specs=placed, out_specs=split, check_vma=False)
```

time: 244 us -> 164 us (0.67)
  blocking collectives: 95.8 us -> 30.1 us
  waiting for transfers between devices: 84.6 us -> 44.1 us
  starting transfers between devices: 14.2 us -> 54.2 us
  Pallas kernels: 0 us -> 20 us
  between operations: 13.6 us -> 0.36 us
  matrix products: 16.1 us -> 5.07 us
  local copies, waits for them, and re-layouts: 13.3 us -> 4.05 us
    all_to_all x2 -> x1, blocking collectives: 95.8 us -> 30.1 us  [on_device(): lax.all_to_all(total.astype(jnp.bfloat16).reshape(dense), 'expert', split...]
    reduce_scatter x1 -> x0, waiting for transfers between devices: 41.4 us -> none  [on_device(): lax.psum_scatter(partial_rows.astype(jnp.bfloat16), 'dp', scatter_dimensi...]
    ppermute x0 -> x11, starting transfers between devices: none -> 30.6 us  [the longest x3 10.9 us: on_device(): lax.ppermute(ffn(rows, weights, other_weights), 'dp', to_chip(chips - k))]
    all_gather x1 -> x0, waiting for transfers between devices: 25.4 us -> none  [on_device(): block_rows = lax.all_gather(arrived, 'dp', axis=0, tiled=True)]
    pallas_call x0 -> x5, Pallas kernels: none -> 20 us  [the longest x4 15.6 us: ffn(): pl.pallas_call(ffn_kernel, grid=(hidden // chunk,), in_specs=[whole] + [b...]
    all_to_all x2, waiting for transfers between devices: 17.8 us -> 33.5 us  [the longest x1 20.4 us: on_device(): lax.all_to_all(outgoing.reshape(dense), 'expert', split_axis=0, concat_ax...]
    dot_general x3 -> x2, matrix products: 14.8 us -> 3 us  [the longest x1 1.53 us: on_device(): jnp.dot((wanted[:, None] == code[None, :]).astype(jnp.bfloat16), cells, p...]
    ppermute x0 -> x11, waiting for transfers between devices: none -> 10.6 us  [the longest x3 6.77 us: on_device(): others = [lax.ppermute(arrived, 'dp', to_chip(k)) for k in range(1, chips)]]
  transfers between devices with their start and end apart: 4 -> 13, of which waited for: 3 -> 4; matrix products, arithmetic and copies ran while one was open for 2% -> 3% of each run, Pallas kernels for 0% -> 12%
where the time goes in v1:
time: 164 us; the launch traced here: 160 us
  starting transfers between devices  54.2 us (33%)
  waiting for transfers between devices  44.1 us (27%)
  blocking collectives  30.1 us (18%)
  Pallas kernels  20 us (12%)
  matrix products  5.07 us (3%)
  local copies, waits for them, and re-layouts  4.05 us (2%)
  other arithmetic  2.64 us (2%)
    all_to_all x1, blocking collectives, on_device(): lax.all_to_all(total.astype(jnp.bfloat16).reshape(dense), 'expert', split...  30.1 us
    all_to_all x1, waiting for transfers between devices, on_device(): lax.all_to_all(outgoing.reshape(dense), 'expert', split_axis=0, concat_ax...  20.4 us
    pallas_call x4, Pallas kernels, ffn(): pl.pallas_call(ffn_kernel, grid=(hidden // chunk,), in_specs=[whole] + [b...  15.6 us
    all_to_all x1, starting transfers between devices, on_device(): lax.all_to_all(outgoing.reshape(dense), 'expert', split_axis=0, concat_ax...  14.1 us
    all_to_all x1, waiting for transfers between devices, on_device(): lax.all_to_all(sums, 'dp', split_axis=0, concat_axis=0, tiled=True, axis_...  13 us
    ppermute x3, starting transfers between devices, on_device(): lax.ppermute(ffn(rows, weights, other_weights), 'dp', to_chip(chips - k))  10.9 us
    all_to_all x1, starting transfers between devices, on_device(): lax.all_to_all(sums, 'dp', split_axis=0, concat_axis=0, tiled=True, axis_...  9.47 us
    ppermute x3, starting transfers between devices, on_device(): others = [lax.ppermute(arrived, 'dp', to_chip(k)) for k in range(1, chips)]  9.21 us
  transfers between devices with their start and end apart: 13, of which 4 were waited for; matrix products, arithmetic and copies ran while one was open for 3% of the time, Pallas kernels for 12%

profile of v1, /device:TPU:6, one launch (start us, length us, event | category | flops | bytes accessed | tf_op | source)
XLA Modules:
  0.0 160.4 jit_solution(16754717257950385836)
XLA Ops:
  0.0 1.9 %collective-permute-start.1 = (bf16[256,1024]{1,0:T(8,128)(2,1)}, bf16[256,1024]{1,0:T(8,128)(2,1)S(1)}, u32[]{:S(2)}, u32[]{:S(2)}) collective-permute-start(bf16[256,1024]{1,0:T(8,128)(2,1)} %param.12), channel_id=1, source_target_pairs={{0,64},{64,0},{128,192},{192,128},{256,320},{320,256},{384,448},{4... | collective-permute-start | bytes 1572872 | tf_op jit(solution)/shard_map/ppermute | solution.py:106
  1.9 0.8 reduce-window.8
  2.8 0.1 convert_reduce_fusion.1
  2.8 0.7 multiply_add_fusion
  3.5 2.4 %collective-permute-start = (s32[256]{0:T(256)S(1)}, s32[256]{0:T(256)S(1)}, u32[]{:S(2)}, u32[]{:S(2)}) collective-permute-start(s32[256]{0:T(256)S(1)} %multiply_add_fusion), channel_id=1, source_target_pairs={{0,64},{64,0},{128,192},{192,128},{256,320},{320,256},{384,448},{4... | collective-permute-start | bytes 3080 | tf_op jit(solution)/shard_map/ppermute | solution.py:112
  5.9 1.5 fusion.2
  7.5 4.4 %dequantize.1 = (bf16[512,1024]{1,0:T(8,128)(2,1)}, bf16[512,1024]{1,0:T(8,128)(2,1)}, bf16[512,1024]{1,0:T(8,128)(2,1)}) custom-call(s32[4,8]{1,0:T(4,128)} %bitcast.19, s32[4,8]{1,0:T(4,128)} %bitcast.20, s32[4,8]{1,0:T(4,128)} %bitcast.21, bf16[512,1024]{1,0:T(8,128)(2,1)} %bitcast.14, bf16[512,1024]{1,0:T(8,128)(2,1)} %bitcast.15, bf16[512,1024]{1,0:T(8,128)(2,1)} %bitcast.16), custom_call_target="tpu_custom_call" | custom-call | tf_op jit(solution)/shard_map/dequantize/pallas_call | solution.py:26
  11.9 0.0 collective-permute-done
  11.9 0.0 collective-permute-done.1
  11.9 1.5 add_convert_fusion
  13.4 9.5 %all-to-all-start = ((bf16[4,128,1024]{2,1,0:T(8,128)(2,1)}), bf16[4,128,1024]{2,1,0:T(8,128)(2,1)S(1)}, u32[]{:S(2)}, u32[]{:S(2)}) async-start(bf16[4,128,1024]{2,1,0:T(8,128)(2,1)} %bitcast.8), calls=%async_computation | async-start | bytes 2097152 | tf_op jit(solution)/shard_map/all_to_all | solution.py:127
  22.8 0.0 copy-done.8
  22.8 0.1 fusion.10
  22.9 0.2 reduce_window_sum.18
  23.1 0.2 select_reduce_fusion
  23.3 13.0 %all-to-all-done = bf16[4,128,1024]{2,1,0:T(8,128)(2,1)S(1)} async-done(((bf16[4,128,1024]{2,1,0:T(8,128)(2,1)}), bf16[4,128,1024]{2,1,0:T(8,128)(2,1)S(1)}, u32[]{:S(2)}, u32[]{:S(2)}) %all-to-all-start) | async-done | bytes 1048608 | tf_op jit(solution)/shard_map/all_to_all | solution.py:127
  36.3 0.2 convert_reduce_fusion
  36.5 0.0 copy-done.5
  36.5 0.0 copy-start.3
  36.5 0.0 copy-start
  36.5 0.0 copy-start.1
  36.6 0.0 copy-start.2
  36.6 0.2 multiply_reduce_fusion
  36.7 0.6 copy-done.3
  37.3 0.0 copy-done.7
  37.3 1.1 convolution_convert_fusion
  38.4 1.9 %reshape.86 = bf16[64,24,128]{2,1,0:T(8,128)(2,1)} reshape(bf16[192,1024]{1,0:T(8,128)(2,1)} %convolution_convert_fusion) | data formatting | bytes 786432 | tf_op jit(solution)/shard_map/reshape | solution.py:147
  40.3 14.1 %all-to-all-start.1 = ((bf16[64,24,128]{2,1,0:T(8,128)(2,1)}), bf16[64,24,128]{2,1,0:T(8,128)(2,1)}, u32[]{:S(2)}, u32[]{:S(2)}) async-start(bf16[64,24,128]{2,1,0:T(8,128)(2,1)} %reshape.86), calls=%async_computation.1 | async-start | bytes 786432 | tf_op jit(solution)/shard_map/all_to_all | solution.py:146
  54.5 0.0 copy-done
  54.5 1.9 %collective-permute-start.2 = (bf16[512,1024]{1,0:T(8,128)(2,1)S(1)}, bf16[512,1024]{1,0:T(8,128)(2,1)}, u32[]{:S(2)}, u32[]{:S(2)}) collective-permute-start(bf16[512,1024]{1,0:T(8,128)(2,1)S(1)} %copy-done), channel_id=1, source_target_pairs={{0,64},{64,0},{128,192},{192,128},{256,320},{320,256},{384,448},{4... | collective-permute-start | bytes 3145736 | tf_op jit(solution)/shard_map/ppermute | solution.py:130
  56.4 0.0 copy-done.1
  56.4 2.4 %collective-permute-start.3 = (bf16[512,1024]{1,0:T(8,128)(2,1)S(1)}, bf16[512,1024]{1,0:T(8,128)(2,1)}, u32[]{:S(2)}, u32[]{:S(2)}) collective-permute-start(bf16[512,1024]{1,0:T(8,128)(2,1)S(1)} %copy-done.1), channel_id=1, source_target_pairs={{0,64},{64,0},{128,192},{192,128},{256,320},{320,256},{384,448},{4... | collective-permute-start | bytes 3145736 | tf_op jit(solution)/shard_map/ppermute | solution.py:130
  58.8 0.0 copy-done.2
  58.8 1.9 %collective-permute-start.4 = (bf16[512,1024]{1,0:T(8,128)(2,1)S(1)}, bf16[512,1024]{1,0:T(8,128)(2,1)}, u32[]{:S(2)}, u32[]{:S(2)}) collective-permute-start(bf16[512,1024]{1,0:T(8,128)(2,1)S(1)} %copy-done.2), channel_id=1, source_target_pairs={{0,64},{64,0},{128,192},{192,128},{256,320},{320,256},{384,448},{4... | collective-permute-start | bytes 3145736 | tf_op jit(solution)/shard_map/ppermute | solution.py:130
  60.8 20.4 %all-to-all-done.1 = bf16[64,24,128]{2,1,0:T(8,128)(2,1)} async-done(((bf16[64,24,128]{2,1,0:T(8,128)(2,1)}), bf16[64,24,128]{2,1,0:T(8,128)(2,1)}, u32[]{:S(2)}, u32[]{:S(2)}) %all-to-all-start.1) | async-done | bytes 393248 | tf_op jit(solution)/shard_map/all_to_all | solution.py:146
  81.2 1.2 reshape.87.x_ref
  82.4 4.0 %collective-permute-start.5 = (bf16[192,1024]{1,0:T(8,128)(2,1)S(1)}, bf16[192,1024]{1,0:T(8,128)(2,1)S(1)}, u32[]{:S(2)}, u32[]{:S(2)}) collective-permute-start(bf16[192,1024]{1,0:T(8,128)(2,1)S(1)} %reshape.87.x_ref), channel_id=1, source_target_pairs={{0,128},{64,192},{128,256},{192,320},{256,384},{320,448},{384,0},{... | collective-permute-start | bytes 1179656 | tf_op jit(solution)/shard_map/ppermute | solution.py:150
  86.3 2.0 %collective-permute-start.7 = (bf16[192,1024]{1,0:T(8,128)(2,1)S(1)}, bf16[192,1024]{1,0:T(8,128)(2,1)S(1)}, u32[]{:S(2)}, u32[]{:S(2)}) collective-permute-start(bf16[192,1024]{1,0:T(8,128)(2,1)S(1)} %reshape.87.x_ref), channel_id=1, source_target_pairs={{0,256},{64,320},{128,384},{192,448},{256,0},{320,64},{384,128},{4... | collective-permute-start | bytes 1179656 | tf_op jit(solution)/shard_map/ppermute | solution.py:150
  88.3 0.0 collective-permute-done.2.refs_3_
  88.3 3.3 %collective-permute-start.9 = (bf16[192,1024]{1,0:T(8,128)(2,1)S(1)}, bf16[192,1024]{1,0:T(8,128)(2,1)S(1)}, u32[]{:S(2)}, u32[]{:S(2)}) collective-permute-start(bf16[192,1024]{1,0:T(8,128)(2,1)S(1)} %reshape.87.x_ref), channel_id=1, source_target_pairs={{0,384},{64,448},{128,0},{192,64},{256,128},{320,192},{384,256},{4... | collective-permute-start | bytes 1179656 | tf_op jit(solution)/shard_map/ppermute | solution.py:150
  91.6 0.0 collective-permute-done.3.refs_4_
  91.6 0.0 collective-permute-done.4.refs_5_
  91.6 6.8 %collective-permute-done.5.x_ref = bf16[192,1024]{1,0:T(8,128)(2,1)S(1)} collective-permute-done((bf16[192,1024]{1,0:T(8,128)(2,1)S(1)}, bf16[192,1024]{1,0:T(8,128)(2,1)S(1)}, u32[]{:S(2)}, u32[]{:S(2)}) %collective-permute-start.5) | collective-permute-done | bytes 393248 | tf_op jit(solution)/shard_map/ppermute | solution.py:150
  98.4 3.9 %ffn.5 = bf16[192,1024]{1,0:T(8,128)(2,1)S(1)} custom-call(bf16[192,1024]{1,0:T(8,128)(2,1)S(1)} %collective-permute-done.5.x_ref, bf16[512,1024]{1,0:T(8,128)(2,1)S(1)} %copy-done, bf16[512,1024]{1,0:T(8,128)(2,1)S(1)} %copy-done.1, bf16[512,1024]{1,0:T(8,128)(2,1)S(1)} %copy-done.2, bf16[512,1024]{1,0:T(8,128)(2,1)} %collective-permute-done.2.refs_3_, ...), custom_call_target="tpu_custom_call" | custom-call | tf_op jit(solution)/shard_map/ffn/pallas_call | solution.py:67
  102.3 1.9 %collective-permute-start.6 = (bf16[192,1024]{1,0:T(8,128)(2,1)S(1)}, bf16[192,1024]{1,0:T(8,128)(2,1)S(1)}, u32[]{:S(2)}, u32[]{:S(2)}) collective-permute-start(bf16[192,1024]{1,0:T(8,128)(2,1)S(1)} %ffn.5), channel_id=1, source_target_pairs={{0,384},{64,448},{128,0},{192,64},{256,128},{320,192},{384,256},{4... | collective-permute-start | bytes 1179656 | tf_op jit(solution)/shard_map/ppermute | solution.py:153
  104.2 0.0 collective-permute-done.7.x_ref
  104.2 3.9 %ffn.6 = bf16[192,1024]{1,0:T(8,128)(2,1)S(1)} custom-call(bf16[192,1024]{1,0:T(8,128)(2,1)S(1)} %collective-permute-done.7.x_ref, bf16[512,1024]{1,0:T(8,128)(2,1)S(1)} %copy-done, bf16[512,1024]{1,0:T(8,128)(2,1)S(1)} %copy-done.1, bf16[512,1024]{1,0:T(8,128)(2,1)S(1)} %copy-done.2, bf16[512,1024]{1,0:T(8,128)(2,1)} %collective-permute-done.2.refs_3_, ...), custom_call_target="tpu_custom_call" | custom-call | tf_op jit(solution)/shard_map/ffn/pallas_call | solution.py:67
  108.1 7.0 %collective-permute-start.8 = (bf16[192,1024]{1,0:T(8,128)(2,1)S(1)}, bf16[192,1024]{1,0:T(8,128)(2,1)S(1)}, u32[]{:S(2)}, u32[]{:S(2)}) collective-permute-start(bf16[192,1024]{1,0:T(8,128)(2,1)S(1)} %ffn.6), channel_id=1, source_target_pairs={{0,256},{64,320},{128,384},{192,448},{256,0},{320,64},{384,128},{4... | collective-permute-start | bytes 1179656 | tf_op jit(solution)/shard_map/ppermute | solution.py:153
  115.2 0.0 collective-permute-done.9.x_ref
  115.2 3.9 %ffn.7 = bf16[192,1024]{1,0:T(8,128)(2,1)S(1)} custom-call(bf16[192,1024]{1,0:T(8,128)(2,1)S(1)} %collective-permute-done.9.x_ref, bf16[512,1024]{1,0:T(8,128)(2,1)S(1)} %copy-done, bf16[512,1024]{1,0:T(8,128)(2,1)S(1)} %copy-done.1, bf16[512,1024]{1,0:T(8,128)(2,1)S(1)} %copy-done.2, bf16[512,1024]{1,0:T(8,128)(2,1)} %collective-permute-done.2.refs_3_, ...), custom_call_target="tpu_custom_call" | custom-call | tf_op jit(solution)/shard_map/ffn/pallas_call | solution.py:67
  119.1 1.9 %collective-permute-start.10 = (bf16[192,1024]{1,0:T(8,128)(2,1)S(1)}, bf16[192,1024]{1,0:T(8,128)(2,1)S(1)}, u32[]{:S(2)}, u32[]{:S(2)}) collective-permute-start(bf16[192,1024]{1,0:T(8,128)(2,1)S(1)} %ffn.7), channel_id=1, source_target_pairs={{0,128},{64,192},{128,256},{192,320},{256,384},{320,448},{384,0},{... | collective-permute-start | bytes 1179656 | tf_op jit(solution)/shard_map/ppermute | solution.py:153
  121.0 3.9 %ffn.4 = bf16[192,1024]{1,0:T(8,128)(2,1)S(1)} custom-call(bf16[192,1024]{1,0:T(8,128)(2,1)S(1)} %reshape.87.x_ref, bf16[512,1024]{1,0:T(8,128)(2,1)S(1)} %copy-done, bf16[512,1024]{1,0:T(8,128)(2,1)S(1)} %copy-done.1, bf16[512,1024]{1,0:T(8,128)(2,1)S(1)} %copy-done.2, bf16[512,1024]{1,0:T(8,128)(2,1)} %collective-permute-done.2.refs_3_, ...), custom_call_target="tpu_custom_call" | custom-call | tf_op jit(solution)/shard_map/ffn/pallas_call | solution.py:67
  124.9 0.0 copy-start.4
  124.9 0.0 copy-start.6
  124.9 0.0 collective-permute-done.6
  124.9 0.0 collective-permute-done.8
  124.9 3.8 %collective-permute-done.10 = bf16[192,1024]{1,0:T(8,128)(2,1)S(1)} collective-permute-done((bf16[192,1024]{1,0:T(8,128)(2,1)S(1)}, bf16[192,1024]{1,0:T(8,128)(2,1)S(1)}, u32[]{:S(2)}, u32[]{:S(2)}) %collective-permute-start.10) | collective-permute-done | bytes 393248 | tf_op jit(solution)/shard_map/ppermute | solution.py:153
  128.7 0.3 add_convert_fusion.1
  129.0 0.2 reshape.88
  129.2 30.1 %all_to_all.15 = bf16[64,24,128]{2,1,0:T(8,128)(2,1)S(1)} all-to-all(bf16[64,24,128]{2,1,0:T(8,128)(2,1)S(1)} %reshape.88), channel_id=1, replica_groups=mesh['dp'=8,'expert'=64] {'expert'}, dimensions={0} | all-to-all | bytes 786432 | tf_op jit(solution)/shard_map/all_to_all | solution.py:155
  159.2 0.2 reshape.89
  159.4 0.0 copy-done.4
  159.4 0.0 copy-done.6
  159.4 1.0 fusion
  (6 shorter events, 0.0 us)
Async XLA Ops:
  0.0 11.9 %collective-permute-start.1 = (bf16[256,1024]{1,0:T(8,128)(2,1)}, bf16[256,1024]{1,0:T(8,128)(2,1)S(1)}, u32[]{:S(2)}, u32[]{:S(2)}) collective-permute-start(bf16[256,1024]{1,0:T(8,128)(2,1)} %param.12), channel_id=1, source_target_pairs={{0,64},{64,0},{128,192},{192,128},{256,320},{320,256},{384,448},{4... | collective-permute-start | bytes 1572872 | tf_op jit(solution)/shard_map/ppermute | solution.py:106
  3.5 8.4 %collective-permute-start = (s32[256]{0:T(256)S(1)}, s32[256]{0:T(256)S(1)}, u32[]{:S(2)}, u32[]{:S(2)}) collective-permute-start(s32[256]{0:T(256)S(1)} %multiply_add_fusion), channel_id=1, source_target_pairs={{0,64},{64,0},{128,192},{192,128},{256,320},{320,256},{384,448},{4... | collective-permute-start | bytes 3080 | tf_op jit(solution)/shard_map/ppermute | solution.py:112
  11.9 11.0 %copy-start.8 = (s32[128,1]{0,1:T(1,128)S(1)}, s32[128,1]{0,1:T(1,128)}, u32[]{:S(2)}) copy-start(s32[128,1]{0,1:T(1,128)} %param.17) | copy-start | bytes 1540
  13.4 23.1 %copy-start.5 = (bf16[128,1024]{1,0:T(8,128)(2,1)S(1)}, bf16[128,1024]{1,0:T(8,128)(2,1)}, u32[]{:S(2)}) copy-start(bf16[128,1024]{1,0:T(8,128)(2,1)} %param.15) | copy-start | bytes 786436
  13.4 23.9 %copy-start.7 = (f32[1024]{0:T(1024)S(1)}, f32[1024]{0:T(1024)}, u32[]{:S(2)}) copy-start(f32[1024]{0:T(1024)} %param.16) | copy-start | bytes 12292
  13.4 23.0 %all-to-all-start = ((bf16[4,128,1024]{2,1,0:T(8,128)(2,1)}), bf16[4,128,1024]{2,1,0:T(8,128)(2,1)S(1)}, u32[]{:S(2)}, u32[]{:S(2)}) async-start(bf16[4,128,1024]{2,1,0:T(8,128)(2,1)} %bitcast.8), calls=%async_computation | async-start | bytes 2097152 | tf_op jit(solution)/shard_map/all_to_all | solution.py:127
  36.5 0.8 copy-start.3
  36.5 17.9 %copy-start = (bf16[512,1024]{1,0:T(8,128)(2,1)S(1)}, bf16[512,1024]{1,0:T(8,128)(2,1)}, u32[]{:S(2)}) copy-start(bf16[512,1024]{1,0:T(8,128)(2,1)} %get-tuple-element.16.refs_0_) | copy-start | bytes 3145732
  36.5 19.9 %copy-start.1 = (bf16[512,1024]{1,0:T(8,128)(2,1)S(1)}, bf16[512,1024]{1,0:T(8,128)(2,1)}, u32[]{:S(2)}) copy-start(bf16[512,1024]{1,0:T(8,128)(2,1)} %get-tuple-element.17.refs_1_) | copy-start | bytes 3145732
  36.6 22.3 %copy-start.2 = (bf16[512,1024]{1,0:T(8,128)(2,1)S(1)}, bf16[512,1024]{1,0:T(8,128)(2,1)}, u32[]{:S(2)}) copy-start(bf16[512,1024]{1,0:T(8,128)(2,1)} %get-tuple-element.18.refs_2_) | copy-start | bytes 3145732
  40.3 40.9 %all-to-all-start.1 = ((bf16[64,24,128]{2,1,0:T(8,128)(2,1)}), bf16[64,24,128]{2,1,0:T(8,128)(2,1)}, u32[]{:S(2)}, u32[]{:S(2)}) async-start(bf16[64,24,128]{2,1,0:T(8,128)(2,1)} %reshape.86), calls=%async_computation.1 | async-start | bytes 786432 | tf_op jit(solution)/shard_map/all_to_all | solution.py:146
  54.5 33.9 %collective-permute-start.2 = (bf16[512,1024]{1,0:T(8,128)(2,1)S(1)}, bf16[512,1024]{1,0:T(8,128)(2,1)}, u32[]{:S(2)}, u32[]{:S(2)}) collective-permute-start(bf16[512,1024]{1,0:T(8,128)(2,1)S(1)} %copy-done), channel_id=1, source_target_pairs={{0,64},{64,0},{128,192},{192,128},{256,320},{320,256},{384,448},{4... | collective-permute-start | bytes 3145736 | tf_op jit(solution)/shard_map/ppermute | solution.py:130
  56.4 35.2 %collective-permute-start.3 = (bf16[512,1024]{1,0:T(8,128)(2,1)S(1)}, bf16[512,1024]{1,0:T(8,128)(2,1)}, u32[]{:S(2)}, u32[]{:S(2)}) collective-permute-start(bf16[512,1024]{1,0:T(8,128)(2,1)S(1)} %copy-done.1), channel_id=1, source_target_pairs={{0,64},{64,0},{128,192},{192,128},{256,320},{320,256},{384,448},{4... | collective-permute-start | bytes 3145736 | tf_op jit(solution)/shard_map/ppermute | solution.py:130
  58.8 32.8 %collective-permute-start.4 = (bf16[512,1024]{1,0:T(8,128)(2,1)S(1)}, bf16[512,1024]{1,0:T(8,128)(2,1)}, u32[]{:S(2)}, u32[]{:S(2)}) collective-permute-start(bf16[512,1024]{1,0:T(8,128)(2,1)S(1)} %copy-done.2), channel_id=1, source_target_pairs={{0,64},{64,0},{128,192},{192,128},{256,320},{320,256},{384,448},{4... | collective-permute-start | bytes 3145736 | tf_op jit(solution)/shard_map/ppermute | solution.py:130
  82.4 16.0 %collective-permute-start.5 = (bf16[192,1024]{1,0:T(8,128)(2,1)S(1)}, bf16[192,1024]{1,0:T(8,128)(2,1)S(1)}, u32[]{:S(2)}, u32[]{:S(2)}) collective-permute-start(bf16[192,1024]{1,0:T(8,128)(2,1)S(1)} %reshape.87.x_ref), channel_id=1, source_target_pairs={{0,128},{64,192},{128,256},{192,320},{256,384},{320,448},{384,0},{... | collective-permute-start | bytes 1179656 | tf_op jit(solution)/shard_map/ppermute | solution.py:150
  86.3 17.9 %collective-permute-start.7 = (bf16[192,1024]{1,0:T(8,128)(2,1)S(1)}, bf16[192,1024]{1,0:T(8,128)(2,1)S(1)}, u32[]{:S(2)}, u32[]{:S(2)}) collective-permute-start(bf16[192,1024]{1,0:T(8,128)(2,1)S(1)} %reshape.87.x_ref), channel_id=1, source_target_pairs={{0,256},{64,320},{128,384},{192,448},{256,0},{320,64},{384,128},{4... | collective-permute-start | bytes 1179656 | tf_op jit(solution)/shard_map/ppermute | solution.py:150
  88.3 26.8 %collective-permute-start.9 = (bf16[192,1024]{1,0:T(8,128)(2,1)S(1)}, bf16[192,1024]{1,0:T(8,128)(2,1)S(1)}, u32[]{:S(2)}, u32[]{:S(2)}) collective-permute-start(bf16[192,1024]{1,0:T(8,128)(2,1)S(1)} %reshape.87.x_ref), channel_id=1, source_target_pairs={{0,384},{64,448},{128,0},{192,64},{256,128},{320,192},{384,256},{4... | collective-permute-start | bytes 1179656 | tf_op jit(solution)/shard_map/ppermute | solution.py:150
  102.3 22.6 %collective-permute-start.6 = (bf16[192,1024]{1,0:T(8,128)(2,1)S(1)}, bf16[192,1024]{1,0:T(8,128)(2,1)S(1)}, u32[]{:S(2)}, u32[]{:S(2)}) collective-permute-start(bf16[192,1024]{1,0:T(8,128)(2,1)S(1)} %ffn.5), channel_id=1, source_target_pairs={{0,384},{64,448},{128,0},{192,64},{256,128},{320,192},{384,256},{4... | collective-permute-start | bytes 1179656 | tf_op jit(solution)/shard_map/ppermute | solution.py:153
  108.1 16.8 %collective-permute-start.8 = (bf16[192,1024]{1,0:T(8,128)(2,1)S(1)}, bf16[192,1024]{1,0:T(8,128)(2,1)S(1)}, u32[]{:S(2)}, u32[]{:S(2)}) collective-permute-start(bf16[192,1024]{1,0:T(8,128)(2,1)S(1)} %ffn.6), channel_id=1, source_target_pairs={{0,256},{64,320},{128,384},{192,448},{256,0},{320,64},{384,128},{4... | collective-permute-start | bytes 1179656 | tf_op jit(solution)/shard_map/ppermute | solution.py:153
  119.1 9.7 %collective-permute-start.10 = (bf16[192,1024]{1,0:T(8,128)(2,1)S(1)}, bf16[192,1024]{1,0:T(8,128)(2,1)S(1)}, u32[]{:S(2)}, u32[]{:S(2)}) collective-permute-start(bf16[192,1024]{1,0:T(8,128)(2,1)S(1)} %ffn.7), channel_id=1, source_target_pairs={{0,128},{64,192},{128,256},{192,320},{256,384},{320,448},{384,0},{... | collective-permute-start | bytes 1179656 | tf_op jit(solution)/shard_map/ppermute | solution.py:153
  124.9 34.5 %copy-start.4 = (f32[128,1024]{1,0:T(8,128)S(1)}, f32[128,1024]{1,0:T(8,128)}, u32[]{:S(2)}) copy-start(f32[128,1024]{1,0:T(8,128)} %copy-done.3) | copy-start | bytes 1572868
  124.9 34.5 %copy-start.6 = (bf16[128,1024]{1,0:T(8,128)(2,1)S(1)}, bf16[128,1024]{1,0:T(8,128)(2,1)}, u32[]{:S(2)}) copy-start(bf16[128,1024]{1,0:T(8,128)(2,1)} %param.15) | copy-start | bytes 786436

commit v2 on v1

v2 whole, which is shorter than its diff:
```python
import jax
import jax.numpy as jnp
from jax import lax
from jax.experimental import pallas as pl
from jax.experimental.pallas import tpu as pltpu
from jax.sharding import PartitionSpec as P

QB = 128
CORES = 2
CHUNK = 256
LIMIT = 8 << 20


def in_vmem(x):
    return pltpu.with_memory_space_constraint(x, pltpu.VMEM)


def in_hbm(x):
    return pltpu.with_memory_space_constraint(x, pltpu.HBM)


def code_kernel(counts_ref, bins_ref, code_ref):
    total = bins_ref.shape[1]
    position = lax.broadcasted_iota(jnp.int32, (1, total), 1)
    tile = jnp.zeros((1, total), jnp.int32)
    run_end = jnp.int32(0)
    for k in range(counts_ref.shape[1]):
        run_end = run_end + counts_ref[0, k]
        tile = tile + (position >= run_end).astype(jnp.int32)
    code_ref[...] = tile * QB + bins_ref[...]


def codes(counts, bins):
    return pl.pallas_call(
        code_kernel,
        in_specs=[pl.BlockSpec(memory_space=pltpu.SMEM), pl.BlockSpec(memory_space=pltpu.VMEM)],
        out_specs=pl.BlockSpec(memory_space=pltpu.VMEM),
        out_shape=pltpu.VMEM(bins.shape, jnp.int32),
        compiler_params=pltpu.CompilerParams(vmem_limit_bytes=LIMIT),
        name="codes",
    )(in_hbm(counts), in_hbm(bins))


def splat_kernel(core_ref, code_ref, other_code_ref, cells_ref, other_cells_ref, out_ref, held, sem):
    copy = pltpu.make_async_copy(cells_ref, held, sem)
    copy.start()
    chips, rows, _ = out_ref.shape
    row = lax.broadcasted_iota(jnp.int32, (chips, rows, held.shape[0]), 1)
    chip = lax.broadcasted_iota(jnp.int32, (chips, rows, held.shape[0]), 0)
    bins = ((chip * CORES + core_ref[0]) * rows + row).reshape(chips * rows, held.shape[0])

    def summed(its_code, its_cells):
        match = (bins == its_code[...]).astype(jnp.float32).astype(jnp.bfloat16)
        return jnp.dot(match, its_cells[...], preferred_element_type=jnp.float32)

    total = summed(other_code_ref, other_cells_ref)
    copy.wait()
    total = total + summed(code_ref, held)
    out_ref[...] = total.astype(out_ref.dtype).reshape(out_ref.shape)


def splat(core, code, other_code, cells, other_cells, chips, tile_bins):
    vmem = pl.BlockSpec(memory_space=pltpu.VMEM)
    return pl.pallas_call(
        splat_kernel,
        in_specs=[pl.BlockSpec(memory_space=pltpu.SMEM), vmem, vmem, pl.BlockSpec(memory_space=pl.ANY), vmem],
        out_specs=vmem,
        out_shape=pltpu.VMEM((chips, tile_bins, cells.shape[1]), jnp.bfloat16),
        scratch_shapes=[pltpu.VMEM(cells.shape, jnp.bfloat16), pltpu.SemaphoreType.DMA],
        compiler_params=pltpu.CompilerParams(vmem_limit_bytes=LIMIT),
        name="splat",
    )(core, in_vmem(code), in_vmem(other_code), in_hbm(cells), in_vmem(other_cells))


def dequant_kernel(gs, us, ds, gq, uq, dq, *outs):
    hidden, width = gq.shape

    def scaled(s_ref, q_ref, row, col):
        block = q_ref[row * QB : (row + 1) * QB, col * QB : (col + 1) * QB]
        exponent = jnp.full((1, QB), s_ref[row, col], jnp.int32)
        return block * jnp.exp2(exponent.astype(jnp.float32)).astype(jnp.bfloat16)

    for row in range(hidden // QB):
        out, at = outs[row * QB // CHUNK], row * QB % CHUNK
        for col in range(width // QB):
            rows, cols = slice(row * QB, (row + 1) * QB), slice(col * QB, (col + 1) * QB)
            out[cols, at : at + QB] = scaled(gs, gq, row, col).T
            out[cols, CHUNK + at : CHUNK + at + QB] = scaled(us, uq, row, col).T
            outs[-1][rows, cols] = scaled(ds, dq, row, col)


def dequantize_all(quants, scales):
    rows, cols = quants[0].shape
    vmem = pl.BlockSpec(memory_space=pltpu.VMEM)
    chunks = rows // CHUNK
    return pl.pallas_call(
        dequant_kernel,
        in_specs=[pl.BlockSpec(memory_space=pltpu.SMEM)] * 3 + [vmem] * 3,
        out_specs=[vmem] * (chunks + 1),
        out_shape=[pltpu.HBM((cols, 2 * CHUNK), jnp.bfloat16)] * chunks
        + [pltpu.HBM((rows, cols), jnp.bfloat16)],
        compiler_params=pltpu.CompilerParams(vmem_limit_bytes=LIMIT),
        name="dequantize",
    )(*scales, *quants)


def route_kernel(got_ref, base_ref, gain_ref, slot_ref, out_ref, residual_ref, spread, kept, sem):
    residual = base_ref[...].astype(jnp.float32)
    for chip in range(got_ref.shape[0]):
        residual = residual + got_ref[chip].astype(jnp.float32)
    kept[...] = residual
    copy = pltpu.make_async_copy(kept, residual_ref, sem)
    copy.start()
    mean_sq = jnp.mean(residual * residual, axis=1, keepdims=True)
    normed = (residual * lax.rsqrt(mean_sq + 1e-06) * gain_ref[...]).astype(jnp.bfloat16)
    bins, width = residual.shape
    slots = out_ref.shape[0] * QB // width
    placer = lax.broadcasted_iota(jnp.int32, (slots, bins), 0) == slot_ref[...]
    placed = jnp.dot(
        placer.astype(jnp.float32).astype(jnp.bfloat16), normed, preferred_element_type=jnp.float32
    )
    spread_rows(placed, spread, out_ref)
    copy.wait()


def route(got, base, gain, slot_of, slots):
    bins, width = base.shape
    rows = slots * width // QB
    vmem = pl.BlockSpec(memory_space=pltpu.VMEM)
    return pl.pallas_call(
        route_kernel,
        in_specs=[vmem] * 4,
        out_specs=[vmem, pl.BlockSpec(memory_space=pltpu.HBM)],
        out_shape=[
            pltpu.VMEM((rows, QB), jnp.bfloat16),
            pltpu.HBM((bins, width), jnp.float32),
        ],
        scratch_shapes=[
            pltpu.VMEM((rows, QB), jnp.float32),
            pltpu.VMEM((bins, width), jnp.float32),
            pltpu.SemaphoreType.DMA,
        ],
        compiler_params=pltpu.CompilerParams(vmem_limit_bytes=LIMIT),
        name="route",
    )(in_vmem(got), in_vmem(base), gain, slot_of)


def through_experts(x, weights, wait=None):
    half = len(weights) // 2
    total = None
    for core in range(2):
        first, last = core * half, core * half + half - 1
        for i in range(first, last):
            if wait is not None:
                wait(i)
            both = jnp.dot(x, weights[i][...], preferred_element_type=jnp.float32)
            gate, up = both[:, :CHUNK], both[:, CHUNK:]
            hidden = (gate / (1.0 + jnp.exp(-gate)) * up).astype(jnp.bfloat16)
            if wait is not None and i == first:
                wait(last)
            at = (i - first) * CHUNK
            part = jnp.dot(hidden, weights[last][at : at + CHUNK, :], preferred_element_type=jnp.float32)
            total = part if total is None else total + part
    return total


def load_ffn_kernel(x_ref, *refs):
    count = (len(refs) - 2) // 2
    weights, out_ref, held, sems = refs[:count], refs[count], refs[count + 1 : -1], refs[-1]
    copies = [pltpu.make_async_copy(weights[i], held[i], sems.at[i]) for i in range(count)]
    for copy in copies:
        copy.start()
    out_ref[...] = through_experts(x_ref[...], held, lambda i: copies[i].wait()).astype(out_ref.dtype)


def load_ffn(x, weights):
    vmem = pl.BlockSpec(memory_space=pltpu.VMEM)
    hbm = pl.BlockSpec(memory_space=pltpu.HBM)
    out, *held = pl.pallas_call(
        load_ffn_kernel,
        in_specs=[vmem] + [hbm] * len(weights),
        out_specs=[vmem] * (1 + len(weights)),
        out_shape=[pltpu.VMEM(v.shape, jnp.bfloat16) for v in (x, *weights)],
        scratch_shapes=[pltpu.SemaphoreType.DMA((len(weights),))],
        compiler_params=pltpu.CompilerParams(vmem_limit_bytes=LIMIT),
        name="load_ffn",
    )(in_vmem(x), *(in_hbm(w) for w in weights))
    return out, held


def ffn_kernel(x_ref, *refs):
    *weights, out_ref = refs
    out_ref[...] = through_experts(x_ref[...], weights).astype(out_ref.dtype)


def ffn(x, weights):
    vmem = pl.BlockSpec(memory_space=pltpu.VMEM)
    return pl.pallas_call(
        ffn_kernel,
        in_specs=[vmem] * (1 + len(weights)),
        out_specs=vmem,
        out_shape=pltpu.VMEM(x.shape, jnp.bfloat16),
        compiler_params=pltpu.CompilerParams(vmem_limit_bytes=LIMIT),
        name="ffn",
    )(*(in_vmem(v) for v in (x, *weights)))


def spread_rows(rows, spread, out_ref):
    lanes = rows.shape[1] // QB
    for col in range(lanes):
        spread[pl.ds(col, rows.shape[0], stride=lanes), :] = rows[:, col * QB : (col + 1) * QB]
    out_ref[...] = spread[...].astype(out_ref.dtype)


def combine_kernel(*refs):
    *parts, out_ref, spread = refs
    total = parts[0][...].astype(jnp.float32)
    for part in parts[1:]:
        total = total + part[...].astype(jnp.float32)
    spread_rows(total, spread, out_ref)


def combine(parts):
    slots, width = parts[0].shape
    vmem = pl.BlockSpec(memory_space=pltpu.VMEM)
    rows = slots * width // QB
    return pl.pallas_call(
        combine_kernel,
        in_specs=[vmem] * len(parts),
        out_specs=vmem,
        out_shape=pltpu.VMEM((rows, QB), jnp.bfloat16),
        scratch_shapes=[pltpu.VMEM((rows, QB), jnp.float32)],
        compiler_params=pltpu.CompilerParams(vmem_limit_bytes=LIMIT),
        name="combine",
    )(*(in_vmem(part) for part in parts))


def on_device(
    cells,
    cell_bins,
    tile_counts,
    bin_base,
    norm_gain,
    expert_ids,
    gate_q,
    up_q,
    down_q,
    gate_scales,
    up_scales,
    down_scales,
):
    dp_size = lax.axis_size("dp")
    chips = dp_size // CORES
    expert_count = lax.axis_size("expert") * gate_q.shape[0]
    cell_total, width = cells.shape
    tile_bins = bin_base.shape[0]
    core = (lax.axis_index("dp") % CORES).astype(jnp.int32).reshape(1)
    to_core = [(i, i ^ 1) for i in range(dp_size)]

    def to_chip(k):
        return [(i, (i + CORES * k) % dp_size) for i in range(dp_size)]

    same_core = [[CORES * x + c for x in range(chips)] for c in range(CORES)]

    other_cells = lax.ppermute(cells, "dp", to_core)
    code = codes(tile_counts, cell_bins.reshape(1, cell_total))
    other_code = lax.ppermute(code, "dp", to_core)
    sums = splat(core, code, other_code, cells, other_cells, chips, tile_bins)
    quants = (gate_q[0], up_q[0], down_q[0])
    *quants, sums = lax.optimization_barrier((*quants, sums))
    got = lax.all_to_all(
        sums,
        "dp",
        split_axis=0,
        concat_axis=0,
        tiled=True,
        axis_index_groups=same_core,
    )
    mine = dequantize_all(quants, (gate_scales[0], up_scales[0], down_scales[0]))
    theirs = [lax.ppermute(w, "dp", to_core) for w in mine]

    capacity = max(2, 3 * tile_bins // (2 * expert_count))
    expert_col = expert_ids[:, 0]
    one_hot = (expert_col[:, None] == jnp.arange(expert_count, dtype=jnp.int32)[None, :]).astype(
        jnp.int32
    )
    within = jnp.sum(jnp.cumsum(one_hot, axis=0) * one_hot, axis=1) - 1
    slot_of = expert_col * capacity + within
    slots = expert_count * capacity
    outgoing, residual_in = route(
        got, bin_base, norm_gain.reshape(1, width), slot_of.reshape(1, tile_bins), slots
    )
    dense = (expert_count, capacity * width // QB, QB)
    arrived = lax.all_to_all(
        outgoing.reshape(dense), "expert", split_axis=0, concat_axis=0, tiled=True
    ).reshape(slots, width)

    others = [(k, lax.ppermute(arrived, "dp", to_chip(k))) for k in (1, chips - 1, *range(2, chips - 1))]
    own, held = load_ffn(arrived, [*mine, *theirs])
    backs = [lax.ppermute(ffn(there, held), "dp", to_chip(chips - k)) for k, there in others]
    returned = lax.all_to_all(
        combine([own, *backs]).reshape(dense), "expert", split_axis=0, concat_axis=0, tiled=True
    ).reshape(slots, width)
    placer = (jnp.arange(slots, dtype=jnp.int32)[:, None] == slot_of[None, :]).astype(jnp.bfloat16)
    expert_out = lax.dot_general(
        placer, returned, (((0,), (0,)), ((), ())), preferred_element_type=jnp.float32
    )
    return (residual_in + expert_out).astype(jnp.bfloat16)


def solution(mesh):
    split = P(("dp", "expert"), None)
    placed = (split, P(("dp", "expert")), split, split, P(), split) + (P("expert", "dp", None),) * 6
    return jax.shard_map(on_device, mesh=mesh, in_specs=placed, out_specs=split, check_vma=False)
```

time: 164 us -> 150 us (0.915); the launches traced: 160 us -> 150 us
  blocking collectives: 30.1 us -> 0 us
  waiting for transfers between devices: 44.1 us -> 64.1 us
  starting transfers between devices: 54.2 us -> 62.2 us
  matrix products: 5.07 us -> 0.98 us
  other arithmetic: 2.64 us -> 0.43 us
  Pallas kernels: 20 us -> 18.2 us
    all_to_all x1 -> x0, blocking collectives: 30.1 us -> none  [on_device(): lax.all_to_all(total.astype(jnp.bfloat16).reshape(dense), 'expert', split...]
    all_to_all x0 -> x1, waiting for transfers between devices: none -> 22.8 us  [on_device(): lax.all_to_all(combine([own, *backs]).reshape(dense), 'expert', split_axi...]
    all_to_all x0 -> x1, starting transfers between devices: none -> 7.74 us  [on_device(): lax.all_to_all(combine([own, *backs]).reshape(dense), 'expert', split_axi...]
    all_to_all x1, waiting for transfers between devices: 20.4 us -> 16.2 us  [on_device(): lax.all_to_all(outgoing.reshape(dense), 'expert', split_axis=0, concat_ax...]
    dot_general x3 -> x0, matrix products: 4.09 us -> none  [the longest x1 1.53 us: on_device(): jnp.dot((wanted[:, None] == code[None, :]).astype(jnp.bfloat16), cells, p...]
    unnamed x18 -> x24, local copies, waits for them, and re-layouts: 0.62 us -> 2.87 us
    reshape x3 -> x1, local copies, waits for them, and re-layouts: 2.27 us -> 0.17 us  [on_device(): returned = lax.all_to_all(combine([own, *backs]).reshape(dense), 'expert'...]
    pallas_call x5 -> x9, Pallas kernels: 20 us -> 18.2 us  [the longest x3 5.29 us: ffn(): pl.pallas_call(ffn_kernel, in_specs=[vmem] * (1 + len(weights)), out_spec...]
  transfers between devices with their start and end apart: 13 -> 14, of which waited for: 4 -> 7; matrix products, arithmetic and copies ran while one was open for 3% -> 0% of each run, Pallas kernels for 12% -> 8%
where the time goes in v2:
time: 150 us
  waiting for transfers between devices  64.1 us (43%)
  starting transfers between devices  62.2 us (41%)
  Pallas kernels  18.2 us (12%)
  local copies, waits for them, and re-layouts  3.21 us (2%)
    all_to_all x1, waiting for transfers between devices, on_device(): lax.all_to_all(combine([own, *backs]).reshape(dense), 'expert', split_axi...  22.8 us
    all_to_all x1, waiting for transfers between devices, on_device(): lax.all_to_all(outgoing.reshape(dense), 'expert', split_axis=0, concat_ax...  16.2 us
    all_to_all x1, starting transfers between devices, on_device(): lax.all_to_all(outgoing.reshape(dense), 'expert', split_axis=0, concat_ax...  13.9 us
    all_to_all x1, waiting for transfers between devices, on_device(): lax.all_to_all(sums, 'dp', split_axis=0, concat_axis=0, tiled=True, axis_...  13.3 us
    ppermute x3, starting transfers between devices, on_device(): lax.ppermute(ffn(there, held), 'dp', to_chip(chips - k))  10.9 us
    ppermute x3, starting transfers between devices, on_device(): lax.ppermute(arrived, 'dp', to_chip(k))  9.82 us
    all_to_all x1, starting transfers between devices, on_device(): lax.all_to_all(sums, 'dp', split_axis=0, concat_axis=0, tiled=True, axis_...  9.35 us
    ppermute x3, waiting for transfers between devices, on_device(): lax.ppermute(ffn(there, held), 'dp', to_chip(chips - k))  7.8 us
  transfers between devices with their start and end apart: 14, of which 7 were waited for; matrix products, arithmetic and copies ran while one was open for 0% of the time, Pallas kernels for 8%

profile of v2, /device:TPU:6, one launch (start us, length us, event | category | flops | bytes accessed | tf_op | source)
XLA Modules:
  0.0 149.5 jit_solution(6775940565267449645)
XLA Ops:
  0.0 1.9 %collective-permute-start.1 = (bf16[256,1024]{1,0:T(8,128)(2,1)}, bf16[256,1024]{1,0:T(8,128)(2,1)S(1)}, u32[]{:S(2)}, u32[]{:S(2)}) collective-permute-start(bf16[256,1024]{1,0:T(8,128)(2,1)} %cells_ref.1), channel_id=1, source_target_pairs={{0,64},{64,0},{128,192},{192,128},{256,320},{320,256},{384,448},{4... | collective-permute-start | bytes 1572872 | tf_op jit(solution)/shard_map/ppermute | solution.py:265
  1.9 0.7 codes.1.code_ref
  2.6 2.4 %collective-permute-start = (s32[1,256]{1,0:T(1,128)S(1)}, s32[1,256]{1,0:T(1,128)S(1)}, u32[]{:S(2)}, u32[]{:S(2)}) collective-permute-start(s32[1,256]{1,0:T(1,128)S(1)} %codes.1.code_ref), channel_id=1, source_target_pairs={{0,64},{64,0},{128,192},{192,128},{256,320},{320,256},{384,448},{4... | collective-permute-start | bytes 3080 | tf_op jit(solution)/shard_map/ppermute | solution.py:267
  5.1 0.8 collective-permute-done.other_code_ref
  5.8 0.0 collective-permute-done.1.other_cells_ref
  5.8 2.8 %splat.1 = bf16[4,128,1024]{2,1,0:T(8,128)(2,1)} custom-call(s32[1]{0:T(128)} %bitcast.3.core_ref, s32[1,256]{1,0:T(1,128)S(1)} %codes.1.code_ref, s32[1,256]{1,0:T(1,128)S(1)} %collective-permute-done.other_code_ref, bf16[256,1024]{1,0:T(8,128)(2,1)} %cells_ref.1, bf16[256,1024]{1,0:T(8,128)(2,1)S(1)} %collective-permute-done.1.other_cells_ref), custom_call_target="tpu_custom_call" | custom-call | tf_op jit(solution)/shard_map/splat/pallas_call | solution.py:64
  8.6 0.0 copy-start.11
  8.6 9.4 %all-to-all-start = ((bf16[4,128,1024]{2,1,0:T(8,128)(2,1)}), bf16[4,128,1024]{2,1,0:T(8,128)(2,1)S(1)}, u32[]{:S(2)}, u32[]{:S(2)}) async-start(bf16[4,128,1024]{2,1,0:T(8,128)(2,1)} %splat.1), calls=%async_computation | async-start | bytes 2097152 | tf_op jit(solution)/shard_map/all_to_all | solution.py:271
  18.0 0.0 copy-start.3
  18.0 0.0 copy-done.11
  18.0 0.1 fusion.1
  18.1 0.2 reduce_window_sum.11
  18.3 0.0 copy-start.4
  18.3 0.2 select_reduce_fusion
  18.4 13.3 %all-to-all-done.got_ref = bf16[4,128,1024]{2,1,0:T(8,128)(2,1)S(1)} async-done(((bf16[4,128,1024]{2,1,0:T(8,128)(2,1)}), bf16[4,128,1024]{2,1,0:T(8,128)(2,1)S(1)}, u32[]{:S(2)}, u32[]{:S(2)}) %all-to-all-start) | async-done | bytes 1048608 | tf_op jit(solution)/shard_map/all_to_all | solution.py:271
  31.8 0.0 copy-done.3
  31.8 0.0 copy-done.4
  31.8 1.8 %route.1 = (bf16[1536,128]{1,0:T(8,128)(2,1)}, f32[128,1024]{1,0:T(8,128)}) custom-call(bf16[4,128,1024]{2,1,0:T(8,128)(2,1)S(1)} %all-to-all-done.got_ref, bf16[128,1024]{1,0:T(8,128)(2,1)S(1)} %copy-done.3, f32[1,1024]{1,0:T(1,128)S(1)} %bitcast.21, s32[1,128]{1,0:T(1,128)S(1)} %bitcast_add_fusion.slot_ref), custom_call_target="tpu_custom_call" | custom-call | tf_op jit(solution)/shard_map/route/pallas_call | solution.py:130
  33.6 0.0 copy-start.7
  33.6 13.9 %all-to-all-start.1 = ((bf16[64,24,128]{2,1,0:T(8,128)(2,1)}), bf16[64,24,128]{2,1,0:T(8,128)(2,1)S(1)}, u32[]{:S(2)}, u32[]{:S(2)}) async-start(bf16[64,24,128]{2,1,0:T(8,128)(2,1)} %bitcast.9), calls=%async_computation.1 | async-start | bytes 786432 | tf_op jit(solution)/shard_map/all_to_all | solution.py:294
  47.6 0.0 copy-start.6
  47.6 0.0 copy-start.5
  47.6 0.0 copy-done
  47.6 0.0 copy-done.1
  47.6 0.0 copy-done.7
  47.6 0.6 copy-done.6
  48.2 0.0 copy-done.5
  48.3 1.2 copy-done.2
  49.5 2.8 %dequantize.1 = (bf16[1024,512]{1,0:T(8,128)(2,1)}, bf16[1024,512]{1,0:T(8,128)(2,1)}, bf16[512,1024]{1,0:T(8,128)(2,1)}) custom-call(s32[4,8]{1,0:T(4,128)S(1)} %bitcast.22, s32[4,8]{1,0:T(4,128)S(1)} %bitcast.23, s32[4,8]{1,0:T(4,128)S(1)} %bitcast.24, bf16[512,1024]{1,0:T(8,128)(2,1)S(1)} %bitcast.18, bf16[512,1024]{1,0:T(8,128)(2,1)S(1)} %bitcast.19, ...), custom_call_target="tpu_custom_call" | custom-call | tf_op jit(solution)/shard_map/dequantize/pallas_call | solution.py:96
  52.3 1.9 %collective-permute-start.2 = (bf16[1024,512]{1,0:T(8,128)(2,1)}, bf16[1024,512]{1,0:T(8,128)(2,1)S(1)}, u32[]{:S(2)}, u32[]{:S(2)}) collective-permute-start(bf16[1024,512]{1,0:T(8,128)(2,1)} %get-tuple-element.27.refs_0_), channel_id=1, source_target_pairs={{0,64},{64,0},{128,192},{192,128},{256,320},{320,256},{384,448},{4... | collective-permute-start | bytes 3145736 | tf_op jit(solution)/shard_map/ppermute | solution.py:280
  54.2 2.4 %collective-permute-start.3 = (bf16[1024,512]{1,0:T(8,128)(2,1)}, bf16[1024,512]{1,0:T(8,128)(2,1)S(1)}, u32[]{:S(2)}, u32[]{:S(2)}) collective-permute-start(bf16[1024,512]{1,0:T(8,128)(2,1)} %get-tuple-element.28.refs_1_), channel_id=1, source_target_pairs={{0,64},{64,0},{128,192},{192,128},{256,320},{320,256},{384,448},{4... | collective-permute-start | bytes 3145736 | tf_op jit(solution)/shard_map/ppermute | solution.py:280
  56.6 1.9 %collective-permute-start.4 = (bf16[512,1024]{1,0:T(8,128)(2,1)}, bf16[512,1024]{1,0:T(8,128)(2,1)}, u32[]{:S(2)}, u32[]{:S(2)}) collective-permute-start(bf16[512,1024]{1,0:T(8,128)(2,1)} %get-tuple-element.29.refs_2_), channel_id=1, source_target_pairs={{0,64},{64,0},{128,192},{192,128},{256,320},{320,256},{384,448},{4... | collective-permute-start | bytes 3145736 | tf_op jit(solution)/shard_map/ppermute | solution.py:280
  58.5 16.2 %all-to-all-done.1 = bf16[64,24,128]{2,1,0:T(8,128)(2,1)S(1)} async-done(((bf16[64,24,128]{2,1,0:T(8,128)(2,1)}), bf16[64,24,128]{2,1,0:T(8,128)(2,1)S(1)}, u32[]{:S(2)}, u32[]{:S(2)}) %all-to-all-start.1) | async-done | bytes 393248 | tf_op jit(solution)/shard_map/all_to_all | solution.py:294
  74.7 0.2 reshape.51.x_ref
  74.9 4.0 %collective-permute-start.5 = (bf16[192,1024]{1,0:T(8,128)(2,1)S(1)}, bf16[192,1024]{1,0:T(8,128)(2,1)S(1)}, u32[]{:S(2)}, u32[]{:S(2)}) collective-permute-start(bf16[192,1024]{1,0:T(8,128)(2,1)S(1)} %reshape.51.x_ref), channel_id=1, source_target_pairs={{0,128},{64,192},{128,256},{192,320},{256,384},{320,448},{384,0},{... | collective-permute-start | bytes 1179656 | tf_op jit(solution)/shard_map/ppermute | solution.py:298
  78.8 1.9 %collective-permute-start.7 = (bf16[192,1024]{1,0:T(8,128)(2,1)S(1)}, bf16[192,1024]{1,0:T(8,128)(2,1)S(1)}, u32[]{:S(2)}, u32[]{:S(2)}) collective-permute-start(bf16[192,1024]{1,0:T(8,128)(2,1)S(1)} %reshape.51.x_ref), channel_id=1, source_target_pairs={{0,384},{64,448},{128,0},{192,64},{256,128},{320,192},{384,256},{4... | collective-permute-start | bytes 1179656 | tf_op jit(solution)/shard_map/ppermute | solution.py:298
  80.8 0.0 collective-permute-done.2.refs_3_
  80.8 0.0 copy-start.8
  80.8 3.9 %collective-permute-start.9 = (bf16[192,1024]{1,0:T(8,128)(2,1)S(1)}, bf16[192,1024]{1,0:T(8,128)(2,1)S(1)}, u32[]{:S(2)}, u32[]{:S(2)}) collective-permute-start(bf16[192,1024]{1,0:T(8,128)(2,1)S(1)} %reshape.51.x_ref), channel_id=1, source_target_pairs={{0,256},{64,320},{128,384},{192,448},{256,0},{320,64},{384,128},{4... | collective-permute-start | bytes 1179656 | tf_op jit(solution)/shard_map/ppermute | solution.py:298
  84.7 0.0 collective-permute-done.3.refs_4_
  84.7 0.0 copy-start.9
  84.7 0.0 collective-permute-done.4.refs_5_
  84.8 0.0 copy-done.8
  84.8 0.9 copy-done.9
  85.7 3.7 %load_ffn.1 = (bf16[192,1024]{1,0:T(8,128)(2,1)S(1)}, bf16[1024,512]{1,0:T(8,128)(2,1)S(1)}, bf16[1024,512]{1,0:T(8,128)(2,1)S(1)}, bf16[512,1024]{1,0:T(8,128)(...) custom-call(bf16[192,1024]{1,0:T(8,128)(2,1)S(1)} %reshape.51.x_ref, ...), custom_call_target="tpu_custom_call" | custom-call | tf_op jit(solution)/shard_map/load_ffn/pallas_call | solution.py:179
  89.4 3.2 %collective-permute-done.5.x_ref = bf16[192,1024]{1,0:T(8,128)(2,1)S(1)} collective-permute-done((bf16[192,1024]{1,0:T(8,128)(2,1)S(1)}, bf16[192,1024]{1,0:T(8,128)(2,1)S(1)}, u32[]{:S(2)}, u32[]{:S(2)}) %collective-permute-start.5) | collective-permute-done | bytes 393248 | tf_op jit(solution)/shard_map/ppermute | solution.py:298
  92.6 1.8 %ffn.3 = bf16[192,1024]{1,0:T(8,128)(2,1)S(1)} custom-call(bf16[192,1024]{1,0:T(8,128)(2,1)S(1)} %collective-permute-done.5.x_ref, bf16[1024,512]{1,0:T(8,128)(2,1)S(1)} %get-tuple-element.31.refs_0_, bf16[1024,512]{1,0:T(8,128)(2,1)S(1)} %get-tuple-element.32.refs_1_, bf16[512,1024]{1,0:T(8,128)(2,1)S(1)} %get-tuple-element.33.refs_2_, ...), custom_call_target="tpu_custom_call" | custom-call | tf_op jit(solution)/shard_map/ffn/pallas_call | solution.py:198
  94.3 1.9 %collective-permute-start.6 = (bf16[192,1024]{1,0:T(8,128)(2,1)S(1)}, bf16[192,1024]{1,0:T(8,128)(2,1)S(1)}, u32[]{:S(2)}, u32[]{:S(2)}) collective-permute-start(bf16[192,1024]{1,0:T(8,128)(2,1)S(1)} %ffn.3), channel_id=1, source_target_pairs={{0,384},{64,448},{128,0},{192,64},{256,128},{320,192},{384,256},{4... | collective-permute-start | bytes 1179656 | tf_op jit(solution)/shard_map/ppermute | solution.py:300
  96.3 0.0 collective-permute-done.7.x_ref
  96.3 1.8 %ffn.4 = bf16[192,1024]{1,0:T(8,128)(2,1)S(1)} custom-call(bf16[192,1024]{1,0:T(8,128)(2,1)S(1)} %collective-permute-done.7.x_ref, bf16[1024,512]{1,0:T(8,128)(2,1)S(1)} %get-tuple-element.31.refs_0_, bf16[1024,512]{1,0:T(8,128)(2,1)S(1)} %get-tuple-element.32.refs_1_, bf16[512,1024]{1,0:T(8,128)(2,1)S(1)} %get-tuple-element.33.refs_2_, ...), custom_call_target="tpu_custom_call" | custom-call | tf_op jit(solution)/shard_map/ffn/pallas_call | solution.py:198
  98.1 5.6 %collective-permute-start.8 = (bf16[192,1024]{1,0:T(8,128)(2,1)S(1)}, bf16[192,1024]{1,0:T(8,128)(2,1)S(1)}, u32[]{:S(2)}, u32[]{:S(2)}) collective-permute-start(bf16[192,1024]{1,0:T(8,128)(2,1)S(1)} %ffn.4), channel_id=1, source_target_pairs={{0,128},{64,192},{128,256},{192,320},{256,384},{320,448},{384,0},{... | collective-permute-start | bytes 1179656 | tf_op jit(solution)/shard_map/ppermute | solution.py:300
  103.6 0.0 collective-permute-done.9.x_ref
  103.6 1.8 %ffn.5 = bf16[192,1024]{1,0:T(8,128)(2,1)S(1)} custom-call(bf16[192,1024]{1,0:T(8,128)(2,1)S(1)} %collective-permute-done.9.x_ref, bf16[1024,512]{1,0:T(8,128)(2,1)S(1)} %get-tuple-element.31.refs_0_, bf16[1024,512]{1,0:T(8,128)(2,1)S(1)} %get-tuple-element.32.refs_1_, bf16[512,1024]{1,0:T(8,128)(2,1)S(1)} %get-tuple-element.33.refs_2_, ...), custom_call_target="tpu_custom_call" | custom-call | tf_op jit(solution)/shard_map/ffn/pallas_call | solution.py:198
  105.4 3.4 %collective-permute-start.10 = (bf16[192,1024]{1,0:T(8,128)(2,1)S(1)}, bf16[192,1024]{1,0:T(8,128)(2,1)S(1)}, u32[]{:S(2)}, u32[]{:S(2)}) collective-permute-start(bf16[192,1024]{1,0:T(8,128)(2,1)S(1)} %ffn.5), channel_id=1, source_target_pairs={{0,256},{64,320},{128,384},{192,448},{256,0},{320,64},{384,128},{4... | collective-permute-start | bytes 1179656 | tf_op jit(solution)/shard_map/ppermute | solution.py:300
  108.8 1.1 collective-permute-done.6.refs_1_
  109.9 0.0 collective-permute-done.8.refs_2_
  109.9 6.7 %collective-permute-done.10.refs_3_ = bf16[192,1024]{1,0:T(8,128)(2,1)S(1)} collective-permute-done((bf16[192,1024]{1,0:T(8,128)(2,1)S(1)}, bf16[192,1024]{1,0:T(8,128)(2,1)S(1)}, u32[]{:S(2)}, u32[]{:S(2)}) %collective-permute-start.10) | collective-permute-done | bytes 393248 | tf_op jit(solution)/shard_map/ppermute | solution.py:300
  116.6 1.2 combine.1
  117.8 7.7 %all-to-all-start.2 = ((bf16[64,24,128]{2,1,0:T(8,128)(2,1)}), bf16[64,24,128]{2,1,0:T(8,128)(2,1)S(1)}, u32[]{:S(2)}, u32[]{:S(2)}) async-start(bf16[64,24,128]{2,1,0:T(8,128)(2,1)} %bitcast.13), calls=%async_computation.2 | async-start | bytes 786432 | tf_op jit(solution)/shard_map/all_to_all | solution.py:301
  125.5 0.0 copy-start.10
  125.5 22.8 %all-to-all-done.2 = bf16[64,24,128]{2,1,0:T(8,128)(2,1)S(1)} async-done(((bf16[64,24,128]{2,1,0:T(8,128)(2,1)}), bf16[64,24,128]{2,1,0:T(8,128)(2,1)S(1)}, u32[]{:S(2)}, u32[]{:S(2)}) %all-to-all-start.2) | async-done | bytes 393248 | tf_op jit(solution)/shard_map/all_to_all | solution.py:301
  148.4 0.2 reshape.53
  148.6 0.0 copy-done.10
  148.6 1.0 fusion
  (5 shorter events, 0.0 us)
Async XLA Ops:
  0.0 5.8 %collective-permute-start.1 = (bf16[256,1024]{1,0:T(8,128)(2,1)}, bf16[256,1024]{1,0:T(8,128)(2,1)S(1)}, u32[]{:S(2)}, u32[]{:S(2)}) collective-permute-start(bf16[256,1024]{1,0:T(8,128)(2,1)} %cells_ref.1), channel_id=1, source_target_pairs={{0,64},{64,0},{128,192},{192,128},{256,320},{320,256},{384,448},{4... | collective-permute-start | bytes 1572872 | tf_op jit(solution)/shard_map/ppermute | solution.py:265
  2.6 3.2 %collective-permute-start = (s32[1,256]{1,0:T(1,128)S(1)}, s32[1,256]{1,0:T(1,128)S(1)}, u32[]{:S(2)}, u32[]{:S(2)}) collective-permute-start(s32[1,256]{1,0:T(1,128)S(1)} %codes.1.code_ref), channel_id=1, source_target_pairs={{0,64},{64,0},{128,192},{192,128},{256,320},{320,256},{384,448},{4... | collective-permute-start | bytes 3080 | tf_op jit(solution)/shard_map/ppermute | solution.py:267
  8.6 9.4 %copy-start.11 = (s32[128,1]{0,1:T(1,128)S(1)}, s32[128,1]{0,1:T(1,128)}, u32[]{:S(2)}) copy-start(s32[128,1]{0,1:T(1,128)} %param.17) | copy-start | bytes 1540
  8.6 23.1 %all-to-all-start = ((bf16[4,128,1024]{2,1,0:T(8,128)(2,1)}), bf16[4,128,1024]{2,1,0:T(8,128)(2,1)S(1)}, u32[]{:S(2)}, u32[]{:S(2)}) async-start(bf16[4,128,1024]{2,1,0:T(8,128)(2,1)} %splat.1), calls=%async_computation | async-start | bytes 2097152 | tf_op jit(solution)/shard_map/all_to_all | solution.py:271
  18.0 13.8 %copy-start.3 = (bf16[128,1024]{1,0:T(8,128)(2,1)S(1)}, bf16[128,1024]{1,0:T(8,128)(2,1)}, u32[]{:S(2)}) copy-start(bf16[128,1024]{1,0:T(8,128)(2,1)} %base_ref.1) | copy-start | bytes 786436
  18.3 13.5 %copy-start.4 = (f32[1024]{0:T(1024)S(1)}, f32[1024]{0:T(1024)}, u32[]{:S(2)}) copy-start(f32[1024]{0:T(1024)} %param.16) | copy-start | bytes 12292
  31.8 15.8 %copy-start = (bf16[1,512,1024]{2,1,0:T(8,128)(2,1)S(1)}, bf16[1,512,1024]{2,1,0:T(8,128)(2,1)}, u32[]{:S(2)}) copy-start(bf16[1,512,1024]{2,1,0:T(8,128)(2,1)} %param.18) | copy-start | bytes 3145732
  31.8 15.8 %copy-start.1 = (bf16[1,512,1024]{2,1,0:T(8,128)(2,1)S(1)}, bf16[1,512,1024]{2,1,0:T(8,128)(2,1)}, u32[]{:S(2)}) copy-start(bf16[1,512,1024]{2,1,0:T(8,128)(2,1)} %param.19) | copy-start | bytes 3145732
  33.6 14.0 %copy-start.7 = (s32[1,4,8]{2,1,0:T(4,128)S(1)}, s32[1,4,8]{2,1,0:T(4,128)}, u32[]{:S(2)}) copy-start(s32[1,4,8]{2,1,0:T(4,128)} %param.23) | copy-start | bytes 388
  33.6 41.0 %all-to-all-start.1 = ((bf16[64,24,128]{2,1,0:T(8,128)(2,1)}), bf16[64,24,128]{2,1,0:T(8,128)(2,1)S(1)}, u32[]{:S(2)}, u32[]{:S(2)}) async-start(bf16[64,24,128]{2,1,0:T(8,128)(2,1)} %bitcast.9), calls=%async_computation.1 | async-start | bytes 786432 | tf_op jit(solution)/shard_map/all_to_all | solution.py:294
  47.6 0.7 copy-start.6
  47.6 0.7 copy-start.5
  48.3 1.2 copy-start.2
  52.3 28.5 %collective-permute-start.2 = (bf16[1024,512]{1,0:T(8,128)(2,1)}, bf16[1024,512]{1,0:T(8,128)(2,1)S(1)}, u32[]{:S(2)}, u32[]{:S(2)}) collective-permute-start(bf16[1024,512]{1,0:T(8,128)(2,1)} %get-tuple-element.27.refs_0_), channel_id=1, source_target_pairs={{0,64},{64,0},{128,192},{192,128},{256,320},{320,256},{384,448},{4... | collective-permute-start | bytes 3145736 | tf_op jit(solution)/shard_map/ppermute | solution.py:280
  54.2 30.5 %collective-permute-start.3 = (bf16[1024,512]{1,0:T(8,128)(2,1)}, bf16[1024,512]{1,0:T(8,128)(2,1)S(1)}, u32[]{:S(2)}, u32[]{:S(2)}) collective-permute-start(bf16[1024,512]{1,0:T(8,128)(2,1)} %get-tuple-element.28.refs_1_), channel_id=1, source_target_pairs={{0,64},{64,0},{128,192},{192,128},{256,320},{320,256},{384,448},{4... | collective-permute-start | bytes 3145736 | tf_op jit(solution)/shard_map/ppermute | solution.py:280
  56.6 28.2 %collective-permute-start.4 = (bf16[512,1024]{1,0:T(8,128)(2,1)}, bf16[512,1024]{1,0:T(8,128)(2,1)}, u32[]{:S(2)}, u32[]{:S(2)}) collective-permute-start(bf16[512,1024]{1,0:T(8,128)(2,1)} %get-tuple-element.29.refs_2_), channel_id=1, source_target_pairs={{0,64},{64,0},{128,192},{192,128},{256,320},{320,256},{384,448},{4... | collective-permute-start | bytes 3145736 | tf_op jit(solution)/shard_map/ppermute | solution.py:280
  74.9 17.7 %collective-permute-start.5 = (bf16[192,1024]{1,0:T(8,128)(2,1)S(1)}, bf16[192,1024]{1,0:T(8,128)(2,1)S(1)}, u32[]{:S(2)}, u32[]{:S(2)}) collective-permute-start(bf16[192,1024]{1,0:T(8,128)(2,1)S(1)} %reshape.51.x_ref), channel_id=1, source_target_pairs={{0,128},{64,192},{128,256},{192,320},{256,384},{320,448},{384,0},{... | collective-permute-start | bytes 1179656 | tf_op jit(solution)/shard_map/ppermute | solution.py:298
  78.8 17.4 %collective-permute-start.7 = (bf16[192,1024]{1,0:T(8,128)(2,1)S(1)}, bf16[192,1024]{1,0:T(8,128)(2,1)S(1)}, u32[]{:S(2)}, u32[]{:S(2)}) collective-permute-start(bf16[192,1024]{1,0:T(8,128)(2,1)S(1)} %reshape.51.x_ref), channel_id=1, source_target_pairs={{0,384},{64,448},{128,0},{192,64},{256,128},{320,192},{384,256},{4... | collective-permute-start | bytes 1179656 | tf_op jit(solution)/shard_map/ppermute | solution.py:298
  80.8 4.0 %copy-start.8 = (bf16[1024,512]{1,0:T(8,128)(2,1)}, bf16[1024,512]{1,0:T(8,128)(2,1)S(1)}, u32[]{:S(2)}) copy-start(bf16[1024,512]{1,0:T(8,128)(2,1)S(1)} %collective-permute-done.2.refs_3_) | copy-start | bytes 3145732
  80.8 22.8 %collective-permute-start.9 = (bf16[192,1024]{1,0:T(8,128)(2,1)S(1)}, bf16[192,1024]{1,0:T(8,128)(2,1)S(1)}, u32[]{:S(2)}, u32[]{:S(2)}) collective-permute-start(bf16[192,1024]{1,0:T(8,128)(2,1)S(1)} %reshape.51.x_ref), channel_id=1, source_target_pairs={{0,256},{64,320},{128,384},{192,448},{256,0},{320,64},{384,128},{4... | collective-permute-start | bytes 1179656 | tf_op jit(solution)/shard_map/ppermute | solution.py:298
  84.7 1.0 copy-start.9
  94.3 15.5 %collective-permute-start.6 = (bf16[192,1024]{1,0:T(8,128)(2,1)S(1)}, bf16[192,1024]{1,0:T(8,128)(2,1)S(1)}, u32[]{:S(2)}, u32[]{:S(2)}) collective-permute-start(bf16[192,1024]{1,0:T(8,128)(2,1)S(1)} %ffn.3), channel_id=1, source_target_pairs={{0,384},{64,448},{128,0},{192,64},{256,128},{320,192},{384,256},{4... | collective-permute-start | bytes 1179656 | tf_op jit(solution)/shard_map/ppermute | solution.py:300
  98.1 11.8 %collective-permute-start.8 = (bf16[192,1024]{1,0:T(8,128)(2,1)S(1)}, bf16[192,1024]{1,0:T(8,128)(2,1)S(1)}, u32[]{:S(2)}, u32[]{:S(2)}) collective-permute-start(bf16[192,1024]{1,0:T(8,128)(2,1)S(1)} %ffn.4), channel_id=1, source_target_pairs={{0,128},{64,192},{128,256},{192,320},{256,384},{320,448},{384,0},{... | collective-permute-start | bytes 1179656 | tf_op jit(solution)/shard_map/ppermute | solution.py:300
  105.4 11.2 %collective-permute-start.10 = (bf16[192,1024]{1,0:T(8,128)(2,1)S(1)}, bf16[192,1024]{1,0:T(8,128)(2,1)S(1)}, u32[]{:S(2)}, u32[]{:S(2)}) collective-permute-start(bf16[192,1024]{1,0:T(8,128)(2,1)S(1)} %ffn.5), channel_id=1, source_target_pairs={{0,256},{64,320},{128,384},{192,448},{256,0},{320,64},{384,128},{4... | collective-permute-start | bytes 1179656 | tf_op jit(solution)/shard_map/ppermute | solution.py:300
  117.8 30.6 %all-to-all-start.2 = ((bf16[64,24,128]{2,1,0:T(8,128)(2,1)}), bf16[64,24,128]{2,1,0:T(8,128)(2,1)S(1)}, u32[]{:S(2)}, u32[]{:S(2)}) async-start(bf16[64,24,128]{2,1,0:T(8,128)(2,1)} %bitcast.13), calls=%async_computation.2 | async-start | bytes 786432 | tf_op jit(solution)/shard_map/all_to_all | solution.py:301
  125.5 23.0 %copy-start.10 = (f32[128,1024]{1,0:T(8,128)S(1)}, f32[128,1024]{1,0:T(8,128)}, u32[]{:S(2)}) copy-start(f32[128,1024]{1,0:T(8,128)} %get-tuple-element.22) | copy-start | bytes 1572868

commit v3 on v2

--- a/solution.py
+++ b/solution.py
@@ -19,57 +19,65 @@
     return pltpu.with_memory_space_constraint(x, pltpu.HBM)
 
 
-def code_kernel(counts_ref, bins_ref, code_ref):
-    total = bins_ref.shape[1]
+def splat_kernel(counts_ref, core_ref, bins_ref, cells_ref, other_ref, own_ref, held, sem):
+    copy = pltpu.make_async_copy(cells_ref, held, sem)
+    copy.start()
+    chips, rows, _ = own_ref.shape
+    total = held.shape[0]
     position = lax.broadcasted_iota(jnp.int32, (1, total), 1)
     tile = jnp.zeros((1, total), jnp.int32)
     run_end = jnp.int32(0)
     for k in range(counts_ref.shape[1]):
         run_end = run_end + counts_ref[0, k]
         tile = tile + (position >= run_end).astype(jnp.int32)
-    code_ref[...] = tile * QB + bins_ref[...]
-
-
-def codes(counts, bins):
-    return pl.pallas_call(
-        code_kernel,
-        in_specs=[pl.BlockSpec(memory_space=pltpu.SMEM), pl.BlockSpec(memory_space=pltpu.VMEM)],
-        out_specs=pl.BlockSpec(memory_space=pltpu.VMEM),
-        out_shape=pltpu.VMEM(bins.shape, jnp.int32),
-        compiler_params=pltpu.CompilerParams(vmem_limit_bytes=LIMIT),
-        name="codes",
-    )(in_hbm(counts), in_hbm(bins))
-
-
-def splat_kernel(core_ref, code_ref, other_code_ref, cells_ref, other_cells_ref, out_ref, held, sem):
-    copy = pltpu.make_async_copy(cells_ref, held, sem)
-    copy.start()
-    chips, rows, _ = out_ref.shape
-    row = lax.broadcasted_iota(jnp.int32, (chips, rows, held.shape[0]), 1)
-    chip = lax.broadcasted_iota(jnp.int32, (chips, rows, held.shape[0]), 0)
-    bins = ((chip * CORES + core_ref[0]) * rows + row).reshape(chips * rows, held.shape[0])
-
-    def summed(its_code, its_cells):
-        match = (bins == its_code[...]).astype(jnp.float32).astype(jnp.bfloat16)
-        return jnp.dot(match, its_cells[...], preferred_element_type=jnp.float32)
-
-    total = summed(other_code_ref, other_cells_ref)
+    code = tile * rows + bins_ref[...]
+    row = lax.broadcasted_iota(jnp.int32, (rows, total), 0)
     copy.wait()
-    total = total + summed(code_ref, held)
-    out_ref[...] = total.astype(out_ref.dtype).reshape(out_ref.shape)
-
-
-def splat(core, code, other_code, cells, other_cells, chips, tile_bins):
-    vmem = pl.BlockSpec(memory_space=pltpu.VMEM)
+    cells = held[...]
+    for core, out_ref in ((1 - core_ref[0], other_ref), (core_ref[0], own_ref)):
+        for chip in range(chips):
+            match = row + (chip * CORES + core) * rows == code
+            out_ref[chip] = jnp.dot(
+                match.astype(jnp.float32).astype(jnp.bfloat16), cells, preferred_element_type=jnp.float32
+            ).astype(out_ref.dtype)
+
+
+def splat(counts, core, bins, cells, chips, tile_bins):
+    vmem = pl.BlockSpec(memory_space=pltpu.VMEM)
+    smem = pl.BlockSpec(memory_space=pltpu.SMEM)
+    shape = (chips, tile_bins, cells.shape[1])
     return pl.pallas_call(
         splat_kernel,
-        in_specs=[pl.BlockSpec(memory_space=pltpu.SMEM), vmem, vmem, pl.BlockSpec(memory_space=pl.ANY), vmem],
-        out_specs=vmem,
-        out_shape=pltpu.VMEM((chips, tile_bins, cells.shape[1]), jnp.bfloat16),
+        in_specs=[smem, smem, vmem, pl.BlockSpec(memory_space=pltpu.HBM)],
+        out_specs=[vmem, vmem],
+        out_shape=[pltpu.VMEM(shape, jnp.bfloat16), pltpu.VMEM(shape, jnp.float32)],
         scratch_shapes=[pltpu.VMEM(cells.shape, jnp.bfloat16), pltpu.SemaphoreType.DMA],
         compiler_params=pltpu.CompilerParams(vmem_limit_bytes=LIMIT),
         name="splat",
-    )(core, in_vmem(code), in_vmem(other_code), in_hbm(cells), in_vmem(other_cells))
+    )(in_hbm(counts), core, in_hbm(bins), in_hbm(cells))
+
+
+def join_kernel(own_ref, got_ref, out_ref, sums, sems):
+    chips = own_ref.shape[0]
+    copies = [pltpu.make_async_copy(sums.at[chip], out_ref.at[chip], sems.at[chip]) for chip in range(chips)]
+    for chip in range(chips):
+        sums[chip] = (own_ref[chip] + got_ref[chip].astype(jnp.float32)).astype(sums.dtype)
+        copies[chip].start()
+    for copy in copies:
+        copy.wait()
+
+
+def join(own, got):
+    vmem = pl.BlockSpec(memory_space=pltpu.VMEM)
+    return pl.pallas_call(
+        join_kernel,
+        in_specs=[vmem, vmem],
+        out_specs=pl.BlockSpec(memory_space=pltpu.HBM),
+        out_shape=pltpu.HBM(got.shape, got.dtype),
+        scratch_shapes=[pltpu.VMEM(got.shape, got.dtype), pltpu.SemaphoreType.DMA((got.shape[0],))],
+        compiler_params=pltpu.CompilerParams(vmem_limit_bytes=LIMIT),
+        name="join",
+    )(in_vmem(own), in_vmem(got))
 
 
 def dequant_kernel(gs, us, ds, gq, uq, dq, *outs):
@@ -262,10 +270,10 @@
 
     same_core = [[CORES * x + c for x in range(chips)] for c in range(CORES)]
 
-    other_cells = lax.ppermute(cells, "dp", to_core)
-    code = codes(tile_counts, cell_bins.reshape(1, cell_total))
-    other_code = lax.ppermute(code, "dp", to_core)
-    sums = splat(core, code, other_code, cells, other_cells, chips, tile_bins)
+    for_other, own_sums = splat(
+        tile_counts, core, cell_bins.reshape(1, cell_total), cells, chips, tile_bins
+    )
+    sums = join(own_sums, lax.ppermute(for_other, "dp", to_core))
     quants = (gate_q[0], up_q[0], down_q[0])
     *quants, sums = lax.optimization_barrier((*quants, sums))
     got = lax.all_to_all(

time: 150 us -> 150 us (level)
  starting transfers between devices: 62.2 us -> 60 us
    ppermute x2 -> x1, starting transfers between devices: 4.32 us -> 1.92 us  [on_device(): sums = join(own_sums, lax.ppermute(for_other, 'dp', to_core))]
    ppermute x2 -> x1, waiting for transfers between devices: 0.79 us -> 2.63 us  [on_device(): sums = join(own_sums, lax.ppermute(for_other, 'dp', to_core))]
  transfers between devices with their start and end apart: 14 -> 13, of which waited for: 7 -> 7; matrix products, arithmetic and copies ran while one was open for 0% -> 1% of each run, Pallas kernels for 8% -> 8%
where the time goes in v3:
time: 150 us; the launch traced here: 149 us
  waiting for transfers between devices  64.8 us (43%)
  starting transfers between devices  60 us (40%)
  Pallas kernels  18.3 us (12%)
  local copies, waits for them, and re-layouts  2.57 us (2%)
  other arithmetic  1.75 us (1%)
    all_to_all x1, waiting for transfers between devices, on_device(): lax.all_to_all(combine([own, *backs]).reshape(dense), 'expert', split_axi...  22.7 us
    all_to_all x1, waiting for transfers between devices, on_device(): lax.all_to_all(outgoing.reshape(dense), 'expert', split_axis=0, concat_ax...  16.7 us
    all_to_all x1, starting transfers between devices, on_device(): lax.all_to_all(outgoing.reshape(dense), 'expert', split_axis=0, concat_ax...  13.9 us
    all_to_all x1, waiting for transfers between devices, on_device(): lax.all_to_all(sums, 'dp', split_axis=0, concat_axis=0, tiled=True, axis_...  11.8 us
    ppermute x3, starting transfers between devices, on_device(): lax.ppermute(ffn(there, held), 'dp', to_chip(chips - k))  11 us
    ppermute x3, starting transfers between devices, on_device(): lax.ppermute(arrived, 'dp', to_chip(k))  9.82 us
    all_to_all x1, starting transfers between devices, on_device(): lax.all_to_all(sums, 'dp', split_axis=0, concat_axis=0, tiled=True, axis_...  9.48 us
    ppermute x3, waiting for transfers between devices, on_device(): lax.ppermute(ffn(there, held), 'dp', to_chip(chips - k))  7.79 us
  transfers between devices with their start and end apart: 13, of which 7 were waited for; matrix products, arithmetic and copies ran while one was open for 1% of the time, Pallas kernels for 8%

profile of v3, /device:TPU:6, one launch (start us, length us, event | category | flops | bytes accessed | tf_op | source)
XLA Modules:
  0.0 148.8 jit_solution(6939394086052982224)
XLA Ops:
  0.0 2.5 %splat.1 = (bf16[4,128,1024]{2,1,0:T(8,128)(2,1)S(1)}, f32[4,128,1024]{2,1,0:T(8,128)S(1)}) custom-call(s32[1,8]{1,0:T(1,128)} %counts_ref.1, s32[1]{0:T(128)} %bitcast.3.core_ref, s32[1,256]{1,0:T(1,128)} %bitcast.27, bf16[256,1024]{1,0:T(8,128)(2,1)} %cells_ref.1), custom_call_target="tpu_custom_call" | custom-call | tf_op jit(solution)/shard_map/splat/pallas_call | solution.py:49
  2.5 1.9 %collective-permute-start = (bf16[4,128,1024]{2,1,0:T(8,128)(2,1)S(1)}, bf16[4,128,1024]{2,1,0:T(8,128)(2,1)S(1)}, u32[]{:S(2)}, u32[]{:S(2)}) collective-permute-start(bf16[4,128,1024]{2,1,0:T(8,128)(2,1)S(1)} %get-tuple-element.24), channel_id=1, source_target_pairs={{0,64},{64,0},{128,192},{192,128},{256,320},{320,256},{384,448},{4... | collective-permute-start | bytes 3145736 | tf_op jit(solution)/shard_map/ppermute | solution.py:276
  4.4 2.6 %collective-permute-done.got_ref = bf16[4,128,1024]{2,1,0:T(8,128)(2,1)S(1)} collective-permute-done((bf16[4,128,1024]{2,1,0:T(8,128)(2,1)S(1)}, bf16[4,128,1024]{2,1,0:T(8,128)(2,1)S(1)}, u32[]{:S(2)}, u32[]{:S(2)}) %collective-permute-start) | collective-permute-done | bytes 1048608 | tf_op jit(solution)/shard_map/ppermute | solution.py:276
  7.0 1.1 join.1
  8.1 0.0 copy-start.11
  8.1 0.0 copy-start.3
  8.1 0.0 copy-start.4
  8.2 0.0 copy-start
  8.2 0.0 copy-start.1
  8.2 0.0 copy-start.5
  8.2 0.0 copy-start.6
  8.2 0.0 copy-start.7
  8.2 9.5 %all-to-all-start = ((bf16[4,128,1024]{2,1,0:T(8,128)(2,1)}), bf16[4,128,1024]{2,1,0:T(8,128)(2,1)S(1)}, u32[]{:S(2)}, u32[]{:S(2)}) async-start(bf16[4,128,1024]{2,1,0:T(8,128)(2,1)} %join.1), calls=%async_computation | async-start | bytes 2097152 | tf_op jit(solution)/shard_map/all_to_all | solution.py:279
  17.7 0.0 copy-done.11
  17.7 0.1 fusion.1
  17.8 0.2 reduce_window_sum.11
  18.0 0.8 select_reduce_fusion
  18.8 0.7 bitcast_add_fusion.slot_ref
  19.5 11.8 %all-to-all-done.got_ref = bf16[4,128,1024]{2,1,0:T(8,128)(2,1)S(1)} async-done(((bf16[4,128,1024]{2,1,0:T(8,128)(2,1)}), bf16[4,128,1024]{2,1,0:T(8,128)(2,1)S(1)}, u32[]{:S(2)}, u32[]{:S(2)}) %all-to-all-start) | async-done | bytes 1048608 | tf_op jit(solution)/shard_map/all_to_all | solution.py:279
  31.3 0.0 copy-done.3
  31.3 0.0 copy-done.4
  31.3 1.8 %route.1 = (bf16[1536,128]{1,0:T(8,128)(2,1)}, f32[128,1024]{1,0:T(8,128)}) custom-call(bf16[4,128,1024]{2,1,0:T(8,128)(2,1)S(1)} %all-to-all-done.got_ref, bf16[128,1024]{1,0:T(8,128)(2,1)S(1)} %copy-done.3, f32[1,1024]{1,0:T(1,128)S(1)} %bitcast.21, s32[1,128]{1,0:T(1,128)S(1)} %bitcast_add_fusion.slot_ref), custom_call_target="tpu_custom_call" | custom-call | tf_op jit(solution)/shard_map/route/pallas_call | solution.py:138
  33.1 13.9 %all-to-all-start.1 = ((bf16[64,24,128]{2,1,0:T(8,128)(2,1)}), bf16[64,24,128]{2,1,0:T(8,128)(2,1)S(1)}, u32[]{:S(2)}, u32[]{:S(2)}) async-start(bf16[64,24,128]{2,1,0:T(8,128)(2,1)} %bitcast.9), calls=%async_computation.1 | async-start | bytes 786432 | tf_op jit(solution)/shard_map/all_to_all | solution.py:302
  47.1 0.0 copy-done
  47.1 0.0 copy-done.1
  47.1 0.0 copy-done.5
  47.1 0.0 copy-done.6
  47.1 0.0 copy-done.7
  47.1 0.0 copy-start.2
  47.1 1.2 copy-done.2
  48.3 2.8 %dequantize.1 = (bf16[1024,512]{1,0:T(8,128)(2,1)}, bf16[1024,512]{1,0:T(8,128)(2,1)}, bf16[512,1024]{1,0:T(8,128)(2,1)}) custom-call(s32[4,8]{1,0:T(4,128)S(1)} %bitcast.22, s32[4,8]{1,0:T(4,128)S(1)} %bitcast.23, s32[4,8]{1,0:T(4,128)S(1)} %bitcast.24, bf16[512,1024]{1,0:T(8,128)(2,1)S(1)} %bitcast.18, bf16[512,1024]{1,0:T(8,128)(2,1)S(1)} %bitcast.19, ...), custom_call_target="tpu_custom_call" | custom-call | tf_op jit(solution)/shard_map/dequantize/pallas_call | solution.py:104
  51.1 1.9 %collective-permute-start.1 = (bf16[1024,512]{1,0:T(8,128)(2,1)}, bf16[1024,512]{1,0:T(8,128)(2,1)S(1)}, u32[]{:S(2)}, u32[]{:S(2)}) collective-permute-start(bf16[1024,512]{1,0:T(8,128)(2,1)} %get-tuple-element.31.refs_0_), channel_id=1, source_target_pairs={{0,64},{64,0},{128,192},{192,128},{256,320},{320,256},{384,448},{4... | collective-permute-start | bytes 3145736 | tf_op jit(solution)/shard_map/ppermute | solution.py:288
  53.0 2.4 %collective-permute-start.2 = (bf16[1024,512]{1,0:T(8,128)(2,1)}, bf16[1024,512]{1,0:T(8,128)(2,1)S(1)}, u32[]{:S(2)}, u32[]{:S(2)}) collective-permute-start(bf16[1024,512]{1,0:T(8,128)(2,1)} %get-tuple-element.32.refs_1_), channel_id=1, source_target_pairs={{0,64},{64,0},{128,192},{192,128},{256,320},{320,256},{384,448},{4... | collective-permute-start | bytes 3145736 | tf_op jit(solution)/shard_map/ppermute | solution.py:288
  55.5 1.9 %collective-permute-start.3 = (bf16[512,1024]{1,0:T(8,128)(2,1)}, bf16[512,1024]{1,0:T(8,128)(2,1)}, u32[]{:S(2)}, u32[]{:S(2)}) collective-permute-start(bf16[512,1024]{1,0:T(8,128)(2,1)} %get-tuple-element.33.refs_2_), channel_id=1, source_target_pairs={{0,64},{64,0},{128,192},{192,128},{256,320},{320,256},{384,448},{4... | collective-permute-start | bytes 3145736 | tf_op jit(solution)/shard_map/ppermute | solution.py:288
  57.4 16.7 %all-to-all-done.1 = bf16[64,24,128]{2,1,0:T(8,128)(2,1)S(1)} async-done(((bf16[64,24,128]{2,1,0:T(8,128)(2,1)}), bf16[64,24,128]{2,1,0:T(8,128)(2,1)S(1)}, u32[]{:S(2)}, u32[]{:S(2)}) %all-to-all-start.1) | async-done | bytes 393248 | tf_op jit(solution)/shard_map/all_to_all | solution.py:302
  74.0 0.2 reshape.51.x_ref
  74.2 4.0 %collective-permute-start.4 = (bf16[192,1024]{1,0:T(8,128)(2,1)S(1)}, bf16[192,1024]{1,0:T(8,128)(2,1)S(1)}, u32[]{:S(2)}, u32[]{:S(2)}) collective-permute-start(bf16[192,1024]{1,0:T(8,128)(2,1)S(1)} %reshape.51.x_ref), channel_id=1, source_target_pairs={{0,128},{64,192},{128,256},{192,320},{256,384},{320,448},{384,0},{... | collective-permute-start | bytes 1179656 | tf_op jit(solution)/shard_map/ppermute | solution.py:306
  78.2 1.9 %collective-permute-start.6 = (bf16[192,1024]{1,0:T(8,128)(2,1)S(1)}, bf16[192,1024]{1,0:T(8,128)(2,1)S(1)}, u32[]{:S(2)}, u32[]{:S(2)}) collective-permute-start(bf16[192,1024]{1,0:T(8,128)(2,1)S(1)} %reshape.51.x_ref), channel_id=1, source_target_pairs={{0,384},{64,448},{128,0},{192,64},{256,128},{320,192},{384,256},{4... | collective-permute-start | bytes 1179656 | tf_op jit(solution)/shard_map/ppermute | solution.py:306
  80.1 0.0 collective-permute-done.1.refs_3_
  80.1 0.0 copy-start.8
  80.2 3.9 %collective-permute-start.8 = (bf16[192,1024]{1,0:T(8,128)(2,1)S(1)}, bf16[192,1024]{1,0:T(8,128)(2,1)S(1)}, u32[]{:S(2)}, u32[]{:S(2)}) collective-permute-start(bf16[192,1024]{1,0:T(8,128)(2,1)S(1)} %reshape.51.x_ref), channel_id=1, source_target_pairs={{0,256},{64,320},{128,384},{192,448},{256,0},{320,64},{384,128},{4... | collective-permute-start | bytes 1179656 | tf_op jit(solution)/shard_map/ppermute | solution.py:306
  84.1 0.0 collective-permute-done.2.refs_4_
  84.1 0.0 copy-start.9
  84.1 0.0 collective-permute-done.3.refs_5_
  84.1 0.9 copy-done.9
  85.1 3.7 %load_ffn.1 = (bf16[192,1024]{1,0:T(8,128)(2,1)S(1)}, bf16[1024,512]{1,0:T(8,128)(2,1)S(1)}, bf16[1024,512]{1,0:T(8,128)(2,1)S(1)}, bf16[512,1024]{1,0:T(8,128)(...) custom-call(bf16[192,1024]{1,0:T(8,128)(2,1)S(1)} %reshape.51.x_ref, ...), custom_call_target="tpu_custom_call" | custom-call | tf_op jit(solution)/shard_map/load_ffn/pallas_call | solution.py:187
  88.8 3.2 %collective-permute-done.4.x_ref = bf16[192,1024]{1,0:T(8,128)(2,1)S(1)} collective-permute-done((bf16[192,1024]{1,0:T(8,128)(2,1)S(1)}, bf16[192,1024]{1,0:T(8,128)(2,1)S(1)}, u32[]{:S(2)}, u32[]{:S(2)}) %collective-permute-start.4) | collective-permute-done | bytes 393248 | tf_op jit(solution)/shard_map/ppermute | solution.py:306
  91.9 1.8 %ffn.3 = bf16[192,1024]{1,0:T(8,128)(2,1)S(1)} custom-call(bf16[192,1024]{1,0:T(8,128)(2,1)S(1)} %collective-permute-done.4.x_ref, bf16[1024,512]{1,0:T(8,128)(2,1)S(1)} %get-tuple-element.35.refs_0_, bf16[1024,512]{1,0:T(8,128)(2,1)S(1)} %get-tuple-element.36.refs_1_, bf16[512,1024]{1,0:T(8,128)(2,1)S(1)} %get-tuple-element.37.refs_2_, ...), custom_call_target="tpu_custom_call" | custom-call | tf_op jit(solution)/shard_map/ffn/pallas_call | solution.py:206
  93.7 1.9 %collective-permute-start.5 = (bf16[192,1024]{1,0:T(8,128)(2,1)S(1)}, bf16[192,1024]{1,0:T(8,128)(2,1)S(1)}, u32[]{:S(2)}, u32[]{:S(2)}) collective-permute-start(bf16[192,1024]{1,0:T(8,128)(2,1)S(1)} %ffn.3), channel_id=1, source_target_pairs={{0,384},{64,448},{128,0},{192,64},{256,128},{320,192},{384,256},{4... | collective-permute-start | bytes 1179656 | tf_op jit(solution)/shard_map/ppermute | solution.py:308
  95.6 0.0 collective-permute-done.6.x_ref
  95.6 1.8 %ffn.4 = bf16[192,1024]{1,0:T(8,128)(2,1)S(1)} custom-call(bf16[192,1024]{1,0:T(8,128)(2,1)S(1)} %collective-permute-done.6.x_ref, bf16[1024,512]{1,0:T(8,128)(2,1)S(1)} %get-tuple-element.35.refs_0_, bf16[1024,512]{1,0:T(8,128)(2,1)S(1)} %get-tuple-element.36.refs_1_, bf16[512,1024]{1,0:T(8,128)(2,1)S(1)} %get-tuple-element.37.refs_2_, ...), custom_call_target="tpu_custom_call" | custom-call | tf_op jit(solution)/shard_map/ffn/pallas_call | solution.py:206
  97.4 5.6 %collective-permute-start.7 = (bf16[192,1024]{1,0:T(8,128)(2,1)S(1)}, bf16[192,1024]{1,0:T(8,128)(2,1)S(1)}, u32[]{:S(2)}, u32[]{:S(2)}) collective-permute-start(bf16[192,1024]{1,0:T(8,128)(2,1)S(1)} %ffn.4), channel_id=1, source_target_pairs={{0,128},{64,192},{128,256},{192,320},{256,384},{320,448},{384,0},{... | collective-permute-start | bytes 1179656 | tf_op jit(solution)/shard_map/ppermute | solution.py:308
  103.0 0.0 collective-permute-done.8.x_ref
  103.0 1.8 %ffn.5 = bf16[192,1024]{1,0:T(8,128)(2,1)S(1)} custom-call(bf16[192,1024]{1,0:T(8,128)(2,1)S(1)} %collective-permute-done.8.x_ref, bf16[1024,512]{1,0:T(8,128)(2,1)S(1)} %get-tuple-element.35.refs_0_, bf16[1024,512]{1,0:T(8,128)(2,1)S(1)} %get-tuple-element.36.refs_1_, bf16[512,1024]{1,0:T(8,128)(2,1)S(1)} %get-tuple-element.37.refs_2_, ...), custom_call_target="tpu_custom_call" | custom-call | tf_op jit(solution)/shard_map/ffn/pallas_call | solution.py:206
  104.8 0.0 copy-start.12
  104.8 3.5 %collective-permute-start.9 = (bf16[192,1024]{1,0:T(8,128)(2,1)S(1)}, bf16[192,1024]{1,0:T(8,128)(2,1)S(1)}, u32[]{:S(2)}, u32[]{:S(2)}) collective-permute-start(bf16[192,1024]{1,0:T(8,128)(2,1)S(1)} %ffn.5), channel_id=1, source_target_pairs={{0,256},{64,320},{128,384},{192,448},{256,0},{320,64},{384,128},{4... | collective-permute-start | bytes 1179656 | tf_op jit(solution)/shard_map/ppermute | solution.py:308
  108.3 0.9 collective-permute-done.5.refs_1_
  109.2 0.0 collective-permute-done.7.refs_2_
  109.2 6.9 %collective-permute-done.9.refs_3_ = bf16[192,1024]{1,0:T(8,128)(2,1)S(1)} collective-permute-done((bf16[192,1024]{1,0:T(8,128)(2,1)S(1)}, bf16[192,1024]{1,0:T(8,128)(2,1)S(1)}, u32[]{:S(2)}, u32[]{:S(2)}) %collective-permute-start.9) | collective-permute-done | bytes 393248 | tf_op jit(solution)/shard_map/ppermute | solution.py:308
  116.1 1.2 combine.1
  117.3 7.7 %all-to-all-start.2 = ((bf16[64,24,128]{2,1,0:T(8,128)(2,1)}), bf16[64,24,128]{2,1,0:T(8,128)(2,1)S(1)}, u32[]{:S(2)}, u32[]{:S(2)}) async-start(bf16[64,24,128]{2,1,0:T(8,128)(2,1)} %bitcast.13), calls=%async_computation.2 | async-start | bytes 786432 | tf_op jit(solution)/shard_map/all_to_all | solution.py:309
  125.0 22.7 %all-to-all-done.2 = bf16[64,24,128]{2,1,0:T(8,128)(2,1)S(1)} async-done(((bf16[64,24,128]{2,1,0:T(8,128)(2,1)}), bf16[64,24,128]{2,1,0:T(8,128)(2,1)S(1)}, u32[]{:S(2)}, u32[]{:S(2)}) %all-to-all-start.2) | async-done | bytes 393248 | tf_op jit(solution)/shard_map/all_to_all | solution.py:309
  147.7 0.2 reshape.53
  147.8 1.0 fusion
  (5 shorter events, 0.0 us)
Async XLA Ops:
  2.5 4.6 %collective-permute-start = (bf16[4,128,1024]{2,1,0:T(8,128)(2,1)S(1)}, bf16[4,128,1024]{2,1,0:T(8,128)(2,1)S(1)}, u32[]{:S(2)}, u32[]{:S(2)}) collective-permute-start(bf16[4,128,1024]{2,1,0:T(8,128)(2,1)S(1)} %get-tuple-element.24), channel_id=1, source_target_pairs={{0,64},{64,0},{128,192},{192,128},{256,320},{320,256},{384,448},{4... | collective-permute-start | bytes 3145736 | tf_op jit(solution)/shard_map/ppermute | solution.py:276
  8.1 9.6 %copy-start.11 = (s32[128,1]{0,1:T(1,128)S(1)}, s32[128,1]{0,1:T(1,128)}, u32[]{:S(2)}) copy-start(s32[128,1]{0,1:T(1,128)} %param.17) | copy-start | bytes 1540
  8.1 23.2 %copy-start.3 = (bf16[128,1024]{1,0:T(8,128)(2,1)S(1)}, bf16[128,1024]{1,0:T(8,128)(2,1)}, u32[]{:S(2)}) copy-start(bf16[128,1024]{1,0:T(8,128)(2,1)} %base_ref.1) | copy-start | bytes 786436
  8.1 23.2 %copy-start.4 = (f32[1024]{0:T(1024)S(1)}, f32[1024]{0:T(1024)}, u32[]{:S(2)}) copy-start(f32[1024]{0:T(1024)} %param.16) | copy-start | bytes 12292
  8.2 38.9 %copy-start = (bf16[1,512,1024]{2,1,0:T(8,128)(2,1)S(1)}, bf16[1,512,1024]{2,1,0:T(8,128)(2,1)}, u32[]{:S(2)}) copy-start(bf16[1,512,1024]{2,1,0:T(8,128)(2,1)} %param.18) | copy-start | bytes 3145732
  8.2 38.9 %copy-start.1 = (bf16[1,512,1024]{2,1,0:T(8,128)(2,1)S(1)}, bf16[1,512,1024]{2,1,0:T(8,128)(2,1)}, u32[]{:S(2)}) copy-start(bf16[1,512,1024]{2,1,0:T(8,128)(2,1)} %param.19) | copy-start | bytes 3145732
  8.2 38.9 %copy-start.5 = (s32[1,4,8]{2,1,0:T(4,128)S(1)}, s32[1,4,8]{2,1,0:T(4,128)}, u32[]{:S(2)}) copy-start(s32[1,4,8]{2,1,0:T(4,128)} %param.21) | copy-start | bytes 388
  8.2 38.9 %copy-start.6 = (s32[1,4,8]{2,1,0:T(4,128)S(1)}, s32[1,4,8]{2,1,0:T(4,128)}, u32[]{:S(2)}) copy-start(s32[1,4,8]{2,1,0:T(4,128)} %param.22) | copy-start | bytes 388
  8.2 38.9 %copy-start.7 = (s32[1,4,8]{2,1,0:T(4,128)S(1)}, s32[1,4,8]{2,1,0:T(4,128)}, u32[]{:S(2)}) copy-start(s32[1,4,8]{2,1,0:T(4,128)} %param.23) | copy-start | bytes 388
  8.2 23.1 %all-to-all-start = ((bf16[4,128,1024]{2,1,0:T(8,128)(2,1)}), bf16[4,128,1024]{2,1,0:T(8,128)(2,1)S(1)}, u32[]{:S(2)}, u32[]{:S(2)}) async-start(bf16[4,128,1024]{2,1,0:T(8,128)(2,1)} %join.1), calls=%async_computation | async-start | bytes 2097152 | tf_op jit(solution)/shard_map/all_to_all | solution.py:279
  33.1 40.9 %all-to-all-start.1 = ((bf16[64,24,128]{2,1,0:T(8,128)(2,1)}), bf16[64,24,128]{2,1,0:T(8,128)(2,1)S(1)}, u32[]{:S(2)}, u32[]{:S(2)}) async-start(bf16[64,24,128]{2,1,0:T(8,128)(2,1)} %bitcast.9), calls=%async_computation.1 | async-start | bytes 786432 | tf_op jit(solution)/shard_map/all_to_all | solution.py:302
  47.1 1.2 copy-start.2
  51.1 29.0 %collective-permute-start.1 = (bf16[1024,512]{1,0:T(8,128)(2,1)}, bf16[1024,512]{1,0:T(8,128)(2,1)S(1)}, u32[]{:S(2)}, u32[]{:S(2)}) collective-permute-start(bf16[1024,512]{1,0:T(8,128)(2,1)} %get-tuple-element.31.refs_0_), channel_id=1, source_target_pairs={{0,64},{64,0},{128,192},{192,128},{256,320},{320,256},{384,448},{4... | collective-permute-start | bytes 3145736 | tf_op jit(solution)/shard_map/ppermute | solution.py:288
  53.0 31.0 %collective-permute-start.2 = (bf16[1024,512]{1,0:T(8,128)(2,1)}, bf16[1024,512]{1,0:T(8,128)(2,1)S(1)}, u32[]{:S(2)}, u32[]{:S(2)}) collective-permute-start(bf16[1024,512]{1,0:T(8,128)(2,1)} %get-tuple-element.32.refs_1_), channel_id=1, source_target_pairs={{0,64},{64,0},{128,192},{192,128},{256,320},{320,256},{384,448},{4... | collective-permute-start | bytes 3145736 | tf_op jit(solution)/shard_map/ppermute | solution.py:288
  55.5 28.6 %collective-permute-start.3 = (bf16[512,1024]{1,0:T(8,128)(2,1)}, bf16[512,1024]{1,0:T(8,128)(2,1)}, u32[]{:S(2)}, u32[]{:S(2)}) collective-permute-start(bf16[512,1024]{1,0:T(8,128)(2,1)} %get-tuple-element.33.refs_2_), channel_id=1, source_target_pairs={{0,64},{64,0},{128,192},{192,128},{256,320},{320,256},{384,448},{4... | collective-permute-start | bytes 3145736 | tf_op jit(solution)/shard_map/ppermute | solution.py:288
  74.2 17.7 %collective-permute-start.4 = (bf16[192,1024]{1,0:T(8,128)(2,1)S(1)}, bf16[192,1024]{1,0:T(8,128)(2,1)S(1)}, u32[]{:S(2)}, u32[]{:S(2)}) collective-permute-start(bf16[192,1024]{1,0:T(8,128)(2,1)S(1)} %reshape.51.x_ref), channel_id=1, source_target_pairs={{0,128},{64,192},{128,256},{192,320},{256,384},{320,448},{384,0},{... | collective-permute-start | bytes 1179656 | tf_op jit(solution)/shard_map/ppermute | solution.py:306
  78.2 17.4 %collective-permute-start.6 = (bf16[192,1024]{1,0:T(8,128)(2,1)S(1)}, bf16[192,1024]{1,0:T(8,128)(2,1)S(1)}, u32[]{:S(2)}, u32[]{:S(2)}) collective-permute-start(bf16[192,1024]{1,0:T(8,128)(2,1)S(1)} %reshape.51.x_ref), channel_id=1, source_target_pairs={{0,384},{64,448},{128,0},{192,64},{256,128},{320,192},{384,256},{4... | collective-permute-start | bytes 1179656 | tf_op jit(solution)/shard_map/ppermute | solution.py:306
  80.1 4.0 %copy-start.8 = (bf16[1024,512]{1,0:T(8,128)(2,1)}, bf16[1024,512]{1,0:T(8,128)(2,1)S(1)}, u32[]{:S(2)}) copy-start(bf16[1024,512]{1,0:T(8,128)(2,1)S(1)} %collective-permute-done.1.refs_3_) | copy-start | bytes 3145732
  80.2 22.8 %collective-permute-start.8 = (bf16[192,1024]{1,0:T(8,128)(2,1)S(1)}, bf16[192,1024]{1,0:T(8,128)(2,1)S(1)}, u32[]{:S(2)}, u32[]{:S(2)}) collective-permute-start(bf16[192,1024]{1,0:T(8,128)(2,1)S(1)} %reshape.51.x_ref), channel_id=1, source_target_pairs={{0,256},{64,320},{128,384},{192,448},{256,0},{320,64},{384,128},{4... | collective-permute-start | bytes 1179656 | tf_op jit(solution)/shard_map/ppermute | solution.py:306
  84.1 1.0 copy-start.9
  93.7 15.5 %collective-permute-start.5 = (bf16[192,1024]{1,0:T(8,128)(2,1)S(1)}, bf16[192,1024]{1,0:T(8,128)(2,1)S(1)}, u32[]{:S(2)}, u32[]{:S(2)}) collective-permute-start(bf16[192,1024]{1,0:T(8,128)(2,1)S(1)} %ffn.3), channel_id=1, source_target_pairs={{0,384},{64,448},{128,0},{192,64},{256,128},{320,192},{384,256},{4... | collective-permute-start | bytes 1179656 | tf_op jit(solution)/shard_map/ppermute | solution.py:308
  97.4 11.8 %collective-permute-start.7 = (bf16[192,1024]{1,0:T(8,128)(2,1)S(1)}, bf16[192,1024]{1,0:T(8,128)(2,1)S(1)}, u32[]{:S(2)}, u32[]{:S(2)}) collective-permute-start(bf16[192,1024]{1,0:T(8,128)(2,1)S(1)} %ffn.4), channel_id=1, source_target_pairs={{0,128},{64,192},{128,256},{192,320},{256,384},{320,448},{384,0},{... | collective-permute-start | bytes 1179656 | tf_op jit(solution)/shard_map/ppermute | solution.py:308
  104.8 20.2 %copy-start.12 = (s32[128,1]{0,1:T(1,128)S(1)}, s32[128,1]{0,1:T(1,128)}, u32[]{:S(2)}) copy-start(s32[128,1]{0,1:T(1,128)} %param.17) | copy-start | bytes 1540
  104.8 43.0 %copy-start.10 = (f32[128,1024]{1,0:T(8,128)S(1)}, f32[128,1024]{1,0:T(8,128)}, u32[]{:S(2)}) copy-start(f32[128,1024]{1,0:T(8,128)} %get-tuple-element.26) | copy-start | bytes 1572868
  104.8 11.3 %collective-permute-start.9 = (bf16[192,1024]{1,0:T(8,128)(2,1)S(1)}, bf16[192,1024]{1,0:T(8,128)(2,1)S(1)}, u32[]{:S(2)}, u32[]{:S(2)}) collective-permute-start(bf16[192,1024]{1,0:T(8,128)(2,1)S(1)} %ffn.5), channel_id=1, source_target_pairs={{0,256},{64,320},{128,384},{192,448},{256,0},{320,64},{384,128},{4... | collective-permute-start | bytes 1179656 | tf_op jit(solution)/shard_map/ppermute | solution.py:308
  117.3 30.4 %all-to-all-start.2 = ((bf16[64,24,128]{2,1,0:T(8,128)(2,1)}), bf16[64,24,128]{2,1,0:T(8,128)(2,1)S(1)}, u32[]{:S(2)}, u32[]{:S(2)}) async-start(bf16[64,24,128]{2,1,0:T(8,128)(2,1)} %bitcast.13), calls=%async_computation.2 | async-start | bytes 786432 | tf_op jit(solution)/shard_map/all_to_all | solution.py:309

commit v4 on v3

--- a/solution.py
+++ b/solution.py
@@ -144,7 +144,7 @@
             pltpu.HBM((bins, width), jnp.float32),
         ],
         scratch_shapes=[
-            pltpu.VMEM((rows, QB), jnp.float32),
+            pltpu.VMEM((rows + width // QB, QB), jnp.float32),
             pltpu.VMEM((bins, width), jnp.float32),
             pltpu.SemaphoreType.DMA,
         ],
@@ -217,7 +217,7 @@
     lanes = rows.shape[1] // QB
     for col in range(lanes):
         spread[pl.ds(col, rows.shape[0], stride=lanes), :] = rows[:, col * QB : (col + 1) * QB]
-    out_ref[...] = spread[...].astype(out_ref.dtype)
+    out_ref[...] = spread[: out_ref.shape[0], :].astype(out_ref.dtype)
 
 
 def combine_kernel(*refs):
@@ -237,7 +237,7 @@
         in_specs=[vmem] * len(parts),
         out_specs=vmem,
         out_shape=pltpu.VMEM((rows, QB), jnp.bfloat16),
-        scratch_shapes=[pltpu.VMEM((rows, QB), jnp.float32)],
+        scratch_shapes=[pltpu.VMEM((rows + width // QB, QB), jnp.float32)],
         compiler_params=pltpu.CompilerParams(vmem_limit_bytes=LIMIT),
         name="combine",
     )(*(in_vmem(part) for part in parts))

time: 150 us -> 150 us (level)
  no operation moved by 1% of the time
where the time goes in v4:
time: 150 us; the launch traced here: 149 us
  waiting for transfers between devices  64.8 us (43%)
  starting transfers between devices  60 us (40%)
  Pallas kernels  18.3 us (12%)
  local copies, waits for them, and re-layouts  2.57 us (2%)
  other arithmetic  1.75 us (1%)
    all_to_all x1, waiting for transfers between devices, on_device(): lax.all_to_all(combine([own, *backs]).reshape(dense), 'expert', split_axi...  22.7 us
    all_to_all x1, waiting for transfers between devices, on_device(): lax.all_to_all(outgoing.reshape(dense), 'expert', split_axis=0, concat_ax...  16.7 us
    all_to_all x1, starting transfers between devices, on_device(): lax.all_to_all(outgoing.reshape(dense), 'expert', split_axis=0, concat_ax...  13.9 us
    all_to_all x1, waiting for transfers between devices, on_device(): lax.all_to_all(sums, 'dp', split_axis=0, concat_axis=0, tiled=True, axis_...  11.8 us
    ppermute x3, starting transfers between devices, on_device(): lax.ppermute(ffn(there, held), 'dp', to_chip(chips - k))  11 us
    ppermute x3, starting transfers between devices, on_device(): lax.ppermute(arrived, 'dp', to_chip(k))  9.82 us
    all_to_all x1, starting transfers between devices, on_device(): lax.all_to_all(sums, 'dp', split_axis=0, concat_axis=0, tiled=True, axis_...  9.48 us
    ppermute x3, waiting for transfers between devices, on_device(): lax.ppermute(ffn(there, held), 'dp', to_chip(chips - k))  7.8 us
  transfers between devices with their start and end apart: 13, of which 7 were waited for; matrix products, arithmetic and copies ran while one was open for 1% of the time, Pallas kernels for 8%

profile of v4, /device:TPU:6, one launch (start us, length us, event | category | flops | bytes accessed | tf_op | source)
XLA Modules:
  0.0 148.8 jit_solution(2313549036960745195)
XLA Ops:
  0.0 2.5 %splat.1 = (bf16[4,128,1024]{2,1,0:T(8,128)(2,1)S(1)}, f32[4,128,1024]{2,1,0:T(8,128)S(1)}) custom-call(s32[1,8]{1,0:T(1,128)} %counts_ref.1, s32[1]{0:T(128)} %bitcast.3.core_ref, s32[1,256]{1,0:T(1,128)} %bitcast.27, bf16[256,1024]{1,0:T(8,128)(2,1)} %cells_ref.1), custom_call_target="tpu_custom_call" | custom-call | tf_op jit(solution)/shard_map/splat/pallas_call | solution.py:49
  2.5 1.9 %collective-permute-start = (bf16[4,128,1024]{2,1,0:T(8,128)(2,1)S(1)}, bf16[4,128,1024]{2,1,0:T(8,128)(2,1)S(1)}, u32[]{:S(2)}, u32[]{:S(2)}) collective-permute-start(bf16[4,128,1024]{2,1,0:T(8,128)(2,1)S(1)} %get-tuple-element.24), channel_id=1, source_target_pairs={{0,64},{64,0},{128,192},{192,128},{256,320},{320,256},{384,448},{4... | collective-permute-start | bytes 3145736 | tf_op jit(solution)/shard_map/ppermute | solution.py:276
  4.4 2.6 %collective-permute-done.got_ref = bf16[4,128,1024]{2,1,0:T(8,128)(2,1)S(1)} collective-permute-done((bf16[4,128,1024]{2,1,0:T(8,128)(2,1)S(1)}, bf16[4,128,1024]{2,1,0:T(8,128)(2,1)S(1)}, u32[]{:S(2)}, u32[]{:S(2)}) %collective-permute-start) | collective-permute-done | bytes 1048608 | tf_op jit(solution)/shard_map/ppermute | solution.py:276
  7.0 1.1 join.1
  8.1 0.0 copy-start.11
  8.1 0.0 copy-start.3
  8.1 0.0 copy-start.4
  8.2 0.0 copy-start
  8.2 0.0 copy-start.1
  8.2 0.0 copy-start.5
  8.2 0.0 copy-start.6
  8.2 0.0 copy-start.7
  8.2 9.5 %all-to-all-start = ((bf16[4,128,1024]{2,1,0:T(8,128)(2,1)}), bf16[4,128,1024]{2,1,0:T(8,128)(2,1)S(1)}, u32[]{:S(2)}, u32[]{:S(2)}) async-start(bf16[4,128,1024]{2,1,0:T(8,128)(2,1)} %join.1), calls=%async_computation | async-start | bytes 2097152 | tf_op jit(solution)/shard_map/all_to_all | solution.py:279
  17.7 0.0 copy-done.11
  17.7 0.1 fusion.1
  17.8 0.2 reduce_window_sum.11
  18.0 0.8 select_reduce_fusion
  18.8 0.7 bitcast_add_fusion.slot_ref
  19.5 11.8 %all-to-all-done.got_ref = bf16[4,128,1024]{2,1,0:T(8,128)(2,1)S(1)} async-done(((bf16[4,128,1024]{2,1,0:T(8,128)(2,1)}), bf16[4,128,1024]{2,1,0:T(8,128)(2,1)S(1)}, u32[]{:S(2)}, u32[]{:S(2)}) %all-to-all-start) | async-done | bytes 1048608 | tf_op jit(solution)/shard_map/all_to_all | solution.py:279
  31.3 0.0 copy-done.3
  31.3 0.0 copy-done.4
  31.3 1.8 %route.1 = (bf16[1536,128]{1,0:T(8,128)(2,1)}, f32[128,1024]{1,0:T(8,128)}) custom-call(bf16[4,128,1024]{2,1,0:T(8,128)(2,1)S(1)} %all-to-all-done.got_ref, bf16[128,1024]{1,0:T(8,128)(2,1)S(1)} %copy-done.3, f32[1,1024]{1,0:T(1,128)S(1)} %bitcast.21, s32[1,128]{1,0:T(1,128)S(1)} %bitcast_add_fusion.slot_ref), custom_call_target="tpu_custom_call" | custom-call | tf_op jit(solution)/shard_map/route/pallas_call | solution.py:138
  33.1 13.9 %all-to-all-start.1 = ((bf16[64,24,128]{2,1,0:T(8,128)(2,1)}), bf16[64,24,128]{2,1,0:T(8,128)(2,1)S(1)}, u32[]{:S(2)}, u32[]{:S(2)}) async-start(bf16[64,24,128]{2,1,0:T(8,128)(2,1)} %bitcast.9), calls=%async_computation.1 | async-start | bytes 786432 | tf_op jit(solution)/shard_map/all_to_all | solution.py:302
  47.1 0.0 copy-done
  47.1 0.0 copy-done.1
  47.1 0.0 copy-done.5
  47.1 0.0 copy-done.6
  47.1 0.0 copy-done.7
  47.1 0.0 copy-start.2
  47.1 1.2 copy-done.2
  48.3 2.8 %dequantize.1 = (bf16[1024,512]{1,0:T(8,128)(2,1)}, bf16[1024,512]{1,0:T(8,128)(2,1)}, bf16[512,1024]{1,0:T(8,128)(2,1)}) custom-call(s32[4,8]{1,0:T(4,128)S(1)} %bitcast.22, s32[4,8]{1,0:T(4,128)S(1)} %bitcast.23, s32[4,8]{1,0:T(4,128)S(1)} %bitcast.24, bf16[512,1024]{1,0:T(8,128)(2,1)S(1)} %bitcast.18, bf16[512,1024]{1,0:T(8,128)(2,1)S(1)} %bitcast.19, ...), custom_call_target="tpu_custom_call" | custom-call | tf_op jit(solution)/shard_map/dequantize/pallas_call | solution.py:104
  51.1 1.9 %collective-permute-start.1 = (bf16[1024,512]{1,0:T(8,128)(2,1)}, bf16[1024,512]{1,0:T(8,128)(2,1)S(1)}, u32[]{:S(2)}, u32[]{:S(2)}) collective-permute-start(bf16[1024,512]{1,0:T(8,128)(2,1)} %get-tuple-element.31.refs_0_), channel_id=1, source_target_pairs={{0,64},{64,0},{128,192},{192,128},{256,320},{320,256},{384,448},{4... | collective-permute-start | bytes 3145736 | tf_op jit(solution)/shard_map/ppermute | solution.py:288
  53.0 2.4 %collective-permute-start.2 = (bf16[1024,512]{1,0:T(8,128)(2,1)}, bf16[1024,512]{1,0:T(8,128)(2,1)S(1)}, u32[]{:S(2)}, u32[]{:S(2)}) collective-permute-start(bf16[1024,512]{1,0:T(8,128)(2,1)} %get-tuple-element.32.refs_1_), channel_id=1, source_target_pairs={{0,64},{64,0},{128,192},{192,128},{256,320},{320,256},{384,448},{4... | collective-permute-start | bytes 3145736 | tf_op jit(solution)/shard_map/ppermute | solution.py:288
  55.5 1.9 %collective-permute-start.3 = (bf16[512,1024]{1,0:T(8,128)(2,1)}, bf16[512,1024]{1,0:T(8,128)(2,1)}, u32[]{:S(2)}, u32[]{:S(2)}) collective-permute-start(bf16[512,1024]{1,0:T(8,128)(2,1)} %get-tuple-element.33.refs_2_), channel_id=1, source_target_pairs={{0,64},{64,0},{128,192},{192,128},{256,320},{320,256},{384,448},{4... | collective-permute-start | bytes 3145736 | tf_op jit(solution)/shard_map/ppermute | solution.py:288
  57.4 16.7 %all-to-all-done.1 = bf16[64,24,128]{2,1,0:T(8,128)(2,1)S(1)} async-done(((bf16[64,24,128]{2,1,0:T(8,128)(2,1)}), bf16[64,24,128]{2,1,0:T(8,128)(2,1)S(1)}, u32[]{:S(2)}, u32[]{:S(2)}) %all-to-all-start.1) | async-done | bytes 393248 | tf_op jit(solution)/shard_map/all_to_all | solution.py:302
  74.0 0.2 reshape.51.x_ref
  74.2 4.0 %collective-permute-start.4 = (bf16[192,1024]{1,0:T(8,128)(2,1)S(1)}, bf16[192,1024]{1,0:T(8,128)(2,1)S(1)}, u32[]{:S(2)}, u32[]{:S(2)}) collective-permute-start(bf16[192,1024]{1,0:T(8,128)(2,1)S(1)} %reshape.51.x_ref), channel_id=1, source_target_pairs={{0,128},{64,192},{128,256},{192,320},{256,384},{320,448},{384,0},{... | collective-permute-start | bytes 1179656 | tf_op jit(solution)/shard_map/ppermute | solution.py:306
  78.2 1.9 %collective-permute-start.6 = (bf16[192,1024]{1,0:T(8,128)(2,1)S(1)}, bf16[192,1024]{1,0:T(8,128)(2,1)S(1)}, u32[]{:S(2)}, u32[]{:S(2)}) collective-permute-start(bf16[192,1024]{1,0:T(8,128)(2,1)S(1)} %reshape.51.x_ref), channel_id=1, source_target_pairs={{0,384},{64,448},{128,0},{192,64},{256,128},{320,192},{384,256},{4... | collective-permute-start | bytes 1179656 | tf_op jit(solution)/shard_map/ppermute | solution.py:306
  80.1 0.0 collective-permute-done.1.refs_3_
  80.1 0.0 copy-start.8
  80.2 3.9 %collective-permute-start.8 = (bf16[192,1024]{1,0:T(8,128)(2,1)S(1)}, bf16[192,1024]{1,0:T(8,128)(2,1)S(1)}, u32[]{:S(2)}, u32[]{:S(2)}) collective-permute-start(bf16[192,1024]{1,0:T(8,128)(2,1)S(1)} %reshape.51.x_ref), channel_id=1, source_target_pairs={{0,256},{64,320},{128,384},{192,448},{256,0},{320,64},{384,128},{4... | collective-permute-start | bytes 1179656 | tf_op jit(solution)/shard_map/ppermute | solution.py:306
  84.1 0.0 collective-permute-done.2.refs_4_
  84.1 0.0 copy-start.9
  84.1 0.0 collective-permute-done.3.refs_5_
  84.1 0.9 copy-done.9
  85.1 3.7 %load_ffn.1 = (bf16[192,1024]{1,0:T(8,128)(2,1)S(1)}, bf16[1024,512]{1,0:T(8,128)(2,1)S(1)}, bf16[1024,512]{1,0:T(8,128)(2,1)S(1)}, bf16[512,1024]{1,0:T(8,128)(...) custom-call(bf16[192,1024]{1,0:T(8,128)(2,1)S(1)} %reshape.51.x_ref, ...), custom_call_target="tpu_custom_call" | custom-call | tf_op jit(solution)/shard_map/load_ffn/pallas_call | solution.py:187
  88.8 3.2 %collective-permute-done.4.x_ref = bf16[192,1024]{1,0:T(8,128)(2,1)S(1)} collective-permute-done((bf16[192,1024]{1,0:T(8,128)(2,1)S(1)}, bf16[192,1024]{1,0:T(8,128)(2,1)S(1)}, u32[]{:S(2)}, u32[]{:S(2)}) %collective-permute-start.4) | collective-permute-done | bytes 393248 | tf_op jit(solution)/shard_map/ppermute | solution.py:306
  91.9 1.8 %ffn.3 = bf16[192,1024]{1,0:T(8,128)(2,1)S(1)} custom-call(bf16[192,1024]{1,0:T(8,128)(2,1)S(1)} %collective-permute-done.4.x_ref, bf16[1024,512]{1,0:T(8,128)(2,1)S(1)} %get-tuple-element.35.refs_0_, bf16[1024,512]{1,0:T(8,128)(2,1)S(1)} %get-tuple-element.36.refs_1_, bf16[512,1024]{1,0:T(8,128)(2,1)S(1)} %get-tuple-element.37.refs_2_, ...), custom_call_target="tpu_custom_call" | custom-call | tf_op jit(solution)/shard_map/ffn/pallas_call | solution.py:206
  93.7 1.9 %collective-permute-start.5 = (bf16[192,1024]{1,0:T(8,128)(2,1)S(1)}, bf16[192,1024]{1,0:T(8,128)(2,1)S(1)}, u32[]{:S(2)}, u32[]{:S(2)}) collective-permute-start(bf16[192,1024]{1,0:T(8,128)(2,1)S(1)} %ffn.3), channel_id=1, source_target_pairs={{0,384},{64,448},{128,0},{192,64},{256,128},{320,192},{384,256},{4... | collective-permute-start | bytes 1179656 | tf_op jit(solution)/shard_map/ppermute | solution.py:308
  95.6 0.0 collective-permute-done.6.x_ref
  95.6 1.8 %ffn.4 = bf16[192,1024]{1,0:T(8,128)(2,1)S(1)} custom-call(bf16[192,1024]{1,0:T(8,128)(2,1)S(1)} %collective-permute-done.6.x_ref, bf16[1024,512]{1,0:T(8,128)(2,1)S(1)} %get-tuple-element.35.refs_0_, bf16[1024,512]{1,0:T(8,128)(2,1)S(1)} %get-tuple-element.36.refs_1_, bf16[512,1024]{1,0:T(8,128)(2,1)S(1)} %get-tuple-element.37.refs_2_, ...), custom_call_target="tpu_custom_call" | custom-call | tf_op jit(solution)/shard_map/ffn/pallas_call | solution.py:206
  97.4 5.6 %collective-permute-start.7 = (bf16[192,1024]{1,0:T(8,128)(2,1)S(1)}, bf16[192,1024]{1,0:T(8,128)(2,1)S(1)}, u32[]{:S(2)}, u32[]{:S(2)}) collective-permute-start(bf16[192,1024]{1,0:T(8,128)(2,1)S(1)} %ffn.4), channel_id=1, source_target_pairs={{0,128},{64,192},{128,256},{192,320},{256,384},{320,448},{384,0},{... | collective-permute-start | bytes 1179656 | tf_op jit(solution)/shard_map/ppermute | solution.py:308
  103.0 0.0 collective-permute-done.8.x_ref
  103.0 1.8 %ffn.5 = bf16[192,1024]{1,0:T(8,128)(2,1)S(1)} custom-call(bf16[192,1024]{1,0:T(8,128)(2,1)S(1)} %collective-permute-done.8.x_ref, bf16[1024,512]{1,0:T(8,128)(2,1)S(1)} %get-tuple-element.35.refs_0_, bf16[1024,512]{1,0:T(8,128)(2,1)S(1)} %get-tuple-element.36.refs_1_, bf16[512,1024]{1,0:T(8,128)(2,1)S(1)} %get-tuple-element.37.refs_2_, ...), custom_call_target="tpu_custom_call" | custom-call | tf_op jit(solution)/shard_map/ffn/pallas_call | solution.py:206
  104.8 0.0 copy-start.12
  104.8 3.5 %collective-permute-start.9 = (bf16[192,1024]{1,0:T(8,128)(2,1)S(1)}, bf16[192,1024]{1,0:T(8,128)(2,1)S(1)}, u32[]{:S(2)}, u32[]{:S(2)}) collective-permute-start(bf16[192,1024]{1,0:T(8,128)(2,1)S(1)} %ffn.5), channel_id=1, source_target_pairs={{0,256},{64,320},{128,384},{192,448},{256,0},{320,64},{384,128},{4... | collective-permute-start | bytes 1179656 | tf_op jit(solution)/shard_map/ppermute | solution.py:308
  108.3 0.9 collective-permute-done.5.refs_1_
  109.2 0.0 collective-permute-done.7.refs_2_
  109.2 6.9 %collective-permute-done.9.refs_3_ = bf16[192,1024]{1,0:T(8,128)(2,1)S(1)} collective-permute-done((bf16[192,1024]{1,0:T(8,128)(2,1)S(1)}, bf16[192,1024]{1,0:T(8,128)(2,1)S(1)}, u32[]{:S(2)}, u32[]{:S(2)}) %collective-permute-start.9) | collective-permute-done | bytes 393248 | tf_op jit(solution)/shard_map/ppermute | solution.py:308
  116.1 1.2 combine.1
  117.3 7.7 %all-to-all-start.2 = ((bf16[64,24,128]{2,1,0:T(8,128)(2,1)}), bf16[64,24,128]{2,1,0:T(8,128)(2,1)S(1)}, u32[]{:S(2)}, u32[]{:S(2)}) async-start(bf16[64,24,128]{2,1,0:T(8,128)(2,1)} %bitcast.13), calls=%async_computation.2 | async-start | bytes 786432 | tf_op jit(solution)/shard_map/all_to_all | solution.py:309
  125.0 22.7 %all-to-all-done.2 = bf16[64,24,128]{2,1,0:T(8,128)(2,1)S(1)} async-done(((bf16[64,24,128]{2,1,0:T(8,128)(2,1)}), bf16[64,24,128]{2,1,0:T(8,128)(2,1)S(1)}, u32[]{:S(2)}, u32[]{:S(2)}) %all-to-all-start.2) | async-done | bytes 393248 | tf_op jit(solution)/shard_map/all_to_all | solution.py:309
  147.7 0.2 reshape.53
  147.8 1.0 fusion
  (5 shorter events, 0.0 us)
Async XLA Ops:
  2.5 4.6 %collective-permute-start = (bf16[4,128,1024]{2,1,0:T(8,128)(2,1)S(1)}, bf16[4,128,1024]{2,1,0:T(8,128)(2,1)S(1)}, u32[]{:S(2)}, u32[]{:S(2)}) collective-permute-start(bf16[4,128,1024]{2,1,0:T(8,128)(2,1)S(1)} %get-tuple-element.24), channel_id=1, source_target_pairs={{0,64},{64,0},{128,192},{192,128},{256,320},{320,256},{384,448},{4... | collective-permute-start | bytes 3145736 | tf_op jit(solution)/shard_map/ppermute | solution.py:276
  8.1 9.6 %copy-start.11 = (s32[128,1]{0,1:T(1,128)S(1)}, s32[128,1]{0,1:T(1,128)}, u32[]{:S(2)}) copy-start(s32[128,1]{0,1:T(1,128)} %param.17) | copy-start | bytes 1540
  8.1 23.2 %copy-start.3 = (bf16[128,1024]{1,0:T(8,128)(2,1)S(1)}, bf16[128,1024]{1,0:T(8,128)(2,1)}, u32[]{:S(2)}) copy-start(bf16[128,1024]{1,0:T(8,128)(2,1)} %base_ref.1) | copy-start | bytes 786436
  8.1 23.2 %copy-start.4 = (f32[1024]{0:T(1024)S(1)}, f32[1024]{0:T(1024)}, u32[]{:S(2)}) copy-start(f32[1024]{0:T(1024)} %param.16) | copy-start | bytes 12292
  8.2 38.9 %copy-start = (bf16[1,512,1024]{2,1,0:T(8,128)(2,1)S(1)}, bf16[1,512,1024]{2,1,0:T(8,128)(2,1)}, u32[]{:S(2)}) copy-start(bf16[1,512,1024]{2,1,0:T(8,128)(2,1)} %param.18) | copy-start | bytes 3145732
  8.2 38.9 %copy-start.1 = (bf16[1,512,1024]{2,1,0:T(8,128)(2,1)S(1)}, bf16[1,512,1024]{2,1,0:T(8,128)(2,1)}, u32[]{:S(2)}) copy-start(bf16[1,512,1024]{2,1,0:T(8,128)(2,1)} %param.19) | copy-start | bytes 3145732
  8.2 38.9 %copy-start.5 = (s32[1,4,8]{2,1,0:T(4,128)S(1)}, s32[1,4,8]{2,1,0:T(4,128)}, u32[]{:S(2)}) copy-start(s32[1,4,8]{2,1,0:T(4,128)} %param.21) | copy-start | bytes 388
  8.2 38.9 %copy-start.6 = (s32[1,4,8]{2,1,0:T(4,128)S(1)}, s32[1,4,8]{2,1,0:T(4,128)}, u32[]{:S(2)}) copy-start(s32[1,4,8]{2,1,0:T(4,128)} %param.22) | copy-start | bytes 388
  8.2 38.9 %copy-start.7 = (s32[1,4,8]{2,1,0:T(4,128)S(1)}, s32[1,4,8]{2,1,0:T(4,128)}, u32[]{:S(2)}) copy-start(s32[1,4,8]{2,1,0:T(4,128)} %param.23) | copy-start | bytes 388
  8.2 23.1 %all-to-all-start = ((bf16[4,128,1024]{2,1,0:T(8,128)(2,1)}), bf16[4,128,1024]{2,1,0:T(8,128)(2,1)S(1)}, u32[]{:S(2)}, u32[]{:S(2)}) async-start(bf16[4,128,1024]{2,1,0:T(8,128)(2,1)} %join.1), calls=%async_computation | async-start | bytes 2097152 | tf_op jit(solution)/shard_map/all_to_all | solution.py:279
  33.1 40.9 %all-to-all-start.1 = ((bf16[64,24,128]{2,1,0:T(8,128)(2,1)}), bf16[64,24,128]{2,1,0:T(8,128)(2,1)S(1)}, u32[]{:S(2)}, u32[]{:S(2)}) async-start(bf16[64,24,128]{2,1,0:T(8,128)(2,1)} %bitcast.9), calls=%async_computation.1 | async-start | bytes 786432 | tf_op jit(solution)/shard_map/all_to_all | solution.py:302
  47.1 1.2 copy-start.2
  51.1 29.0 %collective-permute-start.1 = (bf16[1024,512]{1,0:T(8,128)(2,1)}, bf16[1024,512]{1,0:T(8,128)(2,1)S(1)}, u32[]{:S(2)}, u32[]{:S(2)}) collective-permute-start(bf16[1024,512]{1,0:T(8,128)(2,1)} %get-tuple-element.31.refs_0_), channel_id=1, source_target_pairs={{0,64},{64,0},{128,192},{192,128},{256,320},{320,256},{384,448},{4... | collective-permute-start | bytes 3145736 | tf_op jit(solution)/shard_map/ppermute | solution.py:288
  53.0 31.0 %collective-permute-start.2 = (bf16[1024,512]{1,0:T(8,128)(2,1)}, bf16[1024,512]{1,0:T(8,128)(2,1)S(1)}, u32[]{:S(2)}, u32[]{:S(2)}) collective-permute-start(bf16[1024,512]{1,0:T(8,128)(2,1)} %get-tuple-element.32.refs_1_), channel_id=1, source_target_pairs={{0,64},{64,0},{128,192},{192,128},{256,320},{320,256},{384,448},{4... | collective-permute-start | bytes 3145736 | tf_op jit(solution)/shard_map/ppermute | solution.py:288
  55.5 28.6 %collective-permute-start.3 = (bf16[512,1024]{1,0:T(8,128)(2,1)}, bf16[512,1024]{1,0:T(8,128)(2,1)}, u32[]{:S(2)}, u32[]{:S(2)}) collective-permute-start(bf16[512,1024]{1,0:T(8,128)(2,1)} %get-tuple-element.33.refs_2_), channel_id=1, source_target_pairs={{0,64},{64,0},{128,192},{192,128},{256,320},{320,256},{384,448},{4... | collective-permute-start | bytes 3145736 | tf_op jit(solution)/shard_map/ppermute | solution.py:288
  74.2 17.7 %collective-permute-start.4 = (bf16[192,1024]{1,0:T(8,128)(2,1)S(1)}, bf16[192,1024]{1,0:T(8,128)(2,1)S(1)}, u32[]{:S(2)}, u32[]{:S(2)}) collective-permute-start(bf16[192,1024]{1,0:T(8,128)(2,1)S(1)} %reshape.51.x_ref), channel_id=1, source_target_pairs={{0,128},{64,192},{128,256},{192,320},{256,384},{320,448},{384,0},{... | collective-permute-start | bytes 1179656 | tf_op jit(solution)/shard_map/ppermute | solution.py:306
  78.2 17.4 %collective-permute-start.6 = (bf16[192,1024]{1,0:T(8,128)(2,1)S(1)}, bf16[192,1024]{1,0:T(8,128)(2,1)S(1)}, u32[]{:S(2)}, u32[]{:S(2)}) collective-permute-start(bf16[192,1024]{1,0:T(8,128)(2,1)S(1)} %reshape.51.x_ref), channel_id=1, source_target_pairs={{0,384},{64,448},{128,0},{192,64},{256,128},{320,192},{384,256},{4... | collective-permute-start | bytes 1179656 | tf_op jit(solution)/shard_map/ppermute | solution.py:306
  80.1 4.0 %copy-start.8 = (bf16[1024,512]{1,0:T(8,128)(2,1)}, bf16[1024,512]{1,0:T(8,128)(2,1)S(1)}, u32[]{:S(2)}) copy-start(bf16[1024,512]{1,0:T(8,128)(2,1)S(1)} %collective-permute-done.1.refs_3_) | copy-start | bytes 3145732
  80.2 22.8 %collective-permute-start.8 = (bf16[192,1024]{1,0:T(8,128)(2,1)S(1)}, bf16[192,1024]{1,0:T(8,128)(2,1)S(1)}, u32[]{:S(2)}, u32[]{:S(2)}) collective-permute-start(bf16[192,1024]{1,0:T(8,128)(2,1)S(1)} %reshape.51.x_ref), channel_id=1, source_target_pairs={{0,256},{64,320},{128,384},{192,448},{256,0},{320,64},{384,128},{4... | collective-permute-start | bytes 1179656 | tf_op jit(solution)/shard_map/ppermute | solution.py:306
  84.1 1.0 copy-start.9
  93.7 15.5 %collective-permute-start.5 = (bf16[192,1024]{1,0:T(8,128)(2,1)S(1)}, bf16[192,1024]{1,0:T(8,128)(2,1)S(1)}, u32[]{:S(2)}, u32[]{:S(2)}) collective-permute-start(bf16[192,1024]{1,0:T(8,128)(2,1)S(1)} %ffn.3), channel_id=1, source_target_pairs={{0,384},{64,448},{128,0},{192,64},{256,128},{320,192},{384,256},{4... | collective-permute-start | bytes 1179656 | tf_op jit(solution)/shard_map/ppermute | solution.py:308
  97.4 11.8 %collective-permute-start.7 = (bf16[192,1024]{1,0:T(8,128)(2,1)S(1)}, bf16[192,1024]{1,0:T(8,128)(2,1)S(1)}, u32[]{:S(2)}, u32[]{:S(2)}) collective-permute-start(bf16[192,1024]{1,0:T(8,128)(2,1)S(1)} %ffn.4), channel_id=1, source_target_pairs={{0,128},{64,192},{128,256},{192,320},{256,384},{320,448},{384,0},{... | collective-permute-start | bytes 1179656 | tf_op jit(solution)/shard_map/ppermute | solution.py:308
  104.8 20.2 %copy-start.12 = (s32[128,1]{0,1:T(1,128)S(1)}, s32[128,1]{0,1:T(1,128)}, u32[]{:S(2)}) copy-start(s32[128,1]{0,1:T(1,128)} %param.17) | copy-start | bytes 1540
  104.8 43.0 %copy-start.10 = (f32[128,1024]{1,0:T(8,128)S(1)}, f32[128,1024]{1,0:T(8,128)}, u32[]{:S(2)}) copy-start(f32[128,1024]{1,0:T(8,128)} %get-tuple-element.26) | copy-start | bytes 1572868
  104.8 11.3 %collective-permute-start.9 = (bf16[192,1024]{1,0:T(8,128)(2,1)S(1)}, bf16[192,1024]{1,0:T(8,128)(2,1)S(1)}, u32[]{:S(2)}, u32[]{:S(2)}) collective-permute-start(bf16[192,1024]{1,0:T(8,128)(2,1)S(1)} %ffn.5), channel_id=1, source_target_pairs={{0,256},{64,320},{128,384},{192,448},{256,0},{320,64},{384,128},{4... | collective-permute-start | bytes 1179656 | tf_op jit(solution)/shard_map/ppermute | solution.py:308
  117.3 30.4 %all-to-all-start.2 = ((bf16[64,24,128]{2,1,0:T(8,128)(2,1)}), bf16[64,24,128]{2,1,0:T(8,128)(2,1)S(1)}, u32[]{:S(2)}, u32[]{:S(2)}) async-start(bf16[64,24,128]{2,1,0:T(8,128)(2,1)} %bitcast.13), calls=%async_computation.2 | async-start | bytes 786432 | tf_op jit(solution)/shard_map/all_to_all | solution.py:309

commit v5 on v4

--- a/solution.py
+++ b/solution.py
@@ -8,6 +8,7 @@
 QB = 128
 CORES = 2
 CHUNK = 256
+GROUPS = 4
 LIMIT = 8 << 20
 
 
@@ -112,7 +113,7 @@
     )(*scales, *quants)
 
 
-def route_kernel(got_ref, base_ref, gain_ref, slot_ref, out_ref, residual_ref, spread, kept, sem):
+def route_kernel(got_ref, base_ref, gain_ref, slot_ref, out_ref, residual_ref, spread, packed, sems, kept, sem):
     residual = base_ref[...].astype(jnp.float32)
     for chip in range(got_ref.shape[0]):
         residual = residual + got_ref[chip].astype(jnp.float32)
@@ -127,7 +128,8 @@
     placed = jnp.dot(
         placer.astype(jnp.float32).astype(jnp.bfloat16), normed, preferred_element_type=jnp.float32
     )
-    spread_rows(placed, spread, out_ref)
+    count = slots // GROUPS
+    spread_rows(lambda g: placed[g * count : (g + 1) * count], spread, packed, out_ref, sems)
     copy.wait()
 
 
@@ -138,13 +140,13 @@
     return pl.pallas_call(
         route_kernel,
         in_specs=[vmem] * 4,
-        out_specs=[vmem, pl.BlockSpec(memory_space=pltpu.HBM)],
+        out_specs=[pl.BlockSpec(memory_space=pltpu.HBM)] * 2,
         out_shape=[
-            pltpu.VMEM((rows, QB), jnp.bfloat16),
+            pltpu.HBM((rows, QB), jnp.bfloat16),
             pltpu.HBM((bins, width), jnp.float32),
         ],
-        scratch_shapes=[
-            pltpu.VMEM((rows + width // QB, QB), jnp.float32),
+        scratch_shapes=spread_scratch(rows, width)
+        + [
             pltpu.VMEM((bins, width), jnp.float32),
             pltpu.SemaphoreType.DMA,
         ],
@@ -213,19 +215,41 @@
     )(*(in_vmem(v) for v in (x, *weights)))
 
 
-def spread_rows(rows, spread, out_ref):
-    lanes = rows.shape[1] // QB
-    for col in range(lanes):
-        spread[pl.ds(col, rows.shape[0], stride=lanes), :] = rows[:, col * QB : (col + 1) * QB]
-    out_ref[...] = spread[: out_ref.shape[0], :].astype(out_ref.dtype)
+def spread_rows(rows_of, spread, packed, out_ref, sems):
+    copies = []
+    for group in range(GROUPS):
+        rows = rows_of(group)
+        count, lanes = rows.shape[0], rows.shape[1] // QB
+        for col in range(lanes):
+            spread[group, pl.ds(col, count, stride=lanes), :] = rows[:, col * QB : (col + 1) * QB]
+        packed[group] = spread[group, : count * lanes, :].astype(packed.dtype)
+        at = pl.ds(group * count * lanes, count * lanes)
+        copies.append(pltpu.make_async_copy(packed.at[group], out_ref.at[at], sems.at[group]))
+        copies[-1].start()
+    for copy in copies:
+        copy.wait()
+
+
+def spread_scratch(rows, width):
+    return [
+        pltpu.VMEM((GROUPS, rows // GROUPS + width // QB, QB), jnp.float32),
+        pltpu.VMEM((GROUPS, rows // GROUPS, QB), jnp.bfloat16),
+        pltpu.SemaphoreType.DMA((GROUPS,)),
+    ]
 
 
 def combine_kernel(*refs):
-    *parts, out_ref, spread = refs
-    total = parts[0][...].astype(jnp.float32)
-    for part in parts[1:]:
-        total = total + part[...].astype(jnp.float32)
-    spread_rows(total, spread, out_ref)
+    *parts, out_ref, spread, packed, sems = refs
+    count = parts[0].shape[0] // GROUPS
+
+    def rows_of(group):
+        at = slice(group * count, (group + 1) * count)
+        total = parts[0][at, :].astype(jnp.float32)
+        for part in parts[1:]:
+            total = total + part[at, :].astype(jnp.float32)
+        return total
+
+    spread_rows(rows_of, spread, packed, out_ref, sems)
 
 
 def combine(parts):
@@ -235,9 +259,9 @@
     return pl.pallas_call(
         combine_kernel,
         in_specs=[vmem] * len(parts),
-        out_specs=vmem,
-        out_shape=pltpu.VMEM((rows, QB), jnp.bfloat16),
-        scratch_shapes=[pltpu.VMEM((rows + width // QB, QB), jnp.float32)],
+        out_specs=pl.BlockSpec(memory_space=pltpu.HBM),
+        out_shape=pltpu.HBM((rows, QB), jnp.bfloat16),
+        scratch_shapes=spread_scratch(rows, width),
         compiler_params=pltpu.CompilerParams(vmem_limit_bytes=LIMIT),
         name="combine",
     )(*(in_vmem(part) for part in parts))

time: 150 us -> 149 us (level)
  no operation moved by 1% of the time
where the time goes in v5:
time: 149 us; the launch traced here: 148 us
  waiting for transfers between devices  64.8 us (43%)
  starting transfers between devices  60 us (40%)
  Pallas kernels  17.6 us (12%)
  local copies, waits for them, and re-layouts  2.57 us (2%)
  other arithmetic  1.75 us (1%)
    all_to_all x1, waiting for transfers between devices, on_device(): lax.all_to_all(combine([own, *backs]).reshape(dense), 'expert', split_axi...  22.7 us
    all_to_all x1, waiting for transfers between devices, on_device(): lax.all_to_all(outgoing.reshape(dense), 'expert', split_axis=0, concat_ax...  16.7 us
    all_to_all x1, starting transfers between devices, on_device(): lax.all_to_all(outgoing.reshape(dense), 'expert', split_axis=0, concat_ax...  13.9 us
    all_to_all x1, waiting for transfers between devices, on_device(): lax.all_to_all(sums, 'dp', split_axis=0, concat_axis=0, tiled=True, axis_...  11.8 us
    ppermute x3, starting transfers between devices, on_device(): lax.ppermute(ffn(there, held), 'dp', to_chip(chips - k))  11 us
    ppermute x3, starting transfers between devices, on_device(): lax.ppermute(arrived, 'dp', to_chip(k))  9.82 us
    all_to_all x1, starting transfers between devices, on_device(): lax.all_to_all(sums, 'dp', split_axis=0, concat_axis=0, tiled=True, axis_...  9.48 us
    ppermute x3, waiting for transfers between devices, on_device(): lax.ppermute(ffn(there, held), 'dp', to_chip(chips - k))  7.79 us
  transfers between devices with their start and end apart: 13, of which 7 were waited for; matrix products, arithmetic and copies ran while one was open for 1% of the time, Pallas kernels for 8%

profile of v5, /device:TPU:6, one launch (start us, length us, event | category | flops | bytes accessed | tf_op | source)
XLA Modules:
  0.0 148.1 jit_solution(16045344993777035969)
XLA Ops:
  0.0 2.5 %splat.1 = (bf16[4,128,1024]{2,1,0:T(8,128)(2,1)S(1)}, f32[4,128,1024]{2,1,0:T(8,128)S(1)}) custom-call(s32[1,8]{1,0:T(1,128)} %counts_ref.1, s32[1]{0:T(128)} %bitcast.3.core_ref, s32[1,256]{1,0:T(1,128)} %bitcast.29, bf16[256,1024]{1,0:T(8,128)(2,1)} %cells_ref.1), custom_call_target="tpu_custom_call" | custom-call | tf_op jit(solution)/shard_map/splat/pallas_call | solution.py:50
  2.5 1.9 %collective-permute-start = (bf16[4,128,1024]{2,1,0:T(8,128)(2,1)S(1)}, bf16[4,128,1024]{2,1,0:T(8,128)(2,1)S(1)}, u32[]{:S(2)}, u32[]{:S(2)}) collective-permute-start(bf16[4,128,1024]{2,1,0:T(8,128)(2,1)S(1)} %get-tuple-element.24), channel_id=1, source_target_pairs={{0,64},{64,0},{128,192},{192,128},{256,320},{320,256},{384,448},{4... | collective-permute-start | bytes 3145736 | tf_op jit(solution)/shard_map/ppermute | solution.py:300
  4.4 2.6 %collective-permute-done.got_ref = bf16[4,128,1024]{2,1,0:T(8,128)(2,1)S(1)} collective-permute-done((bf16[4,128,1024]{2,1,0:T(8,128)(2,1)S(1)}, bf16[4,128,1024]{2,1,0:T(8,128)(2,1)S(1)}, u32[]{:S(2)}, u32[]{:S(2)}) %collective-permute-start) | collective-permute-done | bytes 1048608 | tf_op jit(solution)/shard_map/ppermute | solution.py:300
  7.0 1.1 join.1
  8.1 0.0 copy-start.11
  8.1 0.0 copy-start.3
  8.1 0.0 copy-start.4
  8.2 0.0 copy-start
  8.2 0.0 copy-start.1
  8.2 0.0 copy-start.5
  8.2 0.0 copy-start.6
  8.2 0.0 copy-start.7
  8.2 9.5 %all-to-all-start = ((bf16[4,128,1024]{2,1,0:T(8,128)(2,1)}), bf16[4,128,1024]{2,1,0:T(8,128)(2,1)S(1)}, u32[]{:S(2)}, u32[]{:S(2)}) async-start(bf16[4,128,1024]{2,1,0:T(8,128)(2,1)} %join.1), calls=%async_computation | async-start | bytes 2097152 | tf_op jit(solution)/shard_map/all_to_all | solution.py:303
  17.7 0.0 copy-done.11
  17.7 0.1 fusion.1
  17.8 0.2 reduce_window_sum.11
  18.0 0.8 select_reduce_fusion
  18.8 0.7 bitcast_add_fusion.slot_ref
  19.5 11.8 %all-to-all-done.got_ref = bf16[4,128,1024]{2,1,0:T(8,128)(2,1)S(1)} async-done(((bf16[4,128,1024]{2,1,0:T(8,128)(2,1)}), bf16[4,128,1024]{2,1,0:T(8,128)(2,1)S(1)}, u32[]{:S(2)}, u32[]{:S(2)}) %all-to-all-start) | async-done | bytes 1048608 | tf_op jit(solution)/shard_map/all_to_all | solution.py:303
  31.3 0.0 copy-done.3
  31.3 0.0 copy-done.4
  31.3 1.3 route.1
  32.6 13.9 %all-to-all-start.1 = ((bf16[64,24,128]{2,1,0:T(8,128)(2,1)}), bf16[64,24,128]{2,1,0:T(8,128)(2,1)S(1)}, u32[]{:S(2)}, u32[]{:S(2)}) async-start(bf16[64,24,128]{2,1,0:T(8,128)(2,1)} %bitcast.26), calls=%async_computation.1 | async-start | bytes 786432 | tf_op jit(solution)/shard_map/all_to_all | solution.py:326
  46.5 0.0 copy-done
  46.5 0.0 copy-done.1
  46.5 0.0 copy-done.5
  46.6 0.0 copy-done.6
  46.6 0.0 copy-start.2
  46.6 1.2 copy-done.2
  47.8 2.8 %dequantize.1 = (bf16[1024,512]{1,0:T(8,128)(2,1)}, bf16[1024,512]{1,0:T(8,128)(2,1)}, bf16[512,1024]{1,0:T(8,128)(2,1)}) custom-call(s32[4,8]{1,0:T(4,128)S(1)} %bitcast.22, s32[4,8]{1,0:T(4,128)S(1)} %bitcast.23, s32[4,8]{1,0:T(4,128)S(1)} %bitcast.24, bf16[512,1024]{1,0:T(8,128)(2,1)S(1)} %bitcast.18, bf16[512,1024]{1,0:T(8,128)(2,1)S(1)} %bitcast.19, ...), custom_call_target="tpu_custom_call" | custom-call | tf_op jit(solution)/shard_map/dequantize/pallas_call | solution.py:105
  50.6 1.9 %collective-permute-start.1 = (bf16[1024,512]{1,0:T(8,128)(2,1)}, bf16[1024,512]{1,0:T(8,128)(2,1)S(1)}, u32[]{:S(2)}, u32[]{:S(2)}) collective-permute-start(bf16[1024,512]{1,0:T(8,128)(2,1)} %get-tuple-element.31.refs_0_), channel_id=1, source_target_pairs={{0,64},{64,0},{128,192},{192,128},{256,320},{320,256},{384,448},{4... | collective-permute-start | bytes 3145736 | tf_op jit(solution)/shard_map/ppermute | solution.py:312
  52.5 2.4 %collective-permute-start.2 = (bf16[1024,512]{1,0:T(8,128)(2,1)}, bf16[1024,512]{1,0:T(8,128)(2,1)S(1)}, u32[]{:S(2)}, u32[]{:S(2)}) collective-permute-start(bf16[1024,512]{1,0:T(8,128)(2,1)} %get-tuple-element.32.refs_1_), channel_id=1, source_target_pairs={{0,64},{64,0},{128,192},{192,128},{256,320},{320,256},{384,448},{4... | collective-permute-start | bytes 3145736 | tf_op jit(solution)/shard_map/ppermute | solution.py:312
  54.9 1.9 %collective-permute-start.3 = (bf16[512,1024]{1,0:T(8,128)(2,1)}, bf16[512,1024]{1,0:T(8,128)(2,1)}, u32[]{:S(2)}, u32[]{:S(2)}) collective-permute-start(bf16[512,1024]{1,0:T(8,128)(2,1)} %get-tuple-element.33.refs_2_), channel_id=1, source_target_pairs={{0,64},{64,0},{128,192},{192,128},{256,320},{320,256},{384,448},{4... | collective-permute-start | bytes 3145736 | tf_op jit(solution)/shard_map/ppermute | solution.py:312
  56.9 16.7 %all-to-all-done.1 = bf16[64,24,128]{2,1,0:T(8,128)(2,1)S(1)} async-done(((bf16[64,24,128]{2,1,0:T(8,128)(2,1)}), bf16[64,24,128]{2,1,0:T(8,128)(2,1)S(1)}, u32[]{:S(2)}, u32[]{:S(2)}) %all-to-all-start.1) | async-done | bytes 393248 | tf_op jit(solution)/shard_map/all_to_all | solution.py:326
  73.5 0.2 reshape.51.x_ref
  73.7 4.0 %collective-permute-start.4 = (bf16[192,1024]{1,0:T(8,128)(2,1)S(1)}, bf16[192,1024]{1,0:T(8,128)(2,1)S(1)}, u32[]{:S(2)}, u32[]{:S(2)}) collective-permute-start(bf16[192,1024]{1,0:T(8,128)(2,1)S(1)} %reshape.51.x_ref), channel_id=1, source_target_pairs={{0,128},{64,192},{128,256},{192,320},{256,384},{320,448},{384,0},{... | collective-permute-start | bytes 1179656 | tf_op jit(solution)/shard_map/ppermute | solution.py:330
  77.7 1.9 %collective-permute-start.6 = (bf16[192,1024]{1,0:T(8,128)(2,1)S(1)}, bf16[192,1024]{1,0:T(8,128)(2,1)S(1)}, u32[]{:S(2)}, u32[]{:S(2)}) collective-permute-start(bf16[192,1024]{1,0:T(8,128)(2,1)S(1)} %reshape.51.x_ref), channel_id=1, source_target_pairs={{0,384},{64,448},{128,0},{192,64},{256,128},{320,192},{384,256},{4... | collective-permute-start | bytes 1179656 | tf_op jit(solution)/shard_map/ppermute | solution.py:330
  79.6 0.0 collective-permute-done.1.refs_3_
  79.6 0.0 copy-start.8
  79.6 3.9 %collective-permute-start.8 = (bf16[192,1024]{1,0:T(8,128)(2,1)S(1)}, bf16[192,1024]{1,0:T(8,128)(2,1)S(1)}, u32[]{:S(2)}, u32[]{:S(2)}) collective-permute-start(bf16[192,1024]{1,0:T(8,128)(2,1)S(1)} %reshape.51.x_ref), channel_id=1, source_target_pairs={{0,256},{64,320},{128,384},{192,448},{256,0},{320,64},{384,128},{4... | collective-permute-start | bytes 1179656 | tf_op jit(solution)/shard_map/ppermute | solution.py:330
  83.6 0.0 collective-permute-done.2.refs_4_
  83.6 0.0 collective-permute-done.3.refs_5_
  83.6 0.9 copy-done.9
  84.5 3.7 %load_ffn.1 = (bf16[192,1024]{1,0:T(8,128)(2,1)S(1)}, bf16[1024,512]{1,0:T(8,128)(2,1)S(1)}, bf16[1024,512]{1,0:T(8,128)(2,1)S(1)}, bf16[512,1024]{1,0:T(8,128)(...) custom-call(bf16[192,1024]{1,0:T(8,128)(2,1)S(1)} %reshape.51.x_ref, ...), custom_call_target="tpu_custom_call" | custom-call | tf_op jit(solution)/shard_map/load_ffn/pallas_call | solution.py:189
  88.2 3.2 %collective-permute-done.4.x_ref = bf16[192,1024]{1,0:T(8,128)(2,1)S(1)} collective-permute-done((bf16[192,1024]{1,0:T(8,128)(2,1)S(1)}, bf16[192,1024]{1,0:T(8,128)(2,1)S(1)}, u32[]{:S(2)}, u32[]{:S(2)}) %collective-permute-start.4) | collective-permute-done | bytes 393248 | tf_op jit(solution)/shard_map/ppermute | solution.py:330
  91.4 1.8 %ffn.3 = bf16[192,1024]{1,0:T(8,128)(2,1)S(1)} custom-call(bf16[192,1024]{1,0:T(8,128)(2,1)S(1)} %collective-permute-done.4.x_ref, bf16[1024,512]{1,0:T(8,128)(2,1)S(1)} %get-tuple-element.35.refs_0_, bf16[1024,512]{1,0:T(8,128)(2,1)S(1)} %get-tuple-element.36.refs_1_, bf16[512,1024]{1,0:T(8,128)(2,1)S(1)} %get-tuple-element.37.refs_2_, ...), custom_call_target="tpu_custom_call" | custom-call | tf_op jit(solution)/shard_map/ffn/pallas_call | solution.py:208
  93.2 1.9 %collective-permute-start.5 = (bf16[192,1024]{1,0:T(8,128)(2,1)S(1)}, bf16[192,1024]{1,0:T(8,128)(2,1)S(1)}, u32[]{:S(2)}, u32[]{:S(2)}) collective-permute-start(bf16[192,1024]{1,0:T(8,128)(2,1)S(1)} %ffn.3), channel_id=1, source_target_pairs={{0,384},{64,448},{128,0},{192,64},{256,128},{320,192},{384,256},{4... | collective-permute-start | bytes 1179656 | tf_op jit(solution)/shard_map/ppermute | solution.py:332
  95.1 0.0 collective-permute-done.6.x_ref
  95.1 1.8 %ffn.4 = bf16[192,1024]{1,0:T(8,128)(2,1)S(1)} custom-call(bf16[192,1024]{1,0:T(8,128)(2,1)S(1)} %collective-permute-done.6.x_ref, bf16[1024,512]{1,0:T(8,128)(2,1)S(1)} %get-tuple-element.35.refs_0_, bf16[1024,512]{1,0:T(8,128)(2,1)S(1)} %get-tuple-element.36.refs_1_, bf16[512,1024]{1,0:T(8,128)(2,1)S(1)} %get-tuple-element.37.refs_2_, ...), custom_call_target="tpu_custom_call" | custom-call | tf_op jit(solution)/shard_map/ffn/pallas_call | solution.py:208
  96.9 5.6 %collective-permute-start.7 = (bf16[192,1024]{1,0:T(8,128)(2,1)S(1)}, bf16[192,1024]{1,0:T(8,128)(2,1)S(1)}, u32[]{:S(2)}, u32[]{:S(2)}) collective-permute-start(bf16[192,1024]{1,0:T(8,128)(2,1)S(1)} %ffn.4), channel_id=1, source_target_pairs={{0,128},{64,192},{128,256},{192,320},{256,384},{320,448},{384,0},{... | collective-permute-start | bytes 1179656 | tf_op jit(solution)/shard_map/ppermute | solution.py:332
  102.5 0.0 collective-permute-done.8.x_ref
  102.5 1.8 %ffn.5 = bf16[192,1024]{1,0:T(8,128)(2,1)S(1)} custom-call(bf16[192,1024]{1,0:T(8,128)(2,1)S(1)} %collective-permute-done.8.x_ref, bf16[1024,512]{1,0:T(8,128)(2,1)S(1)} %get-tuple-element.35.refs_0_, bf16[1024,512]{1,0:T(8,128)(2,1)S(1)} %get-tuple-element.36.refs_1_, bf16[512,1024]{1,0:T(8,128)(2,1)S(1)} %get-tuple-element.37.refs_2_, ...), custom_call_target="tpu_custom_call" | custom-call | tf_op jit(solution)/shard_map/ffn/pallas_call | solution.py:208
  104.3 0.0 copy-start.12
  104.3 3.5 %collective-permute-start.9 = (bf16[192,1024]{1,0:T(8,128)(2,1)S(1)}, bf16[192,1024]{1,0:T(8,128)(2,1)S(1)}, u32[]{:S(2)}, u32[]{:S(2)}) collective-permute-start(bf16[192,1024]{1,0:T(8,128)(2,1)S(1)} %ffn.5), channel_id=1, source_target_pairs={{0,256},{64,320},{128,384},{192,448},{256,0},{320,64},{384,128},{4... | collective-permute-start | bytes 1179656 | tf_op jit(solution)/shard_map/ppermute | solution.py:332
  107.8 0.9 collective-permute-done.5.refs_1_
  108.7 0.0 collective-permute-done.7.refs_2_
  108.7 6.9 %collective-permute-done.9.refs_3_ = bf16[192,1024]{1,0:T(8,128)(2,1)S(1)} collective-permute-done((bf16[192,1024]{1,0:T(8,128)(2,1)S(1)}, bf16[192,1024]{1,0:T(8,128)(2,1)S(1)}, u32[]{:S(2)}, u32[]{:S(2)}) %collective-permute-start.9) | collective-permute-done | bytes 393248 | tf_op jit(solution)/shard_map/ppermute | solution.py:332
  115.6 1.0 combine.1
  116.6 7.7 %all-to-all-start.2 = ((bf16[64,24,128]{2,1,0:T(8,128)(2,1)}), bf16[64,24,128]{2,1,0:T(8,128)(2,1)S(1)}, u32[]{:S(2)}, u32[]{:S(2)}) async-start(bf16[64,24,128]{2,1,0:T(8,128)(2,1)} %bitcast.25), calls=%async_computation.2 | async-start | bytes 786432 | tf_op jit(solution)/shard_map/all_to_all | solution.py:333
  124.3 0.0 copy-done.12
  124.3 22.7 %all-to-all-done.2 = bf16[64,24,128]{2,1,0:T(8,128)(2,1)S(1)} async-done(((bf16[64,24,128]{2,1,0:T(8,128)(2,1)}), bf16[64,24,128]{2,1,0:T(8,128)(2,1)S(1)}, u32[]{:S(2)}, u32[]{:S(2)}) %all-to-all-start.2) | async-done | bytes 393248 | tf_op jit(solution)/shard_map/all_to_all | solution.py:333
  147.0 0.2 reshape.53
  147.1 0.0 copy-done.10
  147.2 1.0 fusion
  (5 shorter events, 0.0 us)
Async XLA Ops:
  2.5 4.6 %collective-permute-start = (bf16[4,128,1024]{2,1,0:T(8,128)(2,1)S(1)}, bf16[4,128,1024]{2,1,0:T(8,128)(2,1)S(1)}, u32[]{:S(2)}, u32[]{:S(2)}) collective-permute-start(bf16[4,128,1024]{2,1,0:T(8,128)(2,1)S(1)} %get-tuple-element.24), channel_id=1, source_target_pairs={{0,64},{64,0},{128,192},{192,128},{256,320},{320,256},{384,448},{4... | collective-permute-start | bytes 3145736 | tf_op jit(solution)/shard_map/ppermute | solution.py:300
  8.1 9.6 %copy-start.11 = (s32[128,1]{0,1:T(1,128)S(1)}, s32[128,1]{0,1:T(1,128)}, u32[]{:S(2)}) copy-start(s32[128,1]{0,1:T(1,128)} %param.17) | copy-start | bytes 1540
  8.1 23.2 %copy-start.3 = (bf16[128,1024]{1,0:T(8,128)(2,1)S(1)}, bf16[128,1024]{1,0:T(8,128)(2,1)}, u32[]{:S(2)}) copy-start(bf16[128,1024]{1,0:T(8,128)(2,1)} %base_ref.1) | copy-start | bytes 786436
  8.1 23.2 %copy-start.4 = (f32[1024]{0:T(1024)S(1)}, f32[1024]{0:T(1024)}, u32[]{:S(2)}) copy-start(f32[1024]{0:T(1024)} %param.16) | copy-start | bytes 12292
  8.2 38.4 %copy-start = (bf16[1,512,1024]{2,1,0:T(8,128)(2,1)S(1)}, bf16[1,512,1024]{2,1,0:T(8,128)(2,1)}, u32[]{:S(2)}) copy-start(bf16[1,512,1024]{2,1,0:T(8,128)(2,1)} %param.18) | copy-start | bytes 3145732
  8.2 38.4 %copy-start.1 = (bf16[1,512,1024]{2,1,0:T(8,128)(2,1)S(1)}, bf16[1,512,1024]{2,1,0:T(8,128)(2,1)}, u32[]{:S(2)}) copy-start(bf16[1,512,1024]{2,1,0:T(8,128)(2,1)} %param.19) | copy-start | bytes 3145732
  8.2 38.4 %copy-start.5 = (s32[1,4,8]{2,1,0:T(4,128)S(1)}, s32[1,4,8]{2,1,0:T(4,128)}, u32[]{:S(2)}) copy-start(s32[1,4,8]{2,1,0:T(4,128)} %param.21) | copy-start | bytes 388
  8.2 38.4 %copy-start.6 = (s32[1,4,8]{2,1,0:T(4,128)S(1)}, s32[1,4,8]{2,1,0:T(4,128)}, u32[]{:S(2)}) copy-start(s32[1,4,8]{2,1,0:T(4,128)} %param.22) | copy-start | bytes 388
  8.2 38.4 %copy-start.7 = (s32[1,4,8]{2,1,0:T(4,128)S(1)}, s32[1,4,8]{2,1,0:T(4,128)}, u32[]{:S(2)}) copy-start(s32[1,4,8]{2,1,0:T(4,128)} %param.23) | copy-start | bytes 388
  8.2 23.1 %all-to-all-start = ((bf16[4,128,1024]{2,1,0:T(8,128)(2,1)}), bf16[4,128,1024]{2,1,0:T(8,128)(2,1)S(1)}, u32[]{:S(2)}, u32[]{:S(2)}) async-start(bf16[4,128,1024]{2,1,0:T(8,128)(2,1)} %join.1), calls=%async_computation | async-start | bytes 2097152 | tf_op jit(solution)/shard_map/all_to_all | solution.py:303
  32.6 40.9 %all-to-all-start.1 = ((bf16[64,24,128]{2,1,0:T(8,128)(2,1)}), bf16[64,24,128]{2,1,0:T(8,128)(2,1)S(1)}, u32[]{:S(2)}, u32[]{:S(2)}) async-start(bf16[64,24,128]{2,1,0:T(8,128)(2,1)} %bitcast.26), calls=%async_computation.1 | async-start | bytes 786432 | tf_op jit(solution)/shard_map/all_to_all | solution.py:326
  46.6 1.2 copy-start.2
  50.6 29.0 %collective-permute-start.1 = (bf16[1024,512]{1,0:T(8,128)(2,1)}, bf16[1024,512]{1,0:T(8,128)(2,1)S(1)}, u32[]{:S(2)}, u32[]{:S(2)}) collective-permute-start(bf16[1024,512]{1,0:T(8,128)(2,1)} %get-tuple-element.31.refs_0_), channel_id=1, source_target_pairs={{0,64},{64,0},{128,192},{192,128},{256,320},{320,256},{384,448},{4... | collective-permute-start | bytes 3145736 | tf_op jit(solution)/shard_map/ppermute | solution.py:312
  52.5 31.0 %collective-permute-start.2 = (bf16[1024,512]{1,0:T(8,128)(2,1)}, bf16[1024,512]{1,0:T(8,128)(2,1)S(1)}, u32[]{:S(2)}, u32[]{:S(2)}) collective-permute-start(bf16[1024,512]{1,0:T(8,128)(2,1)} %get-tuple-element.32.refs_1_), channel_id=1, source_target_pairs={{0,64},{64,0},{128,192},{192,128},{256,320},{320,256},{384,448},{4... | collective-permute-start | bytes 3145736 | tf_op jit(solution)/shard_map/ppermute | solution.py:312
  54.9 28.6 %collective-permute-start.3 = (bf16[512,1024]{1,0:T(8,128)(2,1)}, bf16[512,1024]{1,0:T(8,128)(2,1)}, u32[]{:S(2)}, u32[]{:S(2)}) collective-permute-start(bf16[512,1024]{1,0:T(8,128)(2,1)} %get-tuple-element.33.refs_2_), channel_id=1, source_target_pairs={{0,64},{64,0},{128,192},{192,128},{256,320},{320,256},{384,448},{4... | collective-permute-start | bytes 3145736 | tf_op jit(solution)/shard_map/ppermute | solution.py:312
  73.7 17.7 %collective-permute-start.4 = (bf16[192,1024]{1,0:T(8,128)(2,1)S(1)}, bf16[192,1024]{1,0:T(8,128)(2,1)S(1)}, u32[]{:S(2)}, u32[]{:S(2)}) collective-permute-start(bf16[192,1024]{1,0:T(8,128)(2,1)S(1)} %reshape.51.x_ref), channel_id=1, source_target_pairs={{0,128},{64,192},{128,256},{192,320},{256,384},{320,448},{384,0},{... | collective-permute-start | bytes 1179656 | tf_op jit(solution)/shard_map/ppermute | solution.py:330
  77.7 17.4 %collective-permute-start.6 = (bf16[192,1024]{1,0:T(8,128)(2,1)S(1)}, bf16[192,1024]{1,0:T(8,128)(2,1)S(1)}, u32[]{:S(2)}, u32[]{:S(2)}) collective-permute-start(bf16[192,1024]{1,0:T(8,128)(2,1)S(1)} %reshape.51.x_ref), channel_id=1, source_target_pairs={{0,384},{64,448},{128,0},{192,64},{256,128},{320,192},{384,256},{4... | collective-permute-start | bytes 1179656 | tf_op jit(solution)/shard_map/ppermute | solution.py:330
  79.6 4.0 %copy-start.8 = (bf16[1024,512]{1,0:T(8,128)(2,1)}, bf16[1024,512]{1,0:T(8,128)(2,1)S(1)}, u32[]{:S(2)}) copy-start(bf16[1024,512]{1,0:T(8,128)(2,1)S(1)} %collective-permute-done.1.refs_3_) | copy-start | bytes 3145732
  79.6 22.8 %collective-permute-start.8 = (bf16[192,1024]{1,0:T(8,128)(2,1)S(1)}, bf16[192,1024]{1,0:T(8,128)(2,1)S(1)}, u32[]{:S(2)}, u32[]{:S(2)}) collective-permute-start(bf16[192,1024]{1,0:T(8,128)(2,1)S(1)} %reshape.51.x_ref), channel_id=1, source_target_pairs={{0,256},{64,320},{128,384},{192,448},{256,0},{320,64},{384,128},{4... | collective-permute-start | bytes 1179656 | tf_op jit(solution)/shard_map/ppermute | solution.py:330
  83.6 1.0 copy-start.9
  93.2 15.5 %collective-permute-start.5 = (bf16[192,1024]{1,0:T(8,128)(2,1)S(1)}, bf16[192,1024]{1,0:T(8,128)(2,1)S(1)}, u32[]{:S(2)}, u32[]{:S(2)}) collective-permute-start(bf16[192,1024]{1,0:T(8,128)(2,1)S(1)} %ffn.3), channel_id=1, source_target_pairs={{0,384},{64,448},{128,0},{192,64},{256,128},{320,192},{384,256},{4... | collective-permute-start | bytes 1179656 | tf_op jit(solution)/shard_map/ppermute | solution.py:332
  96.9 11.8 %collective-permute-start.7 = (bf16[192,1024]{1,0:T(8,128)(2,1)S(1)}, bf16[192,1024]{1,0:T(8,128)(2,1)S(1)}, u32[]{:S(2)}, u32[]{:S(2)}) collective-permute-start(bf16[192,1024]{1,0:T(8,128)(2,1)S(1)} %ffn.4), channel_id=1, source_target_pairs={{0,128},{64,192},{128,256},{192,320},{256,384},{320,448},{384,0},{... | collective-permute-start | bytes 1179656 | tf_op jit(solution)/shard_map/ppermute | solution.py:332
  104.3 20.0 %copy-start.12 = (s32[128,1]{0,1:T(1,128)S(1)}, s32[128,1]{0,1:T(1,128)}, u32[]{:S(2)}) copy-start(s32[128,1]{0,1:T(1,128)} %param.17) | copy-start | bytes 1540
  104.3 42.9 %copy-start.10 = (f32[128,1024]{1,0:T(8,128)S(1)}, f32[128,1024]{1,0:T(8,128)}, u32[]{:S(2)}) copy-start(f32[128,1024]{1,0:T(8,128)} %get-tuple-element.26) | copy-start | bytes 1572868
  104.3 11.3 %collective-permute-start.9 = (bf16[192,1024]{1,0:T(8,128)(2,1)S(1)}, bf16[192,1024]{1,0:T(8,128)(2,1)S(1)}, u32[]{:S(2)}, u32[]{:S(2)}) collective-permute-start(bf16[192,1024]{1,0:T(8,128)(2,1)S(1)} %ffn.5), channel_id=1, source_target_pairs={{0,256},{64,320},{128,384},{192,448},{256,0},{320,64},{384,128},{4... | collective-permute-start | bytes 1179656 | tf_op jit(solution)/shard_map/ppermute | solution.py:332
  116.6 30.4 %all-to-all-start.2 = ((bf16[64,24,128]{2,1,0:T(8,128)(2,1)}), bf16[64,24,128]{2,1,0:T(8,128)(2,1)S(1)}, u32[]{:S(2)}, u32[]{:S(2)}) async-start(bf16[64,24,128]{2,1,0:T(8,128)(2,1)} %bitcast.25), calls=%async_computation.2 | async-start | bytes 786432 | tf_op jit(solution)/shard_map/all_to_all | solution.py:333
